TPU v7x, 32 devices: a whole 2x2x4 slice. The times are simulated.
32 devices in a mesh: scene: 2 (over x), gx: 16 (over z, y, core).
Axes of the slice: x: 2, y: 2, z: 4, core: 2. Of those that a mesh axis runs over, the one named last changes fastest.
Arguments:
- voxels: bfloat16 [64, 128, 8, 128], P(('scene', 'gx')), parts along dimension 0, may hold values from -6 to 6
- prior: float32 [64, 128, 8], P(('scene', 'gx')), parts along dimension 0, may hold values from -6 to 410
- conv_first: bfloat16 [27, 128, 128], replicated, may hold values from -0.109375 to 0.109375
- conv_second: bfloat16 [27, 128, 128], replicated, may hold values from -0.109375 to 0.109375
- score_x: bfloat16 [128, 128], replicated, may hold values from -2 to 2
- score_y: bfloat16 [128, 128], replicated, may hold values from -1.5 to 1.5
- plane_yz_w: bfloat16 [9, 128, 128], replicated, may hold values from -0.1875 to 0.1875
- plane_xz_w: bfloat16 [9, 128, 128], replicated, may hold values from -0.1875 to 0.1875
- norm_gain: float32 [128], replicated, may hold values from 0.1 to 1.9
- mlp_in: bfloat16 [128, 512], replicated, may hold values from -0.5 to 0.5
- mlp_out: bfloat16 [512, 128], replicated, may hold values from -0.25 to 0.25
Outputs:
- encoded: bfloat16 [64, 128, 8, 128], P(('scene', 'gx')), parts along dimension 0
There are 2 independent parts, one for each index of `scene`. A program takes and returns all parts, laid end to end along the dimension named above; an argument that names none is the same for every part. Nothing has to cross between parts.
All inputs are finite; a program needn't handle non-finite values.
Results may differ from a plain program's by a relative error of at most 0.012.
Values may be sent and summed in bfloat16 or wider, within the bound.
No kernel may reach another device: no remote copies, remote signals or barrier semaphores. Data moves between devices by JAX's collectives and lax.ppermute only.
A program may use at most 64 MiB of HBM per device.

v0:
```python
import jax
import jax.numpy as jnp
from jax import lax
from jax.sharding import PartitionSpec as P


def padded_2(shard, sides, width):
    for axis, dim in sides:
        devices, length = (lax.axis_size(axis), shard.shape[dim])
        up = [(i, (i + 1) % devices) for i in range(devices - 1)]
        down = [(j, i) for i, j in up]
        last = lax.slice_in_dim(shard, length - width, length, axis=dim)
        first = lax.slice_in_dim(shard, 0, width, axis=dim)
        before = lax.ppermute(last, axis, up)
        after = lax.ppermute(first, axis, down)
        shard = jnp.concatenate([before, shard, after], axis=dim)
    return shard


def activate(values):
    return jax.nn.gelu(values, approximate=True)


def stack_depth(field):
    depth = field.shape[-2]
    widths = [(0, 0)] * (field.ndim - 2) + [(1, 1), (0, 0)]
    padded = jnp.pad(field, widths)
    return jnp.concatenate([padded[..., shift : shift + depth, :] for shift in range(3)], axis=-1)


def volume_conv(extended, weight):
    rows = extended.shape[0] - 2
    across = extended.shape[1]
    depth = extended.shape[2]
    channels = weight.shape[-1]
    stacked = stack_depth(jnp.pad(extended, ((0, 0), (1, 1), (0, 0), (0, 0))))
    kernel = weight.reshape(3, 3, 3 * channels, channels)
    total = None
    for along_x in range(3):
        for along_y in range(3):
            window = stacked[along_x : along_x + rows, along_y : along_y + across].reshape(
                -1, 3 * channels
            )
            term = jnp.dot(window, kernel[along_x, along_y], preferred_element_type=jnp.float32)
            total = term if total is None else total + term
    return total.reshape(rows, across, depth, channels)


def plane_conv(extended, weight):
    rows = extended.shape[0] - 2
    depth = extended.shape[1]
    channels = weight.shape[-1]
    stacked = stack_depth(extended)
    kernel = weight.reshape(3, 3 * channels, channels)
    total = None
    for along in range(3):
        window = stacked[along : along + rows].reshape(-1, 3 * channels)
        term = jnp.dot(window, kernel[along], preferred_element_type=jnp.float32)
        total = term if total is None else total + term
    return total.reshape(rows, depth, channels)


def with_faces(field):
    return padded_2(field, (("gx", 0),), 1)


def replicated_plane(norm_sum, weighted, weight):
    pooled = (weighted / norm_sum).astype(jnp.bfloat16)
    extended = jnp.pad(pooled, ((1, 1), (0, 0), (0, 0)))
    return plane_conv(extended, weight).astype(jnp.bfloat16)


def on_device(
    voxels,
    prior,
    conv_first,
    conv_second,
    score_x,
    score_y,
    plane_yz_w,
    plane_xz_w,
    norm_gain,
    mlp_in,
    mlp_out,
):
    rows, across, depth, channels = voxels.shape
    first = activate(volume_conv(with_faces(voxels), conv_first)).astype(jnp.bfloat16)
    feature_in = with_faces(first)
    feature = (volume_conv(feature_in, conv_second) + voxels.astype(jnp.float32)).astype(
        jnp.bfloat16
    )
    flat = feature.reshape(-1, channels)
    logit_x = (
        jnp.dot(flat, score_x, preferred_element_type=jnp.float32).reshape(voxels.shape)
        + prior[..., None]
    )
    logit_y = (
        jnp.dot(flat, score_y, preferred_element_type=jnp.float32).reshape(voxels.shape)
        + prior[..., None]
    )
    feature_f = feature.astype(jnp.float32)
    pooled_xz = jnp.sum(jax.nn.softmax(logit_y, axis=1) * feature_f, axis=1).astype(jnp.bfloat16)
    strip = padded_2(pooled_xz, (("gx", 0),), 1)
    plane_xz = plane_conv(strip, plane_xz_w).astype(jnp.bfloat16)
    local_peak = jnp.max(logit_x, axis=0)
    peak = lax.pmax(local_peak.astype(jnp.bfloat16), "gx").astype(local_peak.dtype)
    weights = jnp.exp(logit_x - peak)
    norm_sum, weighted = lax.psum(
        (jnp.sum(weights, axis=0), jnp.sum(weights * feature_f, axis=0)), "gx"
    )
    plane_yz = replicated_plane(norm_sum, weighted, plane_yz_w)
    mixing = plane_yz.astype(jnp.float32)[None] + plane_xz.astype(jnp.float32)[:, None]
    joined = feature_f * mixing
    scale = lax.rsqrt(jnp.mean(joined * joined, axis=-1, keepdims=True) + 1e-06)
    normed = (joined * scale * norm_gain).astype(jnp.bfloat16)
    hidden = activate(
        jnp.dot(normed.reshape(-1, channels), mlp_in, preferred_element_type=jnp.float32)
    ).astype(jnp.bfloat16)
    update = jnp.dot(hidden, mlp_out, preferred_element_type=jnp.float32).reshape(voxels.shape)
    return (joined + update).astype(jnp.bfloat16)


def solution(mesh):
    return jax.shard_map(
        on_device,
        mesh=mesh,
        in_specs=(
            P(("scene", "gx"), None, None, None),
            P(("scene", "gx"), None, None),
            P(),
            P(),
            P(),
            P(),
            P(),
            P(),
            P(),
            P(),
            P(),
        ),
        out_specs=P(("scene", "gx"), None, None, None),
        check_vma=False,
    )
```

profile of v0, /device:TPU:0, one launch (start us, length us, event | category | flops | bytes accessed | tf_op | source)
XLA Modules:
  0.0 260.2 jit_solution(5800322310936605871)
XLA Ops:
  6.5 1.1 fusion.73
  7.6 2.4 collective-permute-start
  10.1 1.3 collective-permute-start.1
  11.4 4.2 %collective-permute-done.1 = bf16[1,128,8,128]{3,2,1,0:T(8,128)(2,1)S(1)} collective-permute-done((bf16[1,128,8,128]{3,2,1,0:T(8,128)(2,1)S(1)}, bf16[1,128,8,128]{3,2,1,0:T(8,128)(2,1)S(1)}, u32[]{:S(2)}, u32[]{:S(2)}) %collective-permute-start.1) | collective-permute-done | bytes 262176 | tf_op jit(solution)/shard_map/ppermute | solution.py:15
  15.6 1.1 fusion.25
  17.2 0.6 pad_maximum_fusion
  17.8 1.8 fusion.70
  20.8 0.6 convolution_add_fusion.14
  21.9 0.6 convolution_add_fusion.12
  22.5 0.6 convolution_add_fusion.11
  23.7 0.6 convolution_add_fusion.9
  24.3 0.6 convolution_add_fusion.8
  25.3 6.7 %collective-permute-start.2 = (bf16[1,128,8,128]{3,2,1,0:T(8,128)(2,1)S(1)}, bf16[1,128,8,128]{3,2,1,0:T(8,128)(2,1)S(1)}, u32[]{:S(2)}, u32[]{:S(2)}) collective-permute-start(bf16[1,128,8,128]{3,2,1,0:T(8,128)(2,1)S(1)} %get-tuple-element.34), channel_id=1, source_target_pairs={{0,1},{1,2},{2,3},{3,4},{4,5},{5,6},{6,7},{7,8},{8,9},{9,10},{10,1... | collective-permute-start | bytes 786440 | tf_op jit(solution)/shard_map/ppermute | solution.py:14
  32.0 1.5 collective-permute-start.3
  33.5 1.9 collective-permute-done.3
  36.4 1.8 fusion.69
  39.4 0.6 convolution_add_fusion.6
  39.9 0.6 convolution_add_fusion.5
  41.1 0.6 convolution_add_fusion.3
  44.3 0.6 fusion.78
  44.9 7.0 %collective-permute-start.4 = (bf16[1,8,128]{2,1,0:T(8,128)(2,1)S(1)}, bf16[1,8,128]{2,1,0:T(8,128)(2,1)S(1)}, u32[]{:S(2)}, u32[]{:S(2)}) collective-permute-start(bf16[1,8,128]{2,1,0:T(8,128)(2,1)S(1)} %get-tuple-element.48), channel_id=1, source_target_pairs={{0,1},{1,2},{2,3},{3,4},{4,5},{5,6},{6,7},{7,8},{8,9},{9,10},{10,1... | collective-permute-start | bytes 6152 | tf_op jit(solution)/shard_map/ppermute | solution.py:14
  51.8 1.3 collective-permute-start.5
  53.2 1.1 fusion.81
  54.9 92.3 %all-reduce.11.cloned.1.call-done = bf16[128,8,128]{2,0,1:T(8,128)(2,1)} async-done(((bf16[128,8,128]{2,0,1:T(8,128)(2,1)}), bf16[128,8,128]{2,0,1:T(8,128)(2,1)}) %all-reduce.11.cloned.1.call-update) | async-done | bytes 262160 | tf_op jit(solution)/shard_map/pmax | solution.py:106
  147.2 1.0 convert_element_type.86
  148.2 1.3 fusion.37
  149.9 95.1 %all-reduce.13.cloned.1.call-done = (f32[128,8,128]{2,0,1:T(8,128)}, f32[128,8,128]{2,0,1:T(8,128)}) async-done(((f32[128,8,128]{2,0,1:T(8,128)}, f32[128,8,128]{2,0,1:T(8,128)}), (f32[128,8,128]{2,0,1:T(8,128)}, f32[128,8,128]{2,0,1:T(8,128)})) %all-reduce.13.cloned.1.call-update) | async-done | bytes 1048592 | tf_op jit(solution)/shard_map/psum | solution.py:108
  245.0 1.3 divide_convert_fusion
  247.7 0.6 convolution_add_fusion.19
  248.3 0.6 fusion.17
  250.2 1.7 fusion.11
  252.2 1.1 copy.36
  (67 shorter events, 12.4 us)
Async XLA Ops:
  6.5 243.5 %copy-start = (bf16[512,128]{1,0:T(8,128)(2,1)S(1)}, bf16[512,128]{1,0:T(8,128)(2,1)}, u32[]{:S(2)}) copy-start(bf16[512,128]{1,0:T(8,128)(2,1)} %param.21) | copy-start | bytes 393220
  6.5 140.7 %all-reduce.11.cloned.1.call-start = ((), (), s32[]{:S(2)}) async-start(), calls=%async_computation | async-start | bytes 524288 | tf_op jit(solution)/shard_map/pmax | solution.py:106
  7.6 3.7 %collective-permute-start = (bf16[1,128,8,128]{3,2,1,0:T(8,128)(2,1)S(1)}, bf16[1,128,8,128]{3,2,1,0:T(8,128)(2,1)S(1)}, u32[]{:S(2)}, u32[]{:S(2)}) collective-permute-start(bf16[1,128,8,128]{3,2,1,0:T(8,128)(2,1)S(1)} %get-tuple-element.36), channel_id=1, source_target_pairs={{0,1},{1,2},{2,3},{3,4},{4,5},{5,6},{6,7},{7,8},{8,9},{9,10},{10,1... | collective-permute-start | bytes 786440 | tf_op jit(solution)/shard_map/ppermute | solution.py:14
  10.1 5.5 %collective-permute-start.1 = (bf16[1,128,8,128]{3,2,1,0:T(8,128)(2,1)S(1)}, bf16[1,128,8,128]{3,2,1,0:T(8,128)(2,1)S(1)}, u32[]{:S(2)}, u32[]{:S(2)}) collective-permute-start(bf16[1,128,8,128]{3,2,1,0:T(8,128)(2,1)S(1)} %get-tuple-element.37), channel_id=1, source_target_pairs={{1,0},{2,1},{3,2},{4,3},{5,4},{6,5},{7,6},{8,7},{9,8},{10,9},{11,1... | collective-permute-start | bytes 786440 | tf_op jit(solution)/shard_map/ppermute | solution.py:15
  17.8 1.8 copy-start.2
  24.8 8.6 %copy-start.4 = (bf16[9,128,128]{2,1,0:T(8,128)(2,1)S(1)}, bf16[9,128,128]{2,1,0:T(8,128)(2,1)}, u32[]{:S(2)}) copy-start(bf16[9,128,128]{2,1,0:T(8,128)(2,1)} %param.17) | copy-start | bytes 884740
  24.9 8.6 %copy-start.5 = (bf16[9,128,128]{2,1,0:T(8,128)(2,1)S(1)}, bf16[9,128,128]{2,1,0:T(8,128)(2,1)}, u32[]{:S(2)}) copy-start(bf16[9,128,128]{2,1,0:T(8,128)(2,1)} %param.18) | copy-start | bytes 884740
  25.3 8.3 %collective-permute-start.2 = (bf16[1,128,8,128]{3,2,1,0:T(8,128)(2,1)S(1)}, bf16[1,128,8,128]{3,2,1,0:T(8,128)(2,1)S(1)}, u32[]{:S(2)}, u32[]{:S(2)}) collective-permute-start(bf16[1,128,8,128]{3,2,1,0:T(8,128)(2,1)S(1)} %get-tuple-element.34), channel_id=1, source_target_pairs={{0,1},{1,2},{2,3},{3,4},{4,5},{5,6},{6,7},{7,8},{8,9},{9,10},{10,1... | collective-permute-start | bytes 786440 | tf_op jit(solution)/shard_map/ppermute | solution.py:14
  32.0 3.4 %collective-permute-start.3 = (bf16[1,128,8,128]{3,2,1,0:T(8,128)(2,1)S(1)}, bf16[1,128,8,128]{3,2,1,0:T(8,128)(2,1)S(1)}, u32[]{:S(2)}, u32[]{:S(2)}) collective-permute-start(bf16[1,128,8,128]{3,2,1,0:T(8,128)(2,1)S(1)} %get-tuple-element.35), channel_id=1, source_target_pairs={{1,0},{2,1},{3,2},{4,3},{5,4},{6,5},{7,6},{8,7},{9,8},{10,9},{11,1... | collective-permute-start | bytes 786440 | tf_op jit(solution)/shard_map/ppermute | solution.py:15
  36.4 1.8 copy-start.3
  42.8 1.0 copy-start.1
  43.4 0.7 copy-start.7
  43.4 0.8 copy-start.10
  44.3 8.9 %copy-start.6 = (bf16[128,128]{1,0:T(8,128)(2,1)S(1)}, bf16[128,128]{1,0:T(8,128)(2,1)}, u32[]{:S(2)}) copy-start(bf16[128,128]{1,0:T(8,128)(2,1)} %param.15) | copy-start | bytes 98308
  44.9 9.6 %collective-permute-start.4 = (bf16[1,8,128]{2,1,0:T(8,128)(2,1)S(1)}, bf16[1,8,128]{2,1,0:T(8,128)(2,1)S(1)}, u32[]{:S(2)}, u32[]{:S(2)}) collective-permute-start(bf16[1,8,128]{2,1,0:T(8,128)(2,1)S(1)} %get-tuple-element.48), channel_id=1, source_target_pairs={{0,1},{1,2},{2,3},{3,4},{4,5},{5,6},{6,7},{7,8},{8,9},{9,10},{10,1... | collective-permute-start | bytes 6152 | tf_op jit(solution)/shard_map/ppermute | solution.py:14
  51.8 3.1 %collective-permute-start.5 = (bf16[1,8,128]{2,1,0:T(8,128)(2,1)S(1)}, bf16[1,8,128]{2,1,0:T(8,128)(2,1)S(1)}, u32[]{:S(2)}, u32[]{:S(2)}) collective-permute-start(bf16[1,8,128]{2,1,0:T(8,128)(2,1)S(1)} %get-tuple-element.49), channel_id=1, source_target_pairs={{1,0},{2,1},{3,2},{4,3},{5,4},{6,5},{7,6},{8,7},{9,8},{10,9},{11,1... | collective-permute-start | bytes 6152 | tf_op jit(solution)/shard_map/ppermute | solution.py:15
  54.2 190.8 %all-reduce.13.cloned.1.call-start = ((), (), s32[]{:S(2)}) async-start(), calls=%async_computation.1 | async-start | bytes 2097152 | tf_op jit(solution)/shard_map/psum | solution.py:108
  248.2 1.1 copy-start.8
  249.3 0.9 copy-start.9
Sparse Core Ops, SparseCore 0:
  54.4 92.7 all-reduce.10
  150.7 94.2 all-reduce.12
where the time goes:
time: 261 us; the launch traced here: 260 us
  waiting for transfers between devices  194 us (74%)
  starting transfers between devices  20.4 us (8%)
  matrix products  15.8 us (6%)
  between operations  13.9 us (5%)
  local copies, waits for them, and re-layouts  8.71 us (3%)
  other arithmetic  7.42 us (3%)
    psum x1, waiting for transfers between devices, on_device(): lax.psum((jnp.sum(weights, axis=0), jnp.sum(weights * feature_f, axis=0))...  95.1 us
    pmax x1, waiting for transfers between devices, on_device(): lax.pmax(local_peak.astype(jnp.bfloat16), 'gx').astype(local_peak.dtype)  92.3 us
    ppermute x3, starting transfers between devices, padded_2(): before = lax.ppermute(last, axis, up)  16 us
    dot_general x18, matrix products, volume_conv(): jnp.dot(window, kernel[along_x, along_y], preferred_element_type=jnp.floa...  10.3 us
    ppermute x3, waiting for transfers between devices, padded_2(): after = lax.ppermute(first, axis, down)  6.46 us
  transfers between devices with their start and end apart: 8, of which 5 were waited for; matrix products, arithmetic and copies ran while one was open for 1% of the time, Pallas kernels for 0%

commit v1 on v0

--- a/solution.py
+++ b/solution.py
@@ -64,8 +64,52 @@
     return padded_2(field, (("gx", 0),), 1)
 
 
-def replicated_plane(norm_sum, weighted, weight):
-    pooled = (weighted / norm_sum).astype(jnp.bfloat16)
+def swap(values, axis, mask):
+    devices = lax.axis_size(axis)
+    return lax.ppermute(values, axis, [(i, i ^ mask) for i in range(devices)])
+
+
+def merge(own, other):
+    peak, other_peak = own[0], other[0]
+    top = jnp.maximum(peak, other_peak)
+    top_f = top.astype(jnp.float32)
+    scale = jnp.exp(peak.astype(jnp.float32) - top_f)
+    other_scale = jnp.exp(other_peak.astype(jnp.float32) - top_f)
+    return (
+        top,
+        own[1] * scale + other[1].astype(jnp.float32) * other_scale,
+        own[2] * scale + other[2].astype(jnp.float32) * other_scale,
+    )
+
+
+def pool_over_axis(peak, norm_sum, weighted, axis):
+    devices = lax.axis_size(axis)
+    index = lax.axis_index(axis)
+    masks = [1 << bit for bit in range(devices.bit_length() - 1)]
+    parts = (peak, norm_sum, weighted)
+    for mask in masks[:-1]:
+        half = parts[0].shape[0] // 2
+        upper = (index // mask) % 2
+        kept = [lax.dynamic_slice_in_dim(p, upper * half, half, 0) for p in parts]
+        sent = [lax.dynamic_slice_in_dim(p, (1 - upper) * half, half, 0) for p in parts]
+        message = jnp.stack([p.astype(jnp.bfloat16) for p in sent])
+        parts = merge(kept, swap(message, axis, mask))
+    for mask in masks[-1:]:
+        message = jnp.stack([p.astype(jnp.bfloat16) for p in parts])
+        parts = merge(parts, swap(message, axis, mask))
+    pooled = (parts[2] / parts[1]).astype(jnp.bfloat16)
+    for mask in reversed(masks[:-1]):
+        upper = (index // mask) % 2
+        other = swap(pooled, axis, mask)
+        pooled = jnp.where(
+            upper == 1,
+            jnp.concatenate([other, pooled], axis=0),
+            jnp.concatenate([pooled, other], axis=0),
+        )
+    return pooled
+
+
+def replicated_plane(pooled, weight):
     extended = jnp.pad(pooled, ((1, 1), (0, 0), (0, 0)))
     return plane_conv(extended, weight).astype(jnp.bfloat16)
 
@@ -102,13 +146,14 @@
     pooled_xz = jnp.sum(jax.nn.softmax(logit_y, axis=1) * feature_f, axis=1).astype(jnp.bfloat16)
     strip = padded_2(pooled_xz, (("gx", 0),), 1)
     plane_xz = plane_conv(strip, plane_xz_w).astype(jnp.bfloat16)
-    local_peak = jnp.max(logit_x, axis=0)
-    peak = lax.pmax(local_peak.astype(jnp.bfloat16), "gx").astype(local_peak.dtype)
-    weights = jnp.exp(logit_x - peak)
-    norm_sum, weighted = lax.psum(
-        (jnp.sum(weights, axis=0), jnp.sum(weights * feature_f, axis=0)), "gx"
+    peak = jnp.max(logit_x, axis=0)
+    coarse = peak.astype(jnp.bfloat16)
+    shift = jnp.exp(jnp.clip(peak - coarse.astype(jnp.float32), -60.0, 60.0))
+    weights = jnp.exp(logit_x - peak) * shift
+    pooled_yz = pool_over_axis(
+        coarse, jnp.sum(weights, axis=0), jnp.sum(weights * feature_f, axis=0), "gx"
     )
-    plane_yz = replicated_plane(norm_sum, weighted, plane_yz_w)
+    plane_yz = replicated_plane(pooled_yz, plane_yz_w)
     mixing = plane_yz.astype(jnp.float32)[None] + plane_xz.astype(jnp.float32)[:, None]
     joined = feature_f * mixing
     scale = lax.rsqrt(jnp.mean(joined * joined, axis=-1, keepdims=True) + 1e-06)

time: 261 us -> 86.5 us (0.33)
  waiting for transfers between devices: 194 us -> 23.6 us
  between operations: 13.9 us -> 0.81 us
  starting transfers between devices: 20.4 us -> 32.6 us
    psum x1 -> x0, waiting for transfers between devices: 95.1 us -> none  [on_device(): lax.psum((jnp.sum(weights, axis=0), jnp.sum(weights * feature_f, axis=0))...]
    pmax x1 -> x0, waiting for transfers between devices: 92.3 us -> none  [on_device(): lax.pmax(local_peak.astype(jnp.bfloat16), 'gx').astype(local_peak.dtype)]
    ppermute x0 -> x7, waiting for transfers between devices: none -> 17.5 us  [swap(): return lax.ppermute(values, axis, [(i, i ^ mask) for i in range(devices)])]
    ppermute x0 -> x7, starting transfers between devices: none -> 16.7 us  [swap(): return lax.ppermute(values, axis, [(i, i ^ mask) for i in range(devices)])]
    ppermute x3, starting transfers between devices: 16 us -> 11.7 us  [padded_2(): before = lax.ppermute(last, axis, up)]
  transfers between devices with their start and end apart: 8 -> 13, of which waited for: 5 -> 8; matrix products, arithmetic and copies ran while one was open for 1% -> 2% of each run, Pallas kernels for 0% -> 0%
where the time goes in v1:
time: 86.5 us; the launch traced here: 86 us
  starting transfers between devices  32.6 us (38%)
  waiting for transfers between devices  23.6 us (27%)
  matrix products  15.1 us (17%)
  local copies, waits for them, and re-layouts  8.86 us (10%)
  other arithmetic  5.02 us (6%)
    ppermute x7, waiting for transfers between devices, swap(): return lax.ppermute(values, axis, [(i, i ^ mask) for i in range(devices)])  17.5 us
    ppermute x7, starting transfers between devices, swap(): return lax.ppermute(values, axis, [(i, i ^ mask) for i in range(devices)])  16.7 us
    ppermute x3, starting transfers between devices, padded_2(): before = lax.ppermute(last, axis, up)  11.7 us
    dot_general x18, matrix products, volume_conv(): jnp.dot(window, kernel[along_x, along_y], preferred_element_type=jnp.floa...  10.3 us
    ppermute x3, waiting for transfers between devices, padded_2(): after = lax.ppermute(first, axis, down)  6.08 us
    ppermute x3, starting transfers between devices, padded_2(): after = lax.ppermute(first, axis, down)  4.28 us
    slice x2, local copies, waits for them, and re-layouts, volume_conv(): stacked[along_x:along_x + rows, along_y:along_y + across]  3.6 us
    dot_general x6, matrix products, plane_conv(): term = jnp.dot(window, kernel[along], preferred_element_type=jnp.float32)  2.12 us
  transfers between devices with their start and end apart: 13, of which 8 were waited for; matrix products, arithmetic and copies ran while one was open for 2% of the time, Pallas kernels for 0%

profile of v1, /device:TPU:0, one launch (start us, length us, event | category | flops | bytes accessed | tf_op | source)
XLA Modules:
  0.0 86.0 jit_solution(17848877437167479569)
XLA Ops:
  0.0 1.1 %fusion.104 = (bf16[1,128,8,128]{3,2,1,0:T(8,128)(2,1)S(1)}, bf16[1,128,8,128]{3,2,1,0:T(8,128)(2,1)S(1)}) fusion(bf16[2,128,8,128]{3,2,1,0:T(8,128)(2,1)} %param.11), kind=kLoop, calls=%fused_computation.213 | loop fusion | bytes 1048576 | tf_op jit(solution)/shard_map/slice | solution.py:12
  1.1 2.4 %collective-permute-start = (bf16[1,128,8,128]{3,2,1,0:T(8,128)(2,1)S(1)}, bf16[1,128,8,128]{3,2,1,0:T(8,128)(2,1)S(1)}, u32[]{:S(2)}, u32[]{:S(2)}) collective-permute-start(bf16[1,128,8,128]{3,2,1,0:T(8,128)(2,1)S(1)} %get-tuple-element.42), channel_id=1, source_target_pairs={{0,1},{1,2},{2,3},{3,4},{4,5},{5,6},{6,7},{7,8},{8,9},{9,10},{10,1... | collective-permute-start | bytes 786440 | tf_op jit(solution)/shard_map/ppermute | solution.py:14
  3.5 1.3 %collective-permute-start.1 = (bf16[1,128,8,128]{3,2,1,0:T(8,128)(2,1)S(1)}, bf16[1,128,8,128]{3,2,1,0:T(8,128)(2,1)S(1)}, u32[]{:S(2)}, u32[]{:S(2)}) collective-permute-start(bf16[1,128,8,128]{3,2,1,0:T(8,128)(2,1)S(1)} %get-tuple-element.43), channel_id=1, source_target_pairs={{1,0},{2,1},{3,2},{4,3},{5,4},{6,5},{7,6},{8,7},{9,8},{10,9},{11,1... | collective-permute-start | bytes 786440 | tf_op jit(solution)/shard_map/ppermute | solution.py:15
  4.8 4.2 %collective-permute-done.1 = bf16[1,128,8,128]{3,2,1,0:T(8,128)(2,1)S(1)} collective-permute-done((bf16[1,128,8,128]{3,2,1,0:T(8,128)(2,1)S(1)}, bf16[1,128,8,128]{3,2,1,0:T(8,128)(2,1)S(1)}, u32[]{:S(2)}, u32[]{:S(2)}) %collective-permute-start.1) | collective-permute-done | bytes 262176 | tf_op jit(solution)/shard_map/ppermute | solution.py:15
  9.1 1.1 %fusion.25 = bf16[4,130,8,128]{3,2,1,0:T(8,128)(2,1)S(1)} fusion(bf16[1,128,8,128]{3,2,1,0:T(8,128)(2,1)S(1)} %collective-permute-done.1, bf16[2,128,8,128]{3,2,1,0:T(8,128)(2,1)} %param.11, bf16[1,128,8,128]{3,2,1,0:T(8,128)(2,1)S(1)} %collective-permute-done), kind=kLoop, calls=%fused_computation.62 | loop fusion | flops 6389760 | bytes 2113536 | tf_op jit(solution)/shard_map/concatenate | solution.py:16
  11.1 1.8 %fusion.100 = (bf16[2,128,8,384]{3,2,1,0:T(8,128)(2,1)S(1)}, bf16[2,128,8,384]{3,2,1,0:T(8,128)(2,1)S(1)}, bf16[2,128,8,384]{3,2,1,0:T(8,128)(2,1)S(1)}, bf16[2,...) fusion(bf16[4,130,8,384]{3,2,1,0:T(8,128)(2,1)S(1)} %pad_maximu, ...), kind=kLoop, calls=%fused_computation.209 | loop fusion | bytes 28311552 | tf_op jit(solution)/shard_map/slice | solution.py:41
  15.2 0.6 convolution_add_fusion.12
  15.8 0.6 convolution_add_fusion.11
  17.0 0.6 convolution_add_fusion.9
  18.6 6.7 %collective-permute-start.2 = (bf16[1,128,8,128]{3,2,1,0:T(8,128)(2,1)S(1)}, bf16[1,128,8,128]{3,2,1,0:T(8,128)(2,1)S(1)}, u32[]{:S(2)}, u32[]{:S(2)}) collective-permute-start(bf16[1,128,8,128]{3,2,1,0:T(8,128)(2,1)S(1)} %get-tuple-element.40), channel_id=1, source_target_pairs={{0,1},{1,2},{2,3},{3,4},{4,5},{5,6},{6,7},{7,8},{8,9},{9,10},{10,1... | collective-permute-start | bytes 786440 | tf_op jit(solution)/shard_map/ppermute | solution.py:14
  25.2 1.5 %collective-permute-start.3 = (bf16[1,128,8,128]{3,2,1,0:T(8,128)(2,1)S(1)}, bf16[1,128,8,128]{3,2,1,0:T(8,128)(2,1)S(1)}, u32[]{:S(2)}, u32[]{:S(2)}) collective-permute-start(bf16[1,128,8,128]{3,2,1,0:T(8,128)(2,1)S(1)} %get-tuple-element.41), channel_id=1, source_target_pairs={{1,0},{2,1},{3,2},{4,3},{5,4},{6,5},{7,6},{8,7},{9,8},{10,9},{11,1... | collective-permute-start | bytes 786440 | tf_op jit(solution)/shard_map/ppermute | solution.py:15
  26.8 1.8 %collective-permute-done.3 = bf16[1,128,8,128]{3,2,1,0:T(8,128)(2,1)S(1)} collective-permute-done((bf16[1,128,8,128]{3,2,1,0:T(8,128)(2,1)S(1)}, bf16[1,128,8,128]{3,2,1,0:T(8,128)(2,1)S(1)}, u32[]{:S(2)}, u32[]{:S(2)}) %collective-permute-start.3) | collective-permute-done | bytes 262176 | tf_op jit(solution)/shard_map/ppermute | solution.py:15
  29.7 1.8 %fusion.99 = (bf16[2,128,8,384]{3,2,1,0:T(8,128)(2,1)S(1)}, bf16[2,128,8,384]{3,2,1,0:T(8,128)(2,1)S(1)}, bf16[2,128,8,384]{3,2,1,0:T(8,128)(2,1)S(1)}, bf16[2,1...) fusion(bf16[4,130,8,384]{3,2,1,0:T(8,128)(2,1)S(1)} %pad_maximu, ...), kind=kLoop, calls=%fused_computation.208 | loop fusion | bytes 28311552 | tf_op jit(solution)/shard_map/slice | solution.py:41
  38.5 5.1 %collective-permute-start.4 = (bf16[3,64,8,128]{3,1,2,0:T(8,128)(2,1)S(1)}, bf16[3,64,8,128]{3,1,2,0:T(8,128)(2,1)S(1)}, u32[]{:S(2)}, u32[]{:S(2)}) collective-permute-start(bf16[3,64,8,128]{3,1,2,0:T(8,128)(2,1)S(1)} %pad_maximum_fusion.3), channel_id=1, source_target_pairs={{0,1},{1,0},{2,3},{3,2},{4,5},{5,4},{6,7},{7,6},{8,9},{9,8},{10,11... | collective-permute-start | bytes 1179656 | tf_op jit(solution)/shard_map/ppermute | solution.py:69
  43.6 0.6 fusion.109
  44.3 2.6 %collective-permute-start.11 = (bf16[1,8,128]{2,1,0:T(8,128)(2,1)S(1)}, bf16[1,8,128]{2,1,0:T(8,128)(2,1)S(1)}, u32[]{:S(2)}, u32[]{:S(2)}) collective-permute-start(bf16[1,8,128]{2,1,0:T(8,128)(2,1)S(1)} %get-tuple-element.54), channel_id=1, source_target_pairs={{0,1},{1,2},{2,3},{3,4},{4,5},{5,6},{6,7},{7,8},{8,9},{9,10},{10,1... | collective-permute-start | bytes 6152 | tf_op jit(solution)/shard_map/ppermute | solution.py:14
  46.9 1.5 %collective-permute-start.12 = (bf16[1,8,128]{2,1,0:T(8,128)(2,1)S(1)}, bf16[1,8,128]{2,1,0:T(8,128)(2,1)S(1)}, u32[]{:S(2)}, u32[]{:S(2)}) collective-permute-start(bf16[1,8,128]{2,1,0:T(8,128)(2,1)S(1)} %get-tuple-element.55), channel_id=1, source_target_pairs={{1,0},{2,1},{3,2},{4,3},{5,4},{6,5},{7,6},{8,7},{9,8},{10,9},{11,1... | collective-permute-start | bytes 6152 | tf_op jit(solution)/shard_map/ppermute | solution.py:15
  48.8 4.4 %collective-permute-start.5 = (bf16[3,32,8,128]{3,1,2,0:T(8,128)(2,1)S(1)}, bf16[3,32,8,128]{3,1,2,0:T(8,128)(2,1)S(1)}, u32[]{:S(2)}, u32[]{:S(2)}) collective-permute-start(bf16[3,32,8,128]{3,1,2,0:T(8,128)(2,1)S(1)} %pad_maximum_fusion.4), channel_id=1, source_target_pairs={{0,2},{1,3},{2,0},{3,1},{4,6},{5,7},{6,4},{7,5},{8,10},{9,11},{10,... | collective-permute-start | bytes 589832 | tf_op jit(solution)/shard_map/ppermute | solution.py:69
  53.3 5.1 %collective-permute-done.5 = bf16[3,32,8,128]{3,1,2,0:T(8,128)(2,1)S(1)} collective-permute-done((bf16[3,32,8,128]{3,1,2,0:T(8,128)(2,1)S(1)}, bf16[3,32,8,128]{3,1,2,0:T(8,128)(2,1)S(1)}, u32[]{:S(2)}, u32[]{:S(2)}) %collective-permute-start.5) | collective-permute-done | bytes 196640 | tf_op jit(solution)/shard_map/ppermute | solution.py:69
  58.6 1.6 %collective-permute-start.6 = (bf16[3,16,8,128]{3,1,2,0:T(8,128)(2,1)S(1)}, bf16[3,16,8,128]{3,1,2,0:T(8,128)(2,1)S(1)}, u32[]{:S(2)}, u32[]{:S(2)}) collective-permute-start(bf16[3,16,8,128]{3,1,2,0:T(8,128)(2,1)S(1)} %pad_maximum_fusion.5), channel_id=1, source_target_pairs={{0,4},{1,5},{2,6},{3,7},{4,0},{5,1},{6,2},{7,3},{8,12},{9,13},{10,... | collective-permute-start | bytes 294920 | tf_op jit(solution)/shard_map/ppermute | solution.py:69
  60.3 3.0 %collective-permute-done.6 = bf16[3,16,8,128]{3,1,2,0:T(8,128)(2,1)S(1)} collective-permute-done((bf16[3,16,8,128]{3,1,2,0:T(8,128)(2,1)S(1)}, bf16[3,16,8,128]{3,1,2,0:T(8,128)(2,1)S(1)}, u32[]{:S(2)}, u32[]{:S(2)}) %collective-permute-start.6) | collective-permute-done | bytes 98336 | tf_op jit(solution)/shard_map/ppermute | solution.py:69
  63.4 2.7 %collective-permute-start.7 = (bf16[3,16,8,128]{3,1,2,0:T(8,128)(2,1)S(1)}, bf16[3,16,8,128]{3,1,2,0:T(8,128)(2,1)S(1)}, u32[]{:S(2)}, u32[]{:S(2)}) collective-permute-start(bf16[3,16,8,128]{3,1,2,0:T(8,128)(2,1)S(1)} %pad_maximum_fusion.6), channel_id=1, source_target_pairs={{0,8},{1,9},{2,10},{3,11},{4,12},{5,13},{6,14},{7,15},{8,0},{9,1},... | collective-permute-start | bytes 294920 | tf_op jit(solution)/shard_map/ppermute | solution.py:69
  66.1 2.9 %collective-permute-done.7 = bf16[3,16,8,128]{3,1,2,0:T(8,128)(2,1)S(1)} collective-permute-done((bf16[3,16,8,128]{3,1,2,0:T(8,128)(2,1)S(1)}, bf16[3,16,8,128]{3,1,2,0:T(8,128)(2,1)S(1)}, u32[]{:S(2)}, u32[]{:S(2)}) %collective-permute-start.7) | collective-permute-done | bytes 98336 | tf_op jit(solution)/shard_map/ppermute | solution.py:69
  69.1 1.7 %collective-permute-start.8 = (bf16[16,8,128]{2,0,1:T(8,128)(2,1)S(1)}, bf16[16,8,128]{2,0,1:T(8,128)(2,1)S(1)}, u32[]{:S(2)}, u32[]{:S(2)}) collective-permute-start(bf16[16,8,128]{2,0,1:T(8,128)(2,1)S(1)} %fusion.66), channel_id=1, source_target_pairs={{0,4},{1,5},{2,6},{3,7},{4,0},{5,1},{6,2},{7,3},{8,12},{9,13},{10,... | collective-permute-start | bytes 98312 | tf_op jit(solution)/shard_map/ppermute | solution.py:69
  70.9 2.2 %collective-permute-done.8 = bf16[16,8,128]{2,0,1:T(8,128)(2,1)S(1)} collective-permute-done((bf16[16,8,128]{2,0,1:T(8,128)(2,1)S(1)}, bf16[16,8,128]{2,0,1:T(8,128)(2,1)S(1)}, u32[]{:S(2)}, u32[]{:S(2)}) %collective-permute-start.8) | collective-permute-done | bytes 32800 | tf_op jit(solution)/shard_map/ppermute | solution.py:69
  73.1 1.1 %collective-permute-start.9 = (bf16[32,8,128]{2,0,1:T(8,128)(2,1)S(1)}, bf16[32,8,128]{2,0,1:T(8,128)(2,1)S(1)}, u32[]{:S(2)}, u32[]{:S(2)}) collective-permute-start(bf16[32,8,128]{2,0,1:T(8,128)(2,1)S(1)} %maximum_select_fusion.2), channel_id=1, source_target_pairs={{0,2},{1,3},{2,0},{3,1},{4,6},{5,7},{6,4},{7,5},{8,10},{9,11},{10,... | collective-permute-start | bytes 196616 | tf_op jit(solution)/shard_map/ppermute | solution.py:69
  74.4 3.1 %collective-permute-done.9 = bf16[32,8,128]{2,0,1:T(8,128)(2,1)S(1)} collective-permute-done((bf16[32,8,128]{2,0,1:T(8,128)(2,1)S(1)}, bf16[32,8,128]{2,0,1:T(8,128)(2,1)S(1)}, u32[]{:S(2)}, u32[]{:S(2)}) %collective-permute-start.9) | collective-permute-done | bytes 65568 | tf_op jit(solution)/shard_map/ppermute | solution.py:69
  77.7 1.2 %collective-permute-done.10 = bf16[64,8,128]{2,0,1:T(8,128)(2,1)S(1)} collective-permute-done((bf16[64,8,128]{2,0,1:T(8,128)(2,1)S(1)}, bf16[64,8,128]{2,0,1:T(8,128)(2,1)S(1)}, u32[]{:S(2)}, u32[]{:S(2)}) %collective-permute-start.10) | collective-permute-done | bytes 131104 | tf_op jit(solution)/shard_map/ppermute | solution.py:69
  80.4 0.6 convolution_add_fusion.19
  81.0 0.6 fusion.17
  82.9 1.7 %fusion.11 = f32[2048,128]{1,0:T(8,128)S(1)} fusion(bf16[512,128]{1,0:T(8,128)(2,1)S(1)} %copy-done, bf16[2048,128]{1,0:T(8,128)(2,1)S(1)} %bitcast.313, bf16[128,512]{1,0:T(8,128)(2,1)S(1)} %copy-done.9), kind=kOutput, calls=%fused_computation.40 | convolution fusion | flops 546308096 | bytes 1835008 | tf_op jit(solution)/shard_map/dot_general | solution.py:164
  84.9 1.1 %copy.32 = bf16[2,128,8,128]{3,2,1,0:T(8,128)(2,1)} copy(bf16[2,128,8,128]{3,1,2,0:T(8,128)(2,1)S(1)} %fusion.35) | data formatting | bytes 1048576 | tf_op jit(solution)/shard_map/convert_element_type | solution.py:165
  (96 shorter events, 16.9 us)
Async XLA Ops:
  0.0 82.8 %copy-start = (bf16[512,128]{1,0:T(8,128)(2,1)S(1)}, bf16[512,128]{1,0:T(8,128)(2,1)}, u32[]{:S(2)}) copy-start(bf16[512,128]{1,0:T(8,128)(2,1)} %param.21) | copy-start | bytes 393220
  1.1 3.7 %collective-permute-start = (bf16[1,128,8,128]{3,2,1,0:T(8,128)(2,1)S(1)}, bf16[1,128,8,128]{3,2,1,0:T(8,128)(2,1)S(1)}, u32[]{:S(2)}, u32[]{:S(2)}) collective-permute-start(bf16[1,128,8,128]{3,2,1,0:T(8,128)(2,1)S(1)} %get-tuple-element.42), channel_id=1, source_target_pairs={{0,1},{1,2},{2,3},{3,4},{4,5},{5,6},{6,7},{7,8},{8,9},{9,10},{10,1... | collective-permute-start | bytes 786440 | tf_op jit(solution)/shard_map/ppermute | solution.py:14
  3.5 5.5 %collective-permute-start.1 = (bf16[1,128,8,128]{3,2,1,0:T(8,128)(2,1)S(1)}, bf16[1,128,8,128]{3,2,1,0:T(8,128)(2,1)S(1)}, u32[]{:S(2)}, u32[]{:S(2)}) collective-permute-start(bf16[1,128,8,128]{3,2,1,0:T(8,128)(2,1)S(1)} %get-tuple-element.43), channel_id=1, source_target_pairs={{1,0},{2,1},{3,2},{4,3},{5,4},{6,5},{7,6},{8,7},{9,8},{10,9},{11,1... | collective-permute-start | bytes 786440 | tf_op jit(solution)/shard_map/ppermute | solution.py:15
  11.1 1.8 %copy-start.2 = (bf16[27,128,128]{2,1,0:T(8,128)(2,1)S(1)}, bf16[27,128,128]{2,1,0:T(8,128)(2,1)}, u32[]{:S(2)}) copy-start(bf16[27,128,128]{2,1,0:T(8,128)(2,1)} %param.13) | copy-start | bytes 2654212
  18.1 8.6 %copy-start.4 = (bf16[9,128,128]{2,1,0:T(8,128)(2,1)S(1)}, bf16[9,128,128]{2,1,0:T(8,128)(2,1)}, u32[]{:S(2)}) copy-start(bf16[9,128,128]{2,1,0:T(8,128)(2,1)} %param.17) | copy-start | bytes 884740
  18.6 8.3 %collective-permute-start.2 = (bf16[1,128,8,128]{3,2,1,0:T(8,128)(2,1)S(1)}, bf16[1,128,8,128]{3,2,1,0:T(8,128)(2,1)S(1)}, u32[]{:S(2)}, u32[]{:S(2)}) collective-permute-start(bf16[1,128,8,128]{3,2,1,0:T(8,128)(2,1)S(1)} %get-tuple-element.40), channel_id=1, source_target_pairs={{0,1},{1,2},{2,3},{3,4},{4,5},{5,6},{6,7},{7,8},{8,9},{9,10},{10,1... | collective-permute-start | bytes 786440 | tf_op jit(solution)/shard_map/ppermute | solution.py:14
  25.2 3.4 %collective-permute-start.3 = (bf16[1,128,8,128]{3,2,1,0:T(8,128)(2,1)S(1)}, bf16[1,128,8,128]{3,2,1,0:T(8,128)(2,1)S(1)}, u32[]{:S(2)}, u32[]{:S(2)}) collective-permute-start(bf16[1,128,8,128]{3,2,1,0:T(8,128)(2,1)S(1)} %get-tuple-element.41), channel_id=1, source_target_pairs={{1,0},{2,1},{3,2},{4,3},{5,4},{6,5},{7,6},{8,7},{9,8},{10,9},{11,1... | collective-permute-start | bytes 786440 | tf_op jit(solution)/shard_map/ppermute | solution.py:15
  29.7 1.8 %copy-start.3 = (bf16[27,128,128]{2,1,0:T(8,128)(2,1)S(1)}, bf16[27,128,128]{2,1,0:T(8,128)(2,1)}, u32[]{:S(2)}) copy-start(bf16[27,128,128]{2,1,0:T(8,128)(2,1)} %param.14) | copy-start | bytes 2654212
  36.1 1.0 %copy-start.1 = (bf16[2,128,8,128]{3,2,1,0:T(8,128)(2,1)S(1)}, bf16[2,128,8,128]{3,2,1,0:T(8,128)(2,1)}, u32[]{:S(2)}) copy-start(bf16[2,128,8,128]{3,2,1,0:T(8,128)(2,1)} %param.11) | copy-start | bytes 1572868
  36.7 0.8 copy-start.6
  36.7 0.8 copy-start.7
  38.4 5.3 %copy-start.10 = (bf16[128,128]{1,0:T(8,128)(2,1)S(1)}, bf16[128,128]{1,0:T(8,128)(2,1)}, u32[]{:S(2)}) copy-start(bf16[128,128]{1,0:T(8,128)(2,1)} %param.16) | copy-start | bytes 98308
  38.5 9.9 %collective-permute-start.4 = (bf16[3,64,8,128]{3,1,2,0:T(8,128)(2,1)S(1)}, bf16[3,64,8,128]{3,1,2,0:T(8,128)(2,1)S(1)}, u32[]{:S(2)}, u32[]{:S(2)}) collective-permute-start(bf16[3,64,8,128]{3,1,2,0:T(8,128)(2,1)S(1)} %pad_maximum_fusion.3), channel_id=1, source_target_pairs={{0,1},{1,0},{2,3},{3,2},{4,5},{5,4},{6,7},{7,6},{8,9},{9,8},{10,11... | collective-permute-start | bytes 1179656 | tf_op jit(solution)/shard_map/ppermute | solution.py:69
  44.3 8.9 %copy-start.5 = (bf16[9,128,128]{2,1,0:T(8,128)(2,1)S(1)}, bf16[9,128,128]{2,1,0:T(8,128)(2,1)}, u32[]{:S(2)}) copy-start(bf16[9,128,128]{2,1,0:T(8,128)(2,1)} %param.18) | copy-start | bytes 884740
  44.3 9.0 %collective-permute-start.11 = (bf16[1,8,128]{2,1,0:T(8,128)(2,1)S(1)}, bf16[1,8,128]{2,1,0:T(8,128)(2,1)S(1)}, u32[]{:S(2)}, u32[]{:S(2)}) collective-permute-start(bf16[1,8,128]{2,1,0:T(8,128)(2,1)S(1)} %get-tuple-element.54), channel_id=1, source_target_pairs={{0,1},{1,2},{2,3},{3,4},{4,5},{5,6},{6,7},{7,8},{8,9},{9,10},{10,1... | collective-permute-start | bytes 6152 | tf_op jit(solution)/shard_map/ppermute | solution.py:14
  46.9 6.4 %collective-permute-start.12 = (bf16[1,8,128]{2,1,0:T(8,128)(2,1)S(1)}, bf16[1,8,128]{2,1,0:T(8,128)(2,1)S(1)}, u32[]{:S(2)}, u32[]{:S(2)}) collective-permute-start(bf16[1,8,128]{2,1,0:T(8,128)(2,1)S(1)} %get-tuple-element.55), channel_id=1, source_target_pairs={{1,0},{2,1},{3,2},{4,3},{5,4},{6,5},{7,6},{8,7},{9,8},{10,9},{11,1... | collective-permute-start | bytes 6152 | tf_op jit(solution)/shard_map/ppermute | solution.py:15
  48.8 9.6 %collective-permute-start.5 = (bf16[3,32,8,128]{3,1,2,0:T(8,128)(2,1)S(1)}, bf16[3,32,8,128]{3,1,2,0:T(8,128)(2,1)S(1)}, u32[]{:S(2)}, u32[]{:S(2)}) collective-permute-start(bf16[3,32,8,128]{3,1,2,0:T(8,128)(2,1)S(1)} %pad_maximum_fusion.4), channel_id=1, source_target_pairs={{0,2},{1,3},{2,0},{3,1},{4,6},{5,7},{6,4},{7,5},{8,10},{9,11},{10,... | collective-permute-start | bytes 589832 | tf_op jit(solution)/shard_map/ppermute | solution.py:69
  58.6 4.7 %collective-permute-start.6 = (bf16[3,16,8,128]{3,1,2,0:T(8,128)(2,1)S(1)}, bf16[3,16,8,128]{3,1,2,0:T(8,128)(2,1)S(1)}, u32[]{:S(2)}, u32[]{:S(2)}) collective-permute-start(bf16[3,16,8,128]{3,1,2,0:T(8,128)(2,1)S(1)} %pad_maximum_fusion.5), channel_id=1, source_target_pairs={{0,4},{1,5},{2,6},{3,7},{4,0},{5,1},{6,2},{7,3},{8,12},{9,13},{10,... | collective-permute-start | bytes 294920 | tf_op jit(solution)/shard_map/ppermute | solution.py:69
  63.4 5.6 %collective-permute-start.7 = (bf16[3,16,8,128]{3,1,2,0:T(8,128)(2,1)S(1)}, bf16[3,16,8,128]{3,1,2,0:T(8,128)(2,1)S(1)}, u32[]{:S(2)}, u32[]{:S(2)}) collective-permute-start(bf16[3,16,8,128]{3,1,2,0:T(8,128)(2,1)S(1)} %pad_maximum_fusion.6), channel_id=1, source_target_pairs={{0,8},{1,9},{2,10},{3,11},{4,12},{5,13},{6,14},{7,15},{8,0},{9,1},... | collective-permute-start | bytes 294920 | tf_op jit(solution)/shard_map/ppermute | solution.py:69
  69.1 4.0 %collective-permute-start.8 = (bf16[16,8,128]{2,0,1:T(8,128)(2,1)S(1)}, bf16[16,8,128]{2,0,1:T(8,128)(2,1)S(1)}, u32[]{:S(2)}, u32[]{:S(2)}) collective-permute-start(bf16[16,8,128]{2,0,1:T(8,128)(2,1)S(1)} %fusion.66), channel_id=1, source_target_pairs={{0,4},{1,5},{2,6},{3,7},{4,0},{5,1},{6,2},{7,3},{8,12},{9,13},{10,... | collective-permute-start | bytes 98312 | tf_op jit(solution)/shard_map/ppermute | solution.py:69
  73.1 4.3 %collective-permute-start.9 = (bf16[32,8,128]{2,0,1:T(8,128)(2,1)S(1)}, bf16[32,8,128]{2,0,1:T(8,128)(2,1)S(1)}, u32[]{:S(2)}, u32[]{:S(2)}) collective-permute-start(bf16[32,8,128]{2,0,1:T(8,128)(2,1)S(1)} %maximum_select_fusion.2), channel_id=1, source_target_pairs={{0,2},{1,3},{2,0},{3,1},{4,6},{5,7},{6,4},{7,5},{8,10},{9,11},{10,... | collective-permute-start | bytes 196616 | tf_op jit(solution)/shard_map/ppermute | solution.py:69
  77.5 1.4 %collective-permute-start.10 = (bf16[64,8,128]{2,0,1:T(8,128)(2,1)S(1)}, bf16[64,8,128]{2,0,1:T(8,128)(2,1)S(1)}, u32[]{:S(2)}, u32[]{:S(2)}) collective-permute-start(bf16[64,8,128]{2,0,1:T(8,128)(2,1)S(1)} %maximum_select_fusion.1), channel_id=1, source_target_pairs={{0,1},{1,0},{2,3},{3,2},{4,5},{5,4},{6,7},{7,6},{8,9},{9,8},{10,11... | collective-permute-start | bytes 393224 | tf_op jit(solution)/shard_map/ppermute | solution.py:69
  80.9 1.1 %copy-start.8 = (f32[128]{0:T(128)S(1)}, f32[128]{0:T(128)}, u32[]{:S(2)}) copy-start(f32[128]{0:T(128)} %param.19) | copy-start | bytes 1540
  82.0 0.9 %copy-start.9 = (bf16[128,512]{1,0:T(8,128)(2,1)S(1)}, bf16[128,512]{1,0:T(8,128)(2,1)}, u32[]{:S(2)}) copy-start(bf16[128,512]{1,0:T(8,128)(2,1)} %param.20) | copy-start | bytes 393220

commit v2 on v0

v2 whole, which is shorter than its diff:
```python
import functools

import jax
import jax.numpy as jnp
from jax import lax
from jax.experimental import pallas as pl
from jax.experimental.pallas import tpu as pltpu
from jax.sharding import PartitionSpec as P

BF = jnp.bfloat16
F32 = jnp.float32
IN_VMEM = pl.BlockSpec(memory_space=pltpu.VMEM)


def activate(values):
    return 0.5 * values * (1.0 + jnp.tanh(0.7978845608028654 * (values + 0.044715 * values**3)))


def beside(blocks):
    return jnp.concatenate(blocks, axis=1)


def shift_depth(before, same, after, shape):
    depth = shape[1]
    place = lax.broadcasted_iota(jnp.int32, shape, 1)
    before = jnp.where(place == 0, 0.0, pltpu.roll(before.reshape(shape), 1, 1))
    after = jnp.where(place == depth - 1, 0.0, pltpu.roll(after.reshape(shape), depth - 1, 1))
    return before + same.reshape(shape) + after


def conv_pair(rows_ref, w_ref, taps, start, span):
    depth, channels = rows_ref.shape[2:]
    shape = (span, depth, channels)
    windows = [
        [rows_ref[r, pl.ds(start + b, span)].reshape(-1, channels) for b in range(3)]
        for r in range(4)
    ]
    zero = jnp.zeros((channels, channels), BF)

    def weight(a, b, c):
        return w_ref[taps[a], 3 * b + c] if 0 <= a < 3 else zero

    def product(rows, left, right):
        lhs = beside([windows[r][b] for r in rows for b in range(3)])
        rhs = jnp.concatenate(
            [
                beside([weight(r - left[0], b, left[1]), weight(r - right[0], b, right[1])])
                for r in rows
                for b in range(3)
            ],
            axis=0,
        )
        total = jnp.dot(lhs, rhs, preferred_element_type=F32)
        return total[:, :channels], total[:, channels:]

    low0, low1 = product((0, 1, 2), (0, 0), (0, 1))
    low2, high0 = product((0, 1, 2, 3), (0, 2), (1, 0))
    high1, high2 = product((1, 2, 3), (1, 1), (1, 2))
    return shift_depth(low0, low1, low2, shape), shift_depth(high0, high1, high2, shape)


def clear_ends(rows_ref):
    rows, length, depth, channels = rows_ref.shape
    blank = jnp.zeros((rows, depth, channels), rows_ref.dtype)
    rows_ref[:, 0] = blank
    rows_ref[:, length - 1] = blank


def first_kernel(axis, own_ref, near_ref, w_ref, out_ref, rows_ref):
    across = own_ref.shape[1]
    side = lax.rem(lax.axis_index(axis), 2)
    clear_ends(rows_ref)
    for row, (source, at) in enumerate(
        ((own_ref, side), (own_ref, 1 - side), (near_ref, side), (near_ref, 1 - side))
    ):
        rows_ref[row, 1 : across + 1] = source[at]
    taps = (2 * side, 1, 2 - 2 * side)
    span = across // 2
    for step in range(2):
        low, high = conv_pair(rows_ref, w_ref, taps, step * span, span)
        out_ref[0, step * span : (step + 1) * span] = activate(low).astype(BF)
        out_ref[1, step * span : (step + 1) * span] = activate(high).astype(BF)


def main_kernel(
    axis,
    first_ref,
    own_ref,
    far_ref,
    w1_ref,
    w2_ref,
    score_ref,
    prior_ref,
    feature_ref,
    message_ref,
    keep_ref,
    strip_ref,
    rows_ref,
    mid_ref,
    logit_ref,
):
    across, depth, channels = own_ref.shape[1:]
    devices = lax.axis_size(axis)
    index = lax.axis_index(axis)
    side = lax.rem(index, 2)
    clear_ends(rows_ref)
    clear_ends(mid_ref)
    for row, (source, at) in enumerate(
        ((own_ref, 1 - side), (own_ref, side), (far_ref, 1 - side), (far_ref, side))
    ):
        rows_ref[row, 1 : across + 1] = source[at]
    mid_ref[2, 1 : across + 1] = first_ref[0]
    mid_ref[3, 1 : across + 1] = first_ref[1]
    span = across // 2
    edge = jnp.logical_or(index == 0, index == devices - 1)
    inside = jnp.where(edge, 0.0, 1.0)
    for step in range(2):
        low, high = conv_pair(rows_ref, w1_ref, (2 - 2 * side, 1, 2 * side), step * span, span)
        mid_ref[1, 1 + step * span : 1 + (step + 1) * span] = activate(low).astype(BF)
        mid_ref[0, 1 + step * span : 1 + (step + 1) * span] = (activate(high) * inside).astype(BF)

    score = score_ref[...]
    tops = [None, None]
    for step in range(2):
        half = 1 - side if step == 0 else side
        start = half * span
        place = pl.ds(start, span)
        outs = conv_pair(mid_ref, w2_ref, (2 * side, 1, 2 - 2 * side), start, span)
        logits, features = [], []
        for u in range(2):
            at = side if u == 0 else 1 - side
            feature = (outs[u] + own_ref[at, place].astype(F32)).astype(BF)
            feature_ref[at, place] = feature
            both = jnp.dot(feature.reshape(-1, channels), score, preferred_element_type=F32)
            columns = prior_ref[at, half]
            prior = jnp.stack(
                [jnp.broadcast_to(columns[:, y : y + 1], (depth, channels)) for y in range(span)]
            )
            logit_y = both[:, channels:].reshape(span, depth, channels) + prior
            logit_ref[u, place] = logit_y
            top = jnp.max(logit_y, axis=0)
            tops[u] = top if tops[u] is None else jnp.maximum(tops[u], top)
            logits.append(both[:, :channels].reshape(span, depth, channels) + prior)
            features.append(feature.astype(F32))
        peak = jnp.maximum(logits[0], logits[1])
        coarse = peak.astype(BF)
        shift = jnp.exp(jnp.clip(peak - coarse.astype(F32), -60.0, 60.0))
        low, high = jnp.exp(logits[0] - peak) * shift, jnp.exp(logits[1] - peak) * shift
        parts = (coarse, low + high, low * features[0] + high * features[1])
        for k, part in enumerate(parts):
            if step == 0:
                message_ref[k * span : (k + 1) * span] = part.astype(BF)
            else:
                keep_ref[k] = part.astype(F32)
    for u in range(2):
        at = side if u == 0 else 1 - side
        weights = jnp.exp(logit_ref[u] - tops[u])
        total = jnp.sum(weights, axis=0)
        pooled = (jnp.sum(weights * feature_ref[at].astype(F32), axis=0) / total).astype(BF)
        strip_ref[u] = pooled
        message_ref[3 * span + 1 - u] = pooled


def last_kernel(
    axis,
    feature_ref,
    pooled_ref,
    strip_ref,
    yz_ref,
    xz_ref,
    gain_ref,
    in_ref,
    out_w_ref,
    out_ref,
    plane_ref,
    mix_ref,
):
    across, depth, channels = feature_ref.shape[1:]
    devices = lax.axis_size(axis)
    index = lax.axis_index(axis)
    side = lax.rem(index, 2)
    bits = devices.bit_length() - 2
    blocks = 1 << bits
    block = across // blocks
    mine = 0
    for bit in range(bits):
        mine = mine * 2 + lax.rem(index // (1 << bit), 2)
    blank = jnp.zeros((depth, channels), BF)
    plane_ref[0] = blank
    plane_ref[across + 1] = blank
    for k in range(blocks):
        place = jnp.bitwise_xor(mine, k)
        plane_ref[pl.ds(1 + place * block, block)] = pooled_ref[k * block : (k + 1) * block]

    def plane_product(windows, weights, shape):
        lhs = beside(windows)
        rhs = jnp.concatenate([beside(w) for w in weights], axis=0)
        total = jnp.dot(lhs, rhs, preferred_element_type=F32)
        parts = [total[:, c * channels : (c + 1) * channels] for c in range(3)]
        return shift_depth(*parts, shape).astype(BF).astype(F32)

    taps = (2 * side, 1, 2 - 2 * side)
    strip = strip_ref[...]
    mixed = plane_product(
        [strip[a : a + 2].reshape(-1, channels) for a in range(3)],
        [[xz_ref[taps[a], c] for c in range(3)] for a in range(3)],
        (2, depth, channels),
    )
    mix_ref[side] = mixed[0]
    mix_ref[1 - side] = mixed[1]
    gain = gain_ref[...]
    span = min(32, across)
    for step in range(across // span):
        start = step * span
        plane = plane_product(
            [plane_ref[start + b : start + b + span].reshape(-1, channels) for b in range(3)],
            [[yz_ref[b, c] for c in range(3)] for b in range(3)],
            (span, depth, channels),
        )
        for row in range(feature_ref.shape[0]):
            feature = feature_ref[row, start : start + span].astype(F32)
            joined = (feature * (plane + mix_ref[row])).reshape(-1, channels)
            mean = jnp.mean(joined * joined, axis=-1, keepdims=True)
            normed = (joined * lax.rsqrt(mean + 1e-06) * gain).astype(BF)
            hidden = activate(jnp.dot(normed, in_ref[...], preferred_element_type=F32)).astype(BF)
            update = jnp.dot(hidden, out_w_ref[...], preferred_element_type=F32)
            out_ref[row, start : start + span] = (
                (joined + update).astype(BF).reshape(span, depth, channels)
            )


def swap(values, axis, mask):
    devices = lax.axis_size(axis)
    return lax.ppermute(values, axis, [(i, i ^ mask) for i in range(devices)])


def merge(own, other):
    peak, other_peak = own[0].astype(F32), other[0].astype(F32)
    top = jnp.maximum(peak, other_peak)
    scale = jnp.exp(peak - top)
    other_scale = jnp.exp(other_peak - top)
    return (
        top,
        own[1] * scale + other[1].astype(F32) * other_scale,
        own[2] * scale + other[2].astype(F32) * other_scale,
    )


def thirds(message):
    size = (message.shape[0] - 1) // 3
    return [message[k * size : (k + 1) * size] for k in range(3)]


def kernel_call(body, outs, scratch, cost, *operands):
    return pl.pallas_call(
        body,
        out_shape=outs,
        in_specs=[IN_VMEM] * len(operands),
        out_specs=jax.tree.map(lambda _: IN_VMEM, outs),
        scratch_shapes=scratch,
        cost_estimate=pl.CostEstimate(
            flops=cost, bytes_accessed=sum(o.size * o.dtype.itemsize for o in operands), transcendentals=0
        ),
    )(*operands)


def on_device(
    axis,
    voxels,
    prior,
    conv_first,
    conv_second,
    score_x,
    score_y,
    plane_yz_w,
    plane_xz_w,
    norm_gain,
    mlp_in,
    mlp_out,
):
    rows, across, depth, channels = voxels.shape
    devices = lax.axis_size(axis)
    if rows != 2 or devices & (devices - 1) or devices < 4:
        raise ValueError("unsupported mesh")
    index = lax.axis_index(axis)
    side = index % 2
    half = across // 2
    pairs = [(i, i + 1) for i in range(1, devices - 1, 2)]
    far = lax.ppermute(voxels, axis, pairs + [(j, i) for i, j in pairs])
    near = swap(voxels, axis, 1)
    w_first = conv_first.reshape(3, 9, channels, channels)
    w_second = conv_second.reshape(3, 9, channels, channels)
    padded = (4, across + 2, depth, channels)
    field = jax.ShapeDtypeStruct(voxels.shape, BF)
    flops = 2 * voxels.size * channels * 27
    first = kernel_call(
        functools.partial(first_kernel, axis),
        field,
        [pltpu.VMEM(padded, BF)],
        flops,
        voxels,
        near,
        w_first,
    )
    score = jnp.concatenate([score_x, score_y], axis=1)
    prior_t = prior.reshape(rows, 2, half, depth).swapaxes(2, 3)
    feature, message, keep, strip = kernel_call(
        functools.partial(main_kernel, axis),
        (
            field,
            jax.ShapeDtypeStruct((3 * half + 2, depth, channels), BF),
            jax.ShapeDtypeStruct((3, half, depth, channels), F32),
            jax.ShapeDtypeStruct((2, depth, channels), BF),
        ),
        [pltpu.VMEM(padded, BF), pltpu.VMEM(padded, BF), pltpu.VMEM(voxels.shape, F32)],
        2 * flops,
        first,
        voxels,
        far,
        w_first,
        w_second,
        score,
        prior_t,
    )
    masks = [1 << bit for bit in range(devices.bit_length() - 1)]
    got = swap(message, axis, 1)
    beyond = got[3 * half]
    travel = got[3 * half + 1]
    parts = merge(keep, thirds(got[:-1]))
    neighbour = index ^ (index + 2 * side - 1)
    before = jnp.zeros((depth, channels), BF)
    for mask in masks[1:]:
        if mask != masks[-1]:
            size = parts[0].shape[0] // 2
            upper = (index // mask) % 2
            sent = [lax.dynamic_slice_in_dim(p, (1 - upper) * size, size, 0) for p in parts]
            parts = [lax.dynamic_slice_in_dim(p, upper * size, size, 0) for p in parts]
        else:
            sent = parts
        message = jnp.concatenate([p.astype(BF) for p in sent] + [travel[None]], axis=0)
        got = swap(message, axis, mask)
        travel = got[-1]
        before = jnp.where(neighbour == 2 * mask - 1, travel, before)
        parts = merge(parts, thirds(got))
    pooled = (parts[2] / parts[1]).astype(BF)
    for mask in reversed(masks[:-1]):
        pooled = jnp.concatenate([pooled, swap(pooled, axis, mask)], axis=0)
    strip = jnp.concatenate([before[None], strip, beyond[None]], axis=0)
    return kernel_call(
        functools.partial(last_kernel, axis),
        field,
        [
            pltpu.VMEM((across + 2, depth, channels), BF),
            pltpu.VMEM((rows, depth, channels), F32),
        ],
        flops // 4,
        feature,
        pooled,
        strip,
        plane_yz_w.reshape(3, 3, channels, channels),
        plane_xz_w.reshape(3, 3, channels, channels),
        norm_gain.reshape(1, channels),
        mlp_in,
        mlp_out,
    )


def solution(mesh):
    spread = ("scene", "gx")
    return jax.shard_map(
        functools.partial(on_device, "gx"),
        mesh=mesh,
        in_specs=(P(spread, None, None, None), P(spread, None, None)) + (P(),) * 9,
        out_specs=P(spread, None, None, None),
        check_vma=False,
    )
```

time: 261 us -> 67.2 us (0.26)
  waiting for transfers between devices: 194 us -> 16.7 us
  Pallas kernels: 0 us -> 19.6 us
  matrix products: 15.8 us -> 0 us
  between operations: 13.9 us -> 0.16 us
  local copies, waits for them, and re-layouts: 8.71 us -> 5.03 us
  other arithmetic: 7.42 us -> 4.32 us
    psum x1 -> x0, waiting for transfers between devices: 95.1 us -> none  [on_device(): lax.psum((jnp.sum(weights, axis=0), jnp.sum(weights * feature_f, axis=0))...]
    pmax x1 -> x0, waiting for transfers between devices: 92.3 us -> none  [on_device(): lax.pmax(local_peak.astype(jnp.bfloat16), 'gx').astype(local_peak.dtype)]
    pallas_call x0 -> x3, Pallas kernels: none -> 19.6 us  [kernel_call(): pl.pallas_call(body, out_shape=outs, in_specs=[IN_VMEM] * len(operands),...]
    dot_general x26 -> x0, matrix products: 15.2 us -> none  [the longest x18 10.3 us: volume_conv(): jnp.dot(window, kernel[along_x, along_y], preferred_element_type=jnp.floa...]
    ppermute x6 -> x9, waiting for transfers between devices: 6.47 us -> 16.7 us  [the longest x8 16.7 us: swap(): return lax.ppermute(values, axis, [(i, i ^ mask) for i in range(devices)])]
    slice x12 -> x4, local copies, waits for them, and re-layouts: 6.31 us -> 0.68 us  [the longest x3 0.68 us: on_device(): travel = got[-1]]
    convert_element_type x6 -> x3, other arithmetic: 3.48 us -> 0.11 us  [the longest x1 0.06 us: on_device(): pooled = (parts[2] / parts[1]).astype(BF)]
    ppermute x6 -> x9, starting transfers between devices: 20.1 us -> 20.6 us  [the longest x8 19.9 us: swap(): return lax.ppermute(values, axis, [(i, i ^ mask) for i in range(devices)])]
  transfers between devices with their start and end apart: 8 -> 9, of which waited for: 5 -> 7; matrix products, arithmetic and copies ran while one was open for 1% -> 5% of each run, Pallas kernels for 0% -> 7%
where the time goes in v2:
time: 67.2 us; the launch traced here: 66.5 us
  starting transfers between devices  20.6 us (31%)
  Pallas kernels  19.6 us (29%)
  waiting for transfers between devices  16.7 us (25%)
  local copies, waits for them, and re-layouts  5.03 us (7%)
  other arithmetic  4.32 us (6%)
    ppermute x8, starting transfers between devices, swap(): return lax.ppermute(values, axis, [(i, i ^ mask) for i in range(devices)])  19.9 us
    pallas_call x3, Pallas kernels, kernel_call(): pl.pallas_call(body, out_shape=outs, in_specs=[IN_VMEM] * len(operands),...  19.6 us
    ppermute x8, waiting for transfers between devices, swap(): return lax.ppermute(values, axis, [(i, i ^ mask) for i in range(devices)])  16.7 us
    unnamed x14, local copies, waits for them, and re-layouts  2.89 us
    concatenate x1, other arithmetic, on_device(): score = jnp.concatenate([score_x, score_y], axis=1)  1.39 us
    reshape x2, local copies, waits for them, and re-layouts, on_device(): prior_t = prior.reshape(rows, 2, half, depth).swapaxes(2, 3)  1.38 us
  transfers between devices with their start and end apart: 9, of which 7 were waited for; matrix products, arithmetic and copies ran while one was open for 5% of the time, Pallas kernels for 7%

profile of v2, /device:TPU:0, one launch (start us, length us, event | category | flops | bytes accessed | tf_op | source)
XLA Modules:
  0.0 66.5 jit_solution(8295949951686577834)
XLA Ops:
  0.0 0.5 collective-permute-start
  0.5 0.7 %collective-permute-start.1 = (bf16[2,128,8,128]{3,2,1,0:T(8,128)(2,1)}, bf16[2,128,8,128]{3,2,1,0:T(8,128)(2,1)S(1)}, u32[]{:S(2)}, u32[]{:S(2)}) collective-permute-start(bf16[2,128,8,128]{3,2,1,0:T(8,128)(2,1)} %own_ref.3), channel_id=1, source_target_pairs={{1,2},{3,4},{5,6},{7,8},{9,10},{11,12},{13,14},{2,1},{4,3},{6,5},{... | collective-permute-start | bytes 1572872 | tf_op jit(solution)/shard_map/ppermute | solution.py:289
  1.2 0.8 %reshape.20 = f32[2,2,64,8]{2,1,3,0:T(2,128)S(1)} reshape(f32[2,128,8]{1,2,0:T(8,128)} %param.12) | data formatting | bytes 16384 | tf_op jit(solution)/shard_map/reshape | solution.py:306
  2.0 0.6 copy.14
  2.6 1.4 %pad_maximum_fusion.5.score_ref = bf16[128,256]{1,0:T(8,128)(2,1)} fusion(bf16[128,128]{1,0:T(8,128)(2,1)S(1)} %copy-done.3, bf16[128,128]{1,0:T(8,128)(2,1)} %param.15), kind=kLoop, calls=%fused_computation.30 | loop fusion | flops 131072 | bytes 131072 | tf_op jit(solution)/shard_map/concatenate | solution.py:305
  4.0 0.8 %copy-done.6 = bf16[2,128,8,128]{3,2,1,0:T(8,128)(2,1)} copy-done((bf16[2,128,8,128]{3,2,1,0:T(8,128)(2,1)}, bf16[2,128,8,128]{3,2,1,0:T(8,128)(2,1)S(1)}, u32[]{:S(2)}) %copy-start.6) | copy-done | bytes 524312
  4.8 4.8 %shard_map.109.first_ref = bf16[2,128,8,128]{3,2,1,0:T(8,128)(2,1)} custom-call(bf16[2,128,8,128]{3,2,1,0:T(8,128)(2,1)} %own_ref.3, bf16[2,128,8,128]{3,2,1,0:T(8,128)(2,1)} %copy-done.6, bf16[3,9,128,128]{3,2,1,0:T(8,128)(2,1)} %bitcast.32), custom_call_target="tpu_custom_call" | custom-call | flops 1811939328 | bytes 1933312 | tf_op jit(solution)/shard_map/pallas_call | solution.py:255
  9.5 0.8 %copy-done.5 = bf16[2,128,8,128]{3,2,1,0:T(8,128)(2,1)} copy-done((bf16[2,128,8,128]{3,2,1,0:T(8,128)(2,1)}, bf16[2,128,8,128]{3,2,1,0:T(8,128)(2,1)S(1)}, u32[]{:S(2)}) %copy-start.5) | copy-done | bytes 524312
  10.3 8.9 %shard_map.110 = (bf16[2,128,8,128]{3,2,1,0:T(8,128)(2,1)}, bf16[194,8,128]{2,1,0:T(8,128)(2,1)}, f32[3,64,8,128]{3,2,1,0:T(8,128)}, bf16[2,8,128]{2,1,0:T(8,128)(2,1)}) custom-call(bf16[2,128,8,128]{3,2,1,0:T(8,128)(2,1)} %shard_map.109.first_ref, bf16[2,128,8,128]{3,2,1,0:T(8,128)(2,1)} %own_ref.3, bf16[2,128,8,128]{3,2,1,0:T(8,128)(2,1)} %copy-done.5, ...), custom_call_target="tpu_custom_call" | custom-call | flops 3623878656 | bytes 3416064 | tf_op jit(solution)/shard_map/pallas_call | solution.py:255
  19.2 7.7 %collective-permute-start.2 = (bf16[194,8,128]{2,1,0:T(8,128)(2,1)}, bf16[194,8,128]{2,1,0:T(8,128)(2,1)S(1)}, u32[]{:S(2)}, u32[]{:S(2)}) collective-permute-start(bf16[194,8,128]{2,1,0:T(8,128)(2,1)} %get-tuple-element.11), channel_id=1, source_target_pairs={{0,1},{1,0},{2,3},{3,2},{4,5},{5,4},{6,7},{7,6},{8,9},{9,8},{10,11... | collective-permute-start | bytes 1191944 | tf_op jit(solution)/shard_map/ppermute | solution.py:234
  26.9 1.6 %collective-permute-done.2 = bf16[194,8,128]{2,1,0:T(8,128)(2,1)S(1)} collective-permute-done((bf16[194,8,128]{2,1,0:T(8,128)(2,1)}, bf16[194,8,128]{2,1,0:T(8,128)(2,1)S(1)}, u32[]{:S(2)}, u32[]{:S(2)}) %collective-permute-start.2) | collective-permute-done | bytes 397344 | tf_op jit(solution)/shard_map/ppermute | solution.py:234
  28.4 1.2 %fusion.3 = (f32[64,8,128]{2,1,0:T(8,128)S(1)}, f32[64,8,128]{2,1,0:T(8,128)S(1)}) fusion(f32[3,64,8,128]{3,2,1,0:T(8,128)} %get-tuple-element.10, bf16[194,8,128]{2,1,0:T(8,128)(2,1)S(1)} %collective-permute-done.2), kind=kLoop, calls=%fused_computation.9 | loop fusion | flops 524288 | bytes 1310720 | tf_op jit(solution)/shard_map/add | solution.py:245
  29.7 0.1 fusion.1
  29.9 2.7 %collective-permute-start.3 = (bf16[97,8,128]{2,1,0:T(8,128)(2,1)S(1)}, bf16[97,8,128]{2,1,0:T(8,128)(2,1)S(1)}, u32[]{:S(2)}, u32[]{:S(2)}) collective-permute-start(bf16[97,8,128]{2,1,0:T(8,128)(2,1)S(1)} %pad_maximum_fusion.1), channel_id=1, source_target_pairs={{0,2},{1,3},{2,0},{3,1},{4,6},{5,7},{6,4},{7,5},{8,10},{9,11},{10,... | collective-permute-start | bytes 595976 | tf_op jit(solution)/shard_map/ppermute | solution.py:234
  32.6 5.2 %collective-permute-done.3 = bf16[97,8,128]{2,1,0:T(8,128)(2,1)S(1)} collective-permute-done((bf16[97,8,128]{2,1,0:T(8,128)(2,1)S(1)}, bf16[97,8,128]{2,1,0:T(8,128)(2,1)S(1)}, u32[]{:S(2)}, u32[]{:S(2)}) %collective-permute-start.3) | collective-permute-done | bytes 198688 | tf_op jit(solution)/shard_map/ppermute | solution.py:234
  37.8 0.1 multiply_add_fusion.1
  38.1 2.1 %collective-permute-start.4 = (bf16[49,8,128]{2,1,0:T(8,128)(2,1)S(1)}, bf16[49,8,128]{2,1,0:T(8,128)(2,1)S(1)}, u32[]{:S(2)}, u32[]{:S(2)}) collective-permute-start(bf16[49,8,128]{2,1,0:T(8,128)(2,1)S(1)} %pad_maximum_fusion.3), channel_id=1, source_target_pairs={{0,4},{1,5},{2,6},{3,7},{4,0},{5,1},{6,2},{7,3},{8,12},{9,13},{10,... | collective-permute-start | bytes 301064 | tf_op jit(solution)/shard_map/ppermute | solution.py:234
  40.2 2.6 %collective-permute-done.4 = bf16[49,8,128]{2,1,0:T(8,128)(2,1)S(1)} collective-permute-done((bf16[49,8,128]{2,1,0:T(8,128)(2,1)S(1)}, bf16[49,8,128]{2,1,0:T(8,128)(2,1)S(1)}, u32[]{:S(2)}, u32[]{:S(2)}) %collective-permute-start.4) | collective-permute-done | bytes 100384 | tf_op jit(solution)/shard_map/ppermute | solution.py:234
  42.8 0.6 copy-done.1
  43.5 0.7 %slice-done = bf16[1,8,128]{2,1,0:T(8,128)(2,1)S(1)} async-done(((bf16[49,8,128]{2,1,0:T(8,128)(2,1)}), bf16[1,8,128]{2,1,0:T(8,128)(2,1)S(1)}, s32[]{:S(2)}) %slice-start) | async-done | bytes 2072 | tf_op jit(solution)/shard_map/slice | solution.py:342
  44.1 3.1 %collective-permute-start.5 = (bf16[49,8,128]{2,1,0:T(8,128)(2,1)S(1)}, bf16[49,8,128]{2,1,0:T(8,128)(2,1)S(1)}, u32[]{:S(2)}, u32[]{:S(2)}) collective-permute-start(bf16[49,8,128]{2,1,0:T(8,128)(2,1)S(1)} %pad_maximum_fusion.4), channel_id=1, source_target_pairs={{0,8},{1,9},{2,10},{3,11},{4,12},{5,13},{6,14},{7,15},{8,0},{9,1},... | collective-permute-start | bytes 301064 | tf_op jit(solution)/shard_map/ppermute | solution.py:234
  47.2 2.6 %collective-permute-done.5 = bf16[49,8,128]{2,1,0:T(8,128)(2,1)S(1)} collective-permute-done((bf16[49,8,128]{2,1,0:T(8,128)(2,1)S(1)}, bf16[49,8,128]{2,1,0:T(8,128)(2,1)S(1)}, u32[]{:S(2)}, u32[]{:S(2)}) %collective-permute-start.5) | collective-permute-done | bytes 100384 | tf_op jit(solution)/shard_map/ppermute | solution.py:234
  49.9 2.1 %collective-permute-start.6 = (bf16[16,8,128]{2,1,0:T(8,128)(2,1)S(1)}, bf16[16,8,128]{2,1,0:T(8,128)(2,1)S(1)}, u32[]{:S(2)}, u32[]{:S(2)}) collective-permute-start(bf16[16,8,128]{2,1,0:T(8,128)(2,1)S(1)} %divide_convert_fusion), channel_id=1, source_target_pairs={{0,4},{1,5},{2,6},{3,7},{4,0},{5,1},{6,2},{7,3},{8,12},{9,13},{10,... | collective-permute-start | bytes 98312 | tf_op jit(solution)/shard_map/ppermute | solution.py:234
  52.1 1.9 %collective-permute-done.6 = bf16[16,8,128]{2,1,0:T(8,128)(2,1)S(1)} collective-permute-done((bf16[16,8,128]{2,1,0:T(8,128)(2,1)S(1)}, bf16[16,8,128]{2,1,0:T(8,128)(2,1)S(1)}, u32[]{:S(2)}, u32[]{:S(2)}) %collective-permute-start.6) | collective-permute-done | bytes 32800 | tf_op jit(solution)/shard_map/ppermute | solution.py:234
  54.0 1.7 %collective-permute-start.7 = (bf16[32,8,128]{2,1,0:T(8,128)(2,1)S(1)}, bf16[32,8,128]{2,1,0:T(8,128)(2,1)S(1)}, u32[]{:S(2)}, u32[]{:S(2)}) collective-permute-start(bf16[32,8,128]{2,1,0:T(8,128)(2,1)S(1)} %pad_maximum_fusion.6), channel_id=1, source_target_pairs={{0,2},{1,3},{2,0},{3,1},{4,6},{5,7},{6,4},{7,5},{8,10},{9,11},{10,... | collective-permute-start | bytes 196616 | tf_op jit(solution)/shard_map/ppermute | solution.py:234
  55.6 2.7 %collective-permute-done.7 = bf16[32,8,128]{2,1,0:T(8,128)(2,1)S(1)} collective-permute-done((bf16[32,8,128]{2,1,0:T(8,128)(2,1)S(1)}, bf16[32,8,128]{2,1,0:T(8,128)(2,1)S(1)}, u32[]{:S(2)}, u32[]{:S(2)}) %collective-permute-start.7) | collective-permute-done | bytes 65568 | tf_op jit(solution)/shard_map/ppermute | solution.py:234
  58.3 0.1 collective-permute-start.8
  58.4 0.7 copy-done.4
  59.1 0.6 pad_maximum_fusion.7.strip_ref
  59.7 0.1 collective-permute-done.8
  59.7 0.7 %pad_maximum_fusion.pooled_ref = bf16[128,8,128]{2,1,0:T(8,128)(2,1)} fusion(bf16[64,8,128]{2,1,0:T(8,128)(2,1)S(1)} %collective-permute-done.8, bf16[32,8,128]{2,1,0:T(8,128)(2,1)S(1)} %collective-permute-done.7, bf16[16,8,128]{2,1,0:T(8,128)(2,1)S(1)} %collective-permute-done.6, bf16[16,8,128]{2,1,0:T(8,128)(2,1)S(1)} %divide_convert_fusion), kind=kLoop, calls=%fused_computation.3 | loop fusion | flops 393216 | bytes 524288 | tf_op jit(solution)/shard_map/concatenate | solution.py:347
  60.5 6.0 %shard_map.111 = bf16[2,128,8,128]{3,2,1,0:T(8,128)(2,1)} custom-call(bf16[2,128,8,128]{3,2,1,0:T(8,128)(2,1)} %get-tuple-element.9.feature_ref, bf16[128,8,128]{2,1,0:T(8,128)(2,1)} %pad_maximum_fusion.pooled_ref, bf16[4,8,128]{2,1,0:T(8,128)(2,1)} %pad_maximum_fusion.7.strip_ref, bf16[3,3,128,128]{3,2,1,0:T(8,128)(2,1)} %bitcast.28, ...), custom_call_target="tpu_custom_call" | custom-call | flops 452984832 | bytes 1647104 | tf_op jit(solution)/shard_map/pallas_call | solution.py:255
  (30 shorter events, 0.4 us)
Async XLA Ops:
  0.0 2.6 %copy-start.3 = (bf16[128,128]{1,0:T(8,128)(2,1)S(1)}, bf16[128,128]{1,0:T(8,128)(2,1)}, u32[]{:S(2)}) copy-start(bf16[128,128]{1,0:T(8,128)(2,1)} %param.16) | copy-start | bytes 98308
  0.0 4.0 %collective-permute-start = (bf16[2,128,8,128]{3,2,1,0:T(8,128)(2,1)}, bf16[2,128,8,128]{3,2,1,0:T(8,128)(2,1)S(1)}, u32[]{:S(2)}, u32[]{:S(2)}) collective-permute-start(bf16[2,128,8,128]{3,2,1,0:T(8,128)(2,1)} %own_ref.3), channel_id=1, source_target_pairs={{0,1},{1,0},{2,3},{3,2},{4,5},{5,4},{6,7},{7,6},{8,9},{9,8},{10,11... | collective-permute-start | bytes 1572872 | tf_op jit(solution)/shard_map/ppermute | solution.py:234
  0.5 9.0 %collective-permute-start.1 = (bf16[2,128,8,128]{3,2,1,0:T(8,128)(2,1)}, bf16[2,128,8,128]{3,2,1,0:T(8,128)(2,1)S(1)}, u32[]{:S(2)}, u32[]{:S(2)}) collective-permute-start(bf16[2,128,8,128]{3,2,1,0:T(8,128)(2,1)} %own_ref.3), channel_id=1, source_target_pairs={{1,2},{3,4},{5,6},{7,8},{9,10},{11,12},{13,14},{2,1},{4,3},{6,5},{... | collective-permute-start | bytes 1572872 | tf_op jit(solution)/shard_map/ppermute | solution.py:289
  4.0 0.8 %copy-start.6 = (bf16[2,128,8,128]{3,2,1,0:T(8,128)(2,1)}, bf16[2,128,8,128]{3,2,1,0:T(8,128)(2,1)S(1)}, u32[]{:S(2)}) copy-start(bf16[2,128,8,128]{3,2,1,0:T(8,128)(2,1)S(1)} %collective-permute-done.near_ref) | copy-start | bytes 1572868
  9.5 0.8 %copy-start.5 = (bf16[2,128,8,128]{3,2,1,0:T(8,128)(2,1)}, bf16[2,128,8,128]{3,2,1,0:T(8,128)(2,1)S(1)}, u32[]{:S(2)}) copy-start(bf16[2,128,8,128]{3,2,1,0:T(8,128)(2,1)S(1)} %collective-permute-done.1.far_ref) | copy-start | bytes 1572868
  19.2 9.3 %collective-permute-start.2 = (bf16[194,8,128]{2,1,0:T(8,128)(2,1)}, bf16[194,8,128]{2,1,0:T(8,128)(2,1)S(1)}, u32[]{:S(2)}, u32[]{:S(2)}) collective-permute-start(bf16[194,8,128]{2,1,0:T(8,128)(2,1)} %get-tuple-element.11), channel_id=1, source_target_pairs={{0,1},{1,0},{2,3},{3,2},{4,5},{5,4},{6,7},{7,6},{8,9},{9,8},{10,11... | collective-permute-start | bytes 1191944 | tf_op jit(solution)/shard_map/ppermute | solution.py:234
  28.4 1.3 %copy-start = (f32[3,64,8,128]{3,2,1,0:T(8,128)S(1)}, f32[3,64,8,128]{3,2,1,0:T(8,128)}, u32[]{:S(2)}) copy-start(f32[3,64,8,128]{3,2,1,0:T(8,128)} %get-tuple-element.10) | copy-start | bytes 2359300
  29.9 7.9 %collective-permute-start.3 = (bf16[97,8,128]{2,1,0:T(8,128)(2,1)S(1)}, bf16[97,8,128]{2,1,0:T(8,128)(2,1)S(1)}, u32[]{:S(2)}, u32[]{:S(2)}) collective-permute-start(bf16[97,8,128]{2,1,0:T(8,128)(2,1)S(1)} %pad_maximum_fusion.1), channel_id=1, source_target_pairs={{0,2},{1,3},{2,0},{3,1},{4,6},{5,7},{6,4},{7,5},{8,10},{9,11},{10,... | collective-permute-start | bytes 595976 | tf_op jit(solution)/shard_map/ppermute | solution.py:234
  38.1 4.7 %collective-permute-start.4 = (bf16[49,8,128]{2,1,0:T(8,128)(2,1)S(1)}, bf16[49,8,128]{2,1,0:T(8,128)(2,1)S(1)}, u32[]{:S(2)}, u32[]{:S(2)}) collective-permute-start(bf16[49,8,128]{2,1,0:T(8,128)(2,1)S(1)} %pad_maximum_fusion.3), channel_id=1, source_target_pairs={{0,4},{1,5},{2,6},{3,7},{4,0},{5,1},{6,2},{7,3},{8,12},{9,13},{10,... | collective-permute-start | bytes 301064 | tf_op jit(solution)/shard_map/ppermute | solution.py:234
  42.8 0.6 copy-start.1
  43.4 0.7 %slice-start = ((bf16[49,8,128]{2,1,0:T(8,128)(2,1)}), bf16[1,8,128]{2,1,0:T(8,128)(2,1)S(1)}, s32[]{:S(2)}) async-start(bf16[49,8,128]{2,1,0:T(8,128)(2,1)} %copy-done.1), calls=%async_computation | async-start | bytes 4096 | tf_op jit(solution)/shard_map/slice | solution.py:342
  44.1 5.7 %copy-start.2 = (bf16[49,8,128]{2,1,0:T(8,128)(2,1)S(1)}, bf16[49,8,128]{2,1,0:T(8,128)(2,1)}, u32[]{:S(2)}) copy-start(bf16[49,8,128]{2,1,0:T(8,128)(2,1)} %copy-done.1) | copy-start | bytes 301060
  44.1 5.7 %collective-permute-start.5 = (bf16[49,8,128]{2,1,0:T(8,128)(2,1)S(1)}, bf16[49,8,128]{2,1,0:T(8,128)(2,1)S(1)}, u32[]{:S(2)}, u32[]{:S(2)}) collective-permute-start(bf16[49,8,128]{2,1,0:T(8,128)(2,1)S(1)} %pad_maximum_fusion.4), channel_id=1, source_target_pairs={{0,8},{1,9},{2,10},{3,11},{4,12},{5,13},{6,14},{7,15},{8,0},{9,1},... | collective-permute-start | bytes 301064 | tf_op jit(solution)/shard_map/ppermute | solution.py:234
  49.9 4.0 %collective-permute-start.6 = (bf16[16,8,128]{2,1,0:T(8,128)(2,1)S(1)}, bf16[16,8,128]{2,1,0:T(8,128)(2,1)S(1)}, u32[]{:S(2)}, u32[]{:S(2)}) collective-permute-start(bf16[16,8,128]{2,1,0:T(8,128)(2,1)S(1)} %divide_convert_fusion), channel_id=1, source_target_pairs={{0,4},{1,5},{2,6},{3,7},{4,0},{5,1},{6,2},{7,3},{8,12},{9,13},{10,... | collective-permute-start | bytes 98312 | tf_op jit(solution)/shard_map/ppermute | solution.py:234
  54.0 4.3 %collective-permute-start.7 = (bf16[32,8,128]{2,1,0:T(8,128)(2,1)S(1)}, bf16[32,8,128]{2,1,0:T(8,128)(2,1)S(1)}, u32[]{:S(2)}, u32[]{:S(2)}) collective-permute-start(bf16[32,8,128]{2,1,0:T(8,128)(2,1)S(1)} %pad_maximum_fusion.6), channel_id=1, source_target_pairs={{0,2},{1,3},{2,0},{3,1},{4,6},{5,7},{6,4},{7,5},{8,10},{9,11},{10,... | collective-permute-start | bytes 196616 | tf_op jit(solution)/shard_map/ppermute | solution.py:234
  58.3 1.4 %collective-permute-start.8 = (bf16[64,8,128]{2,1,0:T(8,128)(2,1)S(1)}, bf16[64,8,128]{2,1,0:T(8,128)(2,1)S(1)}, u32[]{:S(2)}, u32[]{:S(2)}) collective-permute-start(bf16[64,8,128]{2,1,0:T(8,128)(2,1)S(1)} %pad_maximum_fusion.2), channel_id=1, source_target_pairs={{0,1},{1,0},{2,3},{3,2},{4,5},{5,4},{6,7},{7,6},{8,9},{9,8},{10,11... | collective-permute-start | bytes 393224 | tf_op jit(solution)/shard_map/ppermute | solution.py:234
  58.4 0.7 %copy-start.4 = (bf16[2,8,128]{2,1,0:T(8,128)(2,1)S(1)}, bf16[2,8,128]{2,1,0:T(8,128)(2,1)}, u32[]{:S(2)}) copy-start(bf16[2,8,128]{2,1,0:T(8,128)(2,1)} %get-tuple-element.12) | copy-start | bytes 12292

commit v3 on v2

v3 whole, which is shorter than its diff:
```python
import functools

import jax
import jax.numpy as jnp
from jax import lax
from jax.experimental import pallas as pl
from jax.experimental.pallas import tpu as pltpu
from jax.sharding import PartitionSpec as P

BF = jnp.bfloat16
F32 = jnp.float32
IN_VMEM = pl.BlockSpec(memory_space=pltpu.VMEM)
PAIR = ({0: 0, 1: 1, 2: 2}, {1: 0, 2: 1, 3: 2})
LOWER = ({0: 0, 1: 1}, {1: 0})
UPPER = ({2: 2}, {2: 1, 3: 2})


def activate(values):
    return 0.5 * values * (1.0 + jnp.tanh(0.7978845608028654 * (values + 0.044715 * values**3)))


def beside(blocks):
    return jnp.concatenate(blocks, axis=1)


def shift_depth(before, same, after, shape):
    depth = shape[1]
    place = lax.broadcasted_iota(jnp.int32, shape, 1)
    before = jnp.where(place == 0, 0.0, pltpu.roll(before.reshape(shape), 1, 1))
    after = jnp.where(place == depth - 1, 0.0, pltpu.roll(after.reshape(shape), depth - 1, 1))
    return before + same.reshape(shape) + after


def conv_rows(rows_ref, w_ref, taps, start, span, uses, names=None):
    depth, channels = rows_ref.shape[2:]
    shape = (span, depth, channels)
    zero = jnp.zeros((channels, channels), BF)
    windows = {
        r: [
            rows_ref[names[r] if names else r, pl.ds(start + b, span)].reshape(-1, channels)
            for b in range(3)
        ]
        for r in sorted(set(uses[0]) | set(uses[1]))
    }

    def weight(out, row, b, c):
        return w_ref[taps[uses[out][row]], 3 * b + c] if row in uses[out] else zero

    def product(left, right):
        rows = sorted(set(uses[left[0]]) | set(uses[right[0]]))
        lhs = beside([windows[r][b] for r in rows for b in range(3)])
        rhs = jnp.concatenate(
            [
                beside([weight(left[0], r, b, left[1]), weight(right[0], r, b, right[1])])
                for r in rows
                for b in range(3)
            ],
            axis=0,
        )
        total = jnp.dot(lhs, rhs, preferred_element_type=F32)
        return total[:, :channels], total[:, channels:]

    low0, low1 = product((0, 0), (0, 1))
    low2, high0 = product((0, 2), (1, 0))
    high1, high2 = product((1, 1), (1, 2))
    return shift_depth(low0, low1, low2, shape), shift_depth(high0, high1, high2, shape)


def clear_ends(rows_ref, width):
    rows, length, depth, channels = rows_ref.shape
    blank = jnp.zeros((width, depth, channels), rows_ref.dtype)
    for row in range(rows):
        rows_ref[row, :width] = blank
        rows_ref[row, length - width :] = blank


def first_kernel(axis, own_ref, near_ref, w1_ref, w2_ref, edge_ref, part_ref, rows_ref, mid_ref):
    across = own_ref.shape[1]
    side = lax.rem(lax.axis_index(axis), 2)
    clear_ends(rows_ref, 1)
    clear_ends(mid_ref, 1)
    clear_ends(edge_ref, 1)
    for row, (source, at) in enumerate(
        ((own_ref, side), (own_ref, 1 - side), (near_ref, side), (near_ref, 1 - side))
    ):
        rows_ref[row, 1 : across + 1] = source[at]
    taps = (2 * side, 1, 2 - 2 * side)
    back = (2 - 2 * side, 1, 2 * side)
    span = across // 2
    for step in range(2):
        start = step * span
        low, high = conv_rows(rows_ref, w1_ref, taps, start, span, PAIR)
        mid_ref[0, 1 + start : 1 + start + span] = activate(low).astype(BF)
        mid_ref[1, 1 + start : 1 + start + span] = activate(high).astype(BF)
        low, high = conv_rows(rows_ref, w1_ref, back, start, span, LOWER, {0: 1, 1: 0})
        edge_ref[0, 1 + start : 1 + start + span] = low
        edge_ref[1, 1 + start : 1 + start + span] = high
    for step in range(2):
        start = step * span
        low, high = conv_rows(mid_ref, w2_ref, taps, start, span, UPPER, {2: 0, 3: 1})
        for u, part in enumerate((low, high)):
            own = rows_ref[u, 1 + start : 1 + start + span].astype(F32)
            part_ref[u, start : start + span] = part + own


def half_kernel(axis, second, *refs):
    edge_ref, part_ref, far_ref, w1_ref, w2_ref, x_ref, y_ref, prior_ref = refs[:8]
    if second:
        state_ref, feature_ref, message_ref, keep_ref, strip_ref, rows_ref, mid_ref = refs[8:]
    else:
        feature_ref, message_ref, keep_ref, state_ref, rows_ref, mid_ref = refs[8:]
    across, depth, channels = far_ref.shape[1:]
    devices = lax.axis_size(axis)
    index = lax.axis_index(axis)
    side = lax.rem(index, 2)
    span = across // 2
    kept = lax.rem(index // 2, 2)
    half = kept if second else 1 - kept
    clear_ends(rows_ref, 2)
    inner = pl.ds(half * (span - 2), span + 2)
    local = pl.ds(2 - 2 * half, span + 2)
    rows_ref[0, local] = far_ref[1 - side, inner]
    rows_ref[1, local] = far_ref[side, inner]
    back = (2 - 2 * side, 1, 2 * side)
    low, high = conv_rows(rows_ref, w1_ref, back, 0, span + 2, UPPER, {2: 0, 3: 1})
    inside = jnp.where(jnp.logical_or(index == 0, index == devices - 1), 0.0, 1.0)
    around = pl.ds(half * span, span + 2)
    mid_ref[1] = activate(low + edge_ref[0, around]).astype(BF)
    mid_ref[0] = (activate(high + edge_ref[1, around]) * inside).astype(BF)
    blank = jnp.zeros((depth, channels), BF)
    mid_ref[0, half * (span + 1)] = blank
    mid_ref[1, half * (span + 1)] = blank
    outs = conv_rows(mid_ref, w2_ref, (2 * side, 1, 2 - 2 * side), 0, span, LOWER)
    place = pl.ds(half * span, span)
    score = beside([x_ref[...], y_ref[...]])
    logits, features = [], []
    for u in range(2):
        at = side if u == 0 else 1 - side
        feature = (outs[u] + part_ref[u, place]).astype(BF)
        feature_ref[at] = feature
        both = jnp.dot(feature.reshape(-1, channels), score, preferred_element_type=F32)
        columns = prior_ref[at, half]
        prior = jnp.stack(
            [jnp.broadcast_to(columns[:, y : y + 1], (depth, channels)) for y in range(span)]
        )
        feature = feature.astype(F32)
        features.append(feature)
        logits.append(both[:, :channels].reshape(span, depth, channels) + prior)
        logit_y = both[:, channels:].reshape(span, depth, channels) + prior
        top = jnp.max(logit_y, axis=0)
        if second:
            top = jnp.maximum(top, state_ref[u, 0])
        weights = jnp.exp(logit_y - top)
        norm_sum = jnp.sum(weights, axis=0)
        weighted = jnp.sum(weights * feature, axis=0)
        if second:
            scale = jnp.exp(state_ref[u, 0] - top)
            norm_sum = norm_sum + state_ref[u, 1] * scale
            weighted = weighted + state_ref[u, 2] * scale
            pooled = (weighted / norm_sum).astype(BF)
            strip_ref[u] = pooled
            message_ref[3 * (span // 2) + 1 - u] = pooled
        else:
            state_ref[u, 0] = top
            state_ref[u, 1] = norm_sum
            state_ref[u, 2] = weighted
    peak = jnp.maximum(logits[0], logits[1])
    coarse = peak.astype(BF)
    shift = jnp.exp(jnp.clip(peak - coarse.astype(F32), -60.0, 60.0))
    low, high = jnp.exp(logits[0] - peak) * shift, jnp.exp(logits[1] - peak) * shift
    parts = (coarse.astype(F32), low + high, low * features[0] + high * features[1])
    quarter = span // 2
    for piece in range(2):
        cut = slice(piece * quarter, (piece + 1) * quarter)

        @pl.when(side == piece)
        def _():
            for k, part in enumerate(parts):
                keep_ref[k] = part[cut]

        @pl.when(side != piece)
        def _():
            for k, part in enumerate(parts):
                message_ref[k * quarter : (k + 1) * quarter] = part[cut].astype(BF)


def last_kernel(
    axis,
    early_ref,
    late_ref,
    pooled_ref,
    strip_ref,
    yz_ref,
    xz_ref,
    gain_ref,
    in_ref,
    out_w_ref,
    out_ref,
    plane_ref,
    mix_ref,
):
    rows, half, depth, channels = early_ref.shape
    across = 2 * half
    index = lax.axis_index(axis)
    side = lax.rem(index, 2)
    kept = lax.rem(index // 2, 2)
    bits = lax.axis_size(axis).bit_length() - 2
    block = across >> bits
    order = [1, 0] + list(range(2, bits))
    mine = 0
    for bit in order:
        mine = mine * 2 + lax.rem(index // (1 << bit), 2)
    blank = jnp.zeros((depth, channels), BF)
    plane_ref[0] = blank
    plane_ref[across + 1] = blank
    for k in range(1 << bits):
        other = 0
        for bit in order:
            other = other * 2 + (k >> (bits - 1 - bit)) % 2
        place = jnp.bitwise_xor(mine, other)
        plane_ref[pl.ds(1 + place * block, block)] = pooled_ref[k * block : (k + 1) * block]

    def plane_product(windows, weights, shape):
        lhs = beside(windows)
        rhs = jnp.concatenate([beside(w) for w in weights], axis=0)
        total = jnp.dot(lhs, rhs, preferred_element_type=F32)
        parts = [total[:, c * channels : (c + 1) * channels] for c in range(3)]
        return shift_depth(*parts, shape).astype(BF).astype(F32)

    taps = (2 * side, 1, 2 - 2 * side)
    strip = strip_ref[...]
    mixed = plane_product(
        [strip[a : a + rows].reshape(-1, channels) for a in range(3)],
        [[xz_ref[taps[a], c] for c in range(3)] for a in range(3)],
        (rows, depth, channels),
    )
    mix_ref[side] = mixed[0]
    mix_ref[1 - side] = mixed[1]
    gain = gain_ref[...]
    span = min(32, half)
    for step in range(across // span):
        early = step * span < half
        feature_ref = early_ref if early else late_ref
        at = step * span % half
        start = (1 - kept if early else kept) * half + at
        plane = plane_product(
            [plane_ref[pl.ds(start + b, span)].reshape(-1, channels) for b in range(3)],
            [[yz_ref[b, c] for c in range(3)] for b in range(3)],
            (span, depth, channels),
        )
        for row in range(rows):
            feature = feature_ref[row, at : at + span].astype(F32)
            joined = (feature * (plane + mix_ref[row])).reshape(-1, channels)
            mean = jnp.mean(joined * joined, axis=-1, keepdims=True)
            normed = (joined * lax.rsqrt(mean + 1e-06) * gain).astype(BF)
            hidden = activate(jnp.dot(normed, in_ref[...], preferred_element_type=F32)).astype(BF)
            update = jnp.dot(hidden, out_w_ref[...], preferred_element_type=F32)
            out_ref[row, pl.ds(start, span)] = (
                (joined + update).astype(BF).reshape(span, depth, channels)
            )


def swap(values, axis, mask):
    devices = lax.axis_size(axis)
    return lax.ppermute(values, axis, [(i, i ^ mask) for i in range(devices)])


def merge(own, other):
    peak, other_peak = own[0], other[0].astype(F32)
    top = jnp.maximum(peak, other_peak)
    scale = jnp.exp(peak - top)
    other_scale = jnp.exp(other_peak - top)
    return [
        top,
        own[1] * scale + other[1].astype(F32) * other_scale,
        own[2] * scale + other[2].astype(F32) * other_scale,
    ]


def thirds(message):
    size = message.shape[0] // 3
    return [message[k * size : (k + 1) * size] for k in range(3)]


def kernel_call(body, outs, scratch, flops, *operands):
    moved = sum(o.size * o.dtype.itemsize for o in operands)
    return pl.pallas_call(
        body,
        out_shape=outs,
        in_specs=[IN_VMEM] * len(operands),
        out_specs=jax.tree.map(lambda _: IN_VMEM, outs),
        scratch_shapes=scratch,
        compiler_params=pltpu.CompilerParams(vmem_limit_bytes=12 * 1024 * 1024),
        cost_estimate=pl.CostEstimate(flops=flops, bytes_accessed=moved, transcendentals=0),
    )(*operands)


def on_device(
    axis,
    voxels,
    prior,
    conv_first,
    conv_second,
    score_x,
    score_y,
    plane_yz_w,
    plane_xz_w,
    norm_gain,
    mlp_in,
    mlp_out,
):
    rows, across, depth, channels = voxels.shape
    devices = lax.axis_size(axis)
    if rows != 2 or devices & (devices - 1) or devices < 8:
        raise ValueError("unsupported mesh")
    index = lax.axis_index(axis)
    half, quarter = across // 2, across // 4
    w_first = conv_first.reshape(3, 9, channels, channels)
    w_second = conv_second.reshape(3, 9, channels, channels)
    flops = 2 * voxels.size * channels * 27

    def beyond_edge(at):
        return at + 2 * (at % 2) - 1

    pairs = [(i, i + 1) for i in range(1, devices - 1, 2)]
    far = lax.ppermute(voxels, axis, pairs + [(j, i) for i, j in pairs])
    near = swap(voxels, axis, 1)
    edge, part = kernel_call(
        functools.partial(first_kernel, axis),
        (
            jax.ShapeDtypeStruct((rows, across + 2, depth, channels), F32),
            jax.ShapeDtypeStruct(voxels.shape, F32),
        ),
        [
            pltpu.VMEM((4, across + 2, depth, channels), BF),
            pltpu.VMEM((2, across + 2, depth, channels), BF),
        ],
        2 * flops,
        voxels,
        near,
        w_first,
        w_second,
    )
    prior = prior.reshape(rows, 2, half, depth).swapaxes(2, 3)

    def half_call(second, *state):
        feature = jax.ShapeDtypeStruct((rows, half, depth, channels), BF)
        message = jax.ShapeDtypeStruct((3 * quarter + 2 * second, depth, channels), BF)
        keep = jax.ShapeDtypeStruct((3, quarter, depth, channels), F32)
        last = (
            jax.ShapeDtypeStruct((rows, depth, channels), BF)
            if second
            else jax.ShapeDtypeStruct((rows, 3, depth, channels), F32)
        )
        return kernel_call(
            functools.partial(half_kernel, axis, second),
            (feature, message, keep, last),
            [
                pltpu.VMEM((2, half + 4, depth, channels), BF),
                pltpu.VMEM((2, half + 2, depth, channels), BF),
            ],
            3 * flops // 4,
            edge,
            part,
            far,
            w_first,
            w_second,
            score_x,
            score_y,
            prior,
            *state,
        )

    masks = [1 << bit for bit in range(devices.bit_length() - 1)]
    early, message, keep, state = half_call(False)
    got = swap(message, axis, masks[0])
    sent = jnp.concatenate([p.astype(BF) for p in merge(keep, thirds(got))])
    sent, state = lax.optimization_barrier((sent, state))
    arriving = swap(sent, axis, masks[1])
    late, message, keep, strip = half_call(True, state)
    got = swap(message, axis, masks[0])
    beyond = got[3 * quarter]
    carried = [got[3 * quarter + 1]]
    parts = merge(merge(keep, thirds(got[: 3 * quarter])), thirds(arriving))
    for mask in masks[2:]:
        if mask != masks[-1]:
            size = parts[0].shape[0] // 2
            upper = (index // mask) % 2
            sent = [lax.dynamic_slice_in_dim(p, (1 - upper) * size, size, 0) for p in parts]
            parts = [lax.dynamic_slice_in_dim(p, upper * size, size, 0) for p in parts]
        else:
            sent = parts
        message = jnp.concatenate([p.astype(BF) for p in sent] + [carried[-1][None]], axis=0)
        got = swap(message, axis, mask)
        carried.append(got[-1])
        last_row = carried[-1]
        parts = merge(parts, thirds(got[:-1]))
        parts[0], carried[-1] = lax.optimization_barrier((parts[0], last_row))
    pooled = (parts[2] / parts[1]).astype(BF)
    for mask in reversed(masks[2:-1]):
        pooled = jnp.concatenate([pooled, swap(pooled, axis, mask)], axis=0)
    other = index ^ masks[1]
    path = other ^ beyond_edge(other)
    row = carried[0]
    for k, value in enumerate(carried[1:]):
        row = jnp.where(path == (1 << (k + 3)) - 1, value, row)
    got = swap(jnp.concatenate([pooled, row[None]], axis=0), axis, masks[1])
    before = jnp.where((index == 0) | (index == devices - 1), jnp.zeros_like(row), got[-1])
    pooled = jnp.concatenate([pooled, got[:-1]], axis=0)
    pooled = jnp.concatenate([pooled, swap(pooled, axis, masks[0])], axis=0)
    strip = jnp.concatenate([before[None], strip, beyond[None]], axis=0)
    return kernel_call(
        functools.partial(last_kernel, axis),
        jax.ShapeDtypeStruct(voxels.shape, BF),
        [
            pltpu.VMEM((across + 2, depth, channels), BF),
            pltpu.VMEM((rows, depth, channels), F32),
        ],
        flops // 4,
        early,
        late,
        pooled,
        strip,
        plane_yz_w.reshape(3, 3, channels, channels),
        plane_xz_w.reshape(3, 3, channels, channels),
        norm_gain.reshape(1, channels),
        mlp_in,
        mlp_out,
    )


def solution(mesh):
    spread = ("scene", "gx")
    return jax.shard_map(
        functools.partial(on_device, "gx"),
        mesh=mesh,
        in_specs=(P(spread, None, None, None), P(spread, None, None)) + (P(),) * 9,
        out_specs=P(spread, None, None, None),
        check_vma=False,
    )
```

time: 67.2 us -> 56.9 us (0.85)
  Pallas kernels: 19.6 us -> 13.7 us
  other arithmetic: 4.32 us -> 0.51 us
  waiting for transfers between devices: 16.7 us -> 17.8 us
  local copies, waits for them, and re-layouts: 5.03 us -> 4.25 us
  starting transfers between devices: 20.6 us -> 19.9 us
    pallas_call x3 -> x4, Pallas kernels: 19.6 us -> 13.7 us  [kernel_call(): pl.pallas_call(body, out_shape=outs, in_specs=[IN_VMEM] * len(operands),...]
    concatenate x7 -> x6, other arithmetic: 2.18 us -> 0.1 us  [the longest x1 0.03 us: on_device(): pooled = jnp.concatenate([pooled, swap(pooled, axis, masks[0])], axis=0)]
    add x4 -> x0, other arithmetic: 1.44 us -> none  [the longest x2 1.27 us: merge(): own[2] * scale + other[2].astype(F32) * other_scale]
    ppermute x8 -> x9, waiting for transfers between devices: 16.7 us -> 17.8 us  [swap(): return lax.ppermute(values, axis, [(i, i ^ mask) for i in range(devices)])]
    slice x4 -> x2, local copies, waits for them, and re-layouts: 0.68 us -> 0.01 us  [the longest x1 0.01 us: on_device(): pooled = jnp.concatenate([pooled, got[:-1]], axis=0)]
    ppermute x8 -> x9, starting transfers between devices: 19.9 us -> 19.3 us  [swap(): return lax.ppermute(values, axis, [(i, i ^ mask) for i in range(devices)])]
    unnamed x14 -> x24, local copies, waits for them, and re-layouts: 2.89 us -> 3.42 us
  transfers between devices with their start and end apart: 9 -> 10, of which waited for: 7 -> 8; matrix products, arithmetic and copies ran while one was open for 5% -> 1% of each run, Pallas kernels for 7% -> 8%
where the time goes in v3:
time: 56.9 us; the launch traced here: 56.5 us
  starting transfers between devices  19.9 us (35%)
  waiting for transfers between devices  17.8 us (31%)
  Pallas kernels  13.7 us (24%)
  local copies, waits for them, and re-layouts  4.25 us (7%)
    ppermute x9, starting transfers between devices, swap(): return lax.ppermute(values, axis, [(i, i ^ mask) for i in range(devices)])  19.3 us
    ppermute x9, waiting for transfers between devices, swap(): return lax.ppermute(values, axis, [(i, i ^ mask) for i in range(devices)])  17.8 us
    pallas_call x4, Pallas kernels, kernel_call(): pl.pallas_call(body, out_shape=outs, in_specs=[IN_VMEM] * len(operands),...  13.7 us
    unnamed x24, local copies, waits for them, and re-layouts  3.42 us
  transfers between devices with their start and end apart: 10, of which 8 were waited for; matrix products, arithmetic and copies ran while one was open for 1% of the time, Pallas kernels for 8%

profile of v3, /device:TPU:0, one launch (start us, length us, event | category | flops | bytes accessed | tf_op | source)
XLA Modules:
  0.0 56.5 jit_solution(13979279263555456999)
XLA Ops:
  0.0 0.5 collective-permute-start
  0.5 0.7 %collective-permute-start.1 = (bf16[2,128,8,128]{3,2,1,0:T(8,128)(2,1)}, bf16[2,128,8,128]{3,2,1,0:T(8,128)(2,1)S(1)}, u32[]{:S(2)}, u32[]{:S(2)}) collective-permute-start(bf16[2,128,8,128]{3,2,1,0:T(8,128)(2,1)} %own_ref.1), channel_id=1, source_target_pairs={{1,2},{3,4},{5,6},{7,8},{9,10},{11,12},{13,14},{2,1},{4,3},{6,5},{... | collective-permute-start | bytes 1572872 | tf_op jit(solution)/shard_map/ppermute | solution.py:326
  1.2 0.8 %reshape.20 = f32[2,2,64,8]{2,1,3,0:T(2,128)S(1)} reshape(f32[2,128,8]{1,2,0:T(8,128)} %param.12) | data formatting | bytes 16384 | tf_op jit(solution)/shard_map/reshape | solution.py:344
  2.0 0.3 collective-permute-done.near_ref
  2.2 1.2 %copy-done.5 = bf16[27,128,128]{2,1,0:T(8,128)(2,1)S(1)} copy-done((bf16[27,128,128]{2,1,0:T(8,128)(2,1)S(1)}, bf16[27,128,128]{2,1,0:T(8,128)(2,1)}, u32[]{:S(2)}) %copy-start.5) | copy-done | bytes 884760
  3.4 1.2 %copy-done.7 = bf16[27,128,128]{2,1,0:T(8,128)(2,1)S(1)} copy-done((bf16[27,128,128]{2,1,0:T(8,128)(2,1)S(1)}, bf16[27,128,128]{2,1,0:T(8,128)(2,1)}, u32[]{:S(2)}) %copy-start.7) | copy-done | bytes 884760
  4.6 1.0 %copy-done.9 = bf16[2,128,8,128]{3,2,1,0:T(8,128)(2,1)S(1)} copy-done((bf16[2,128,8,128]{3,2,1,0:T(8,128)(2,1)S(1)}, bf16[2,128,8,128]{3,2,1,0:T(8,128)(2,1)}, u32[]{:S(2)}) %copy-start.9) | copy-done | bytes 524312
  5.6 4.5 %shard_map.109 = (f32[2,130,8,128]{3,2,1,0:T(8,128)S(1)}, f32[2,128,8,128]{3,2,1,0:T(8,128)S(1)}) custom-call(bf16[2,128,8,128]{3,2,1,0:T(8,128)(2,1)S(1)} %copy-done.9, bf16[2,128,8,128]{3,2,1,0:T(8,128)(2,1)S(1)} %collective-permute-done.near_ref, bf16[3,9,128,128]{3,2,1,0:T(8,128)(2,1)S(1)} %bitcast.85, bf16[3,9,128,128]{3,2,1,0:T(8,128)(2,1)S(1)} %bitcast.88), custom_call_target="tpu_custom_call" | custom-call | flops 3623878656 | bytes 2818048 | tf_op jit(solution)/shard_map/pallas_call | solution.py:287
  10.2 2.2 %shard_map.110 = (bf16[2,64,8,128]{3,2,1,0:T(8,128)(2,1)S(1)}, bf16[96,8,128]{2,1,0:T(8,128)(2,1)S(1)}, f32[3,32,8,128]{3,2,1,0:T(8,128)S(1)}, f32[2,3,8,128]{3,2,1,0:T(8,128)S(1)}) custom-call(f32[2,130,8,128]{3,2,1,0:T(8,128)S(1)} %get-tuple-element.20.refs_0_, f32[2,128,8,128]{3,2,1,0:T(8,128)S(1)} %get-tuple-element.21.refs_1_, ...), custom_call_target="tpu_custom_call" | custom-call | flops 1358954496 | bytes 4481024 | tf_op jit(solution)/shard_map/pallas_call | solution.py:287
  12.4 6.9 %collective-permute-start.2 = (bf16[96,8,128]{2,1,0:T(8,128)(2,1)S(1)}, bf16[96,8,128]{2,1,0:T(8,128)(2,1)S(1)}, u32[]{:S(2)}, u32[]{:S(2)}) collective-permute-start(bf16[96,8,128]{2,1,0:T(8,128)(2,1)S(1)} %get-tuple-element.24), channel_id=1, source_target_pairs={{0,1},{1,0},{2,3},{3,2},{4,5},{5,4},{6,7},{7,6},{8,9},{9,8},{10,11... | collective-permute-start | bytes 589832 | tf_op jit(solution)/shard_map/ppermute | solution.py:265
  19.3 1.1 %collective-permute-done.2 = bf16[96,8,128]{2,1,0:T(8,128)(2,1)S(1)} collective-permute-done((bf16[96,8,128]{2,1,0:T(8,128)(2,1)S(1)}, bf16[96,8,128]{2,1,0:T(8,128)(2,1)S(1)}, u32[]{:S(2)}, u32[]{:S(2)}) %collective-permute-start.2) | collective-permute-done | bytes 196640 | tf_op jit(solution)/shard_map/ppermute | solution.py:265
  20.4 0.1 fusion.16
  20.5 2.3 %shard_map.111 = (bf16[2,64,8,128]{3,2,1,0:T(8,128)(2,1)S(1)}, bf16[98,8,128]{2,1,0:T(8,128)(2,1)S(1)}, f32[3,32,8,128]{3,2,1,0:T(8,128)S(1)}, bf16[2,8,128]{2,1,0:T(8,128)(2,1)S(1)}) custom-call(f32[2,130,8,128]{3,2,1,0:T(8,128)S(1)} %get-tuple-element.20.refs_0_, f32[2,128,8,128]{3,2,1,0:T(8,128)S(1)} %get-tuple-element.21.refs_1_, ...), custom_call_target="tpu_custom_call" | custom-call | flops 1358954496 | bytes 4505600 | tf_op jit(solution)/shard_map/pallas_call | solution.py:287
  22.9 0.5 collective-permute-start.3
  23.4 2.4 %collective-permute-start.4 = (bf16[96,8,128]{2,1,0:T(8,128)(2,1)S(1)}, bf16[96,8,128]{2,1,0:T(8,128)(2,1)S(1)}, u32[]{:S(2)}, u32[]{:S(2)}) collective-permute-start(bf16[96,8,128]{2,1,0:T(8,128)(2,1)S(1)} %pad_maximum_fusion.1), channel_id=1, source_target_pairs={{0,2},{1,3},{2,0},{3,1},{4,6},{5,7},{6,4},{7,5},{8,10},{9,11},{10,... | collective-permute-start | bytes 589832 | tf_op jit(solution)/shard_map/ppermute | solution.py:265
  25.7 5.4 %collective-permute-done.4 = bf16[96,8,128]{2,1,0:T(8,128)(2,1)S(1)} collective-permute-done((bf16[96,8,128]{2,1,0:T(8,128)(2,1)S(1)}, bf16[96,8,128]{2,1,0:T(8,128)(2,1)S(1)}, u32[]{:S(2)}, u32[]{:S(2)}) %collective-permute-start.4) | collective-permute-done | bytes 196640 | tf_op jit(solution)/shard_map/ppermute | solution.py:265
  31.2 0.1 convert_maximum_fusion
  31.4 2.0 %collective-permute-start.5 = (bf16[49,8,128]{2,1,0:T(8,128)(2,1)S(1)}, bf16[49,8,128]{2,1,0:T(8,128)(2,1)S(1)}, u32[]{:S(2)}, u32[]{:S(2)}) collective-permute-start(bf16[49,8,128]{2,1,0:T(8,128)(2,1)S(1)} %pad_maximum_fusion.3), channel_id=1, source_target_pairs={{0,4},{1,5},{2,6},{3,7},{4,0},{5,1},{6,2},{7,3},{8,12},{9,13},{10,... | collective-permute-start | bytes 301064 | tf_op jit(solution)/shard_map/ppermute | solution.py:265
  33.4 2.7 %collective-permute-done.5 = bf16[49,8,128]{2,1,0:T(8,128)(2,1)S(1)} collective-permute-done((bf16[49,8,128]{2,1,0:T(8,128)(2,1)S(1)}, bf16[49,8,128]{2,1,0:T(8,128)(2,1)S(1)}, u32[]{:S(2)}, u32[]{:S(2)}) %collective-permute-start.5) | collective-permute-done | bytes 100384 | tf_op jit(solution)/shard_map/ppermute | solution.py:265
  36.1 0.0 copy-start
  36.2 0.0 copy-start.3
  36.2 0.0 copy-start.4
  36.3 3.0 %collective-permute-start.6 = (bf16[49,8,128]{2,1,0:T(8,128)(2,1)S(1)}, bf16[49,8,128]{2,1,0:T(8,128)(2,1)S(1)}, u32[]{:S(2)}, u32[]{:S(2)}) collective-permute-start(bf16[49,8,128]{2,1,0:T(8,128)(2,1)S(1)} %pad_maximum_fusion.4), channel_id=1, source_target_pairs={{0,8},{1,9},{2,10},{3,11},{4,12},{5,13},{6,14},{7,15},{8,0},{9,1},... | collective-permute-start | bytes 301064 | tf_op jit(solution)/shard_map/ppermute | solution.py:265
  39.3 2.6 %collective-permute-done.6 = bf16[49,8,128]{2,1,0:T(8,128)(2,1)S(1)} collective-permute-done((bf16[49,8,128]{2,1,0:T(8,128)(2,1)S(1)}, bf16[49,8,128]{2,1,0:T(8,128)(2,1)S(1)}, u32[]{:S(2)}, u32[]{:S(2)}) %collective-permute-start.6) | collective-permute-done | bytes 100384 | tf_op jit(solution)/shard_map/ppermute | solution.py:265
  41.9 0.1 divide_convert_fusion
  42.0 2.1 %collective-permute-start.7 = (bf16[16,8,128]{2,1,0:T(8,128)(2,1)S(1)}, bf16[16,8,128]{2,1,0:T(8,128)(2,1)S(1)}, u32[]{:S(2)}, u32[]{:S(2)}) collective-permute-start(bf16[16,8,128]{2,1,0:T(8,128)(2,1)S(1)} %divide_convert_fusion), channel_id=1, source_target_pairs={{0,4},{1,5},{2,6},{3,7},{4,0},{5,1},{6,2},{7,3},{8,12},{9,13},{10,... | collective-permute-start | bytes 98312 | tf_op jit(solution)/shard_map/ppermute | solution.py:265
  44.1 1.9 %collective-permute-done.7 = bf16[16,8,128]{2,1,0:T(8,128)(2,1)S(1)} collective-permute-done((bf16[16,8,128]{2,1,0:T(8,128)(2,1)S(1)}, bf16[16,8,128]{2,1,0:T(8,128)(2,1)S(1)}, u32[]{:S(2)}, u32[]{:S(2)}) %collective-permute-start.7) | collective-permute-done | bytes 32800 | tf_op jit(solution)/shard_map/ppermute | solution.py:265
  46.0 1.7 %collective-permute-start.8 = (bf16[33,8,128]{2,1,0:T(8,128)(2,1)S(1)}, bf16[33,8,128]{2,1,0:T(8,128)(2,1)S(1)}, u32[]{:S(2)}, u32[]{:S(2)}) collective-permute-start(bf16[33,8,128]{2,1,0:T(8,128)(2,1)S(1)} %pad_maximum_fusion.5), channel_id=1, source_target_pairs={{0,2},{1,3},{2,0},{3,1},{4,6},{5,7},{6,4},{7,5},{8,10},{9,11},{10,... | collective-permute-start | bytes 202760 | tf_op jit(solution)/shard_map/ppermute | solution.py:265
  47.8 2.5 %collective-permute-done.8 = bf16[33,8,128]{2,1,0:T(8,128)(2,1)S(1)} collective-permute-done((bf16[33,8,128]{2,1,0:T(8,128)(2,1)S(1)}, bf16[33,8,128]{2,1,0:T(8,128)(2,1)S(1)}, u32[]{:S(2)}, u32[]{:S(2)}) %collective-permute-start.8) | collective-permute-done | bytes 67616 | tf_op jit(solution)/shard_map/ppermute | solution.py:265
  50.3 0.1 collective-permute-start.9
  50.5 1.3 %collective-permute-done.9 = bf16[64,8,128]{2,1,0:T(8,128)(2,1)S(1)} collective-permute-done((bf16[64,8,128]{2,1,0:T(8,128)(2,1)S(1)}, bf16[64,8,128]{2,1,0:T(8,128)(2,1)S(1)}, u32[]{:S(2)}, u32[]{:S(2)}) %collective-permute-start.9) | collective-permute-done | bytes 131104 | tf_op jit(solution)/shard_map/ppermute | solution.py:265
  51.8 4.6 %shard_map.112 = bf16[2,128,8,128]{3,2,1,0:T(8,128)(2,1)} custom-call(bf16[2,64,8,128]{3,2,1,0:T(8,128)(2,1)S(1)} %get-tuple-element.22.early_ref, bf16[2,64,8,128]{3,2,1,0:T(8,128)(2,1)S(1)} %get-tuple-element.27.late_ref, bf16[128,8,128]{2,1,0:T(8,128)(2,1)S(1)} %pad_maximum_fusion.pooled_ref, bf16[4,8,128]{2,1,0:T(8,128)(2,1)S(1)} %pad_maximum_fusion.6.strip_ref, ...), custom_call_target="tpu_custom_call" | custom-call | flops 452984832 | bytes 1647104 | tf_op jit(solution)/shard_map/pallas_call | solution.py:287
  (40 shorter events, 0.3 us)
Async XLA Ops:
  0.0 2.2 %collective-permute-start = (bf16[2,128,8,128]{3,2,1,0:T(8,128)(2,1)}, bf16[2,128,8,128]{3,2,1,0:T(8,128)(2,1)S(1)}, u32[]{:S(2)}, u32[]{:S(2)}) collective-permute-start(bf16[2,128,8,128]{3,2,1,0:T(8,128)(2,1)} %own_ref.1), channel_id=1, source_target_pairs={{0,1},{1,0},{2,3},{3,2},{4,5},{5,4},{6,7},{7,6},{8,9},{9,8},{10,11... | collective-permute-start | bytes 1572872 | tf_op jit(solution)/shard_map/ppermute | solution.py:265
  0.5 9.7 %collective-permute-start.1 = (bf16[2,128,8,128]{3,2,1,0:T(8,128)(2,1)}, bf16[2,128,8,128]{3,2,1,0:T(8,128)(2,1)S(1)}, u32[]{:S(2)}, u32[]{:S(2)}) collective-permute-start(bf16[2,128,8,128]{3,2,1,0:T(8,128)(2,1)} %own_ref.1), channel_id=1, source_target_pairs={{1,2},{3,4},{5,6},{7,8},{9,10},{11,12},{13,14},{2,1},{4,3},{6,5},{... | collective-permute-start | bytes 1572872 | tf_op jit(solution)/shard_map/ppermute | solution.py:326
  2.2 1.2 %copy-start.5 = (bf16[27,128,128]{2,1,0:T(8,128)(2,1)S(1)}, bf16[27,128,128]{2,1,0:T(8,128)(2,1)}, u32[]{:S(2)}) copy-start(bf16[27,128,128]{2,1,0:T(8,128)(2,1)} %param.13) | copy-start | bytes 2654212
  3.4 1.2 %copy-start.7 = (bf16[27,128,128]{2,1,0:T(8,128)(2,1)S(1)}, bf16[27,128,128]{2,1,0:T(8,128)(2,1)}, u32[]{:S(2)}) copy-start(bf16[27,128,128]{2,1,0:T(8,128)(2,1)} %param.14) | copy-start | bytes 2654212
  4.6 1.0 %copy-start.9 = (bf16[2,128,8,128]{3,2,1,0:T(8,128)(2,1)S(1)}, bf16[2,128,8,128]{3,2,1,0:T(8,128)(2,1)}, u32[]{:S(2)}) copy-start(bf16[2,128,8,128]{3,2,1,0:T(8,128)(2,1)} %own_ref.1) | copy-start | bytes 1572868
  5.6 4.6 %copy-start.6 = (bf16[27,128,128]{2,1,0:T(8,128)(2,1)S(1)}, bf16[27,128,128]{2,1,0:T(8,128)(2,1)}, u32[]{:S(2)}) copy-start(bf16[27,128,128]{2,1,0:T(8,128)(2,1)} %param.13) | copy-start | bytes 2654212
  5.6 4.6 %copy-start.8 = (bf16[27,128,128]{2,1,0:T(8,128)(2,1)S(1)}, bf16[27,128,128]{2,1,0:T(8,128)(2,1)}, u32[]{:S(2)}) copy-start(bf16[27,128,128]{2,1,0:T(8,128)(2,1)} %param.14) | copy-start | bytes 2654212
  5.6 4.6 %copy-start.10 = (bf16[128,128]{1,0:T(8,128)(2,1)S(1)}, bf16[128,128]{1,0:T(8,128)(2,1)}, u32[]{:S(2)}) copy-start(bf16[128,128]{1,0:T(8,128)(2,1)} %refs_5_.3) | copy-start | bytes 98308
  5.6 4.6 %copy-start.11 = (bf16[128,128]{1,0:T(8,128)(2,1)S(1)}, bf16[128,128]{1,0:T(8,128)(2,1)}, u32[]{:S(2)}) copy-start(bf16[128,128]{1,0:T(8,128)(2,1)} %refs_6_.3) | copy-start | bytes 98308
  12.4 8.0 %collective-permute-start.2 = (bf16[96,8,128]{2,1,0:T(8,128)(2,1)S(1)}, bf16[96,8,128]{2,1,0:T(8,128)(2,1)S(1)}, u32[]{:S(2)}, u32[]{:S(2)}) collective-permute-start(bf16[96,8,128]{2,1,0:T(8,128)(2,1)S(1)} %get-tuple-element.24), channel_id=1, source_target_pairs={{0,1},{1,0},{2,3},{3,2},{4,5},{5,4},{6,7},{7,6},{8,9},{9,8},{10,11... | collective-permute-start | bytes 589832 | tf_op jit(solution)/shard_map/ppermute | solution.py:265
  22.9 8.3 %collective-permute-start.3 = (bf16[98,8,128]{2,1,0:T(8,128)(2,1)S(1)}, bf16[98,8,128]{2,1,0:T(8,128)(2,1)S(1)}, u32[]{:S(2)}, u32[]{:S(2)}) collective-permute-start(bf16[98,8,128]{2,1,0:T(8,128)(2,1)S(1)} %get-tuple-element.29), channel_id=1, source_target_pairs={{0,1},{1,0},{2,3},{3,2},{4,5},{5,4},{6,7},{7,6},{8,9},{9,8},{10,11... | collective-permute-start | bytes 602120 | tf_op jit(solution)/shard_map/ppermute | solution.py:265
  23.4 7.8 %collective-permute-start.4 = (bf16[96,8,128]{2,1,0:T(8,128)(2,1)S(1)}, bf16[96,8,128]{2,1,0:T(8,128)(2,1)S(1)}, u32[]{:S(2)}, u32[]{:S(2)}) collective-permute-start(bf16[96,8,128]{2,1,0:T(8,128)(2,1)S(1)} %pad_maximum_fusion.1), channel_id=1, source_target_pairs={{0,2},{1,3},{2,0},{3,1},{4,6},{5,7},{6,4},{7,5},{8,10},{9,11},{10,... | collective-permute-start | bytes 589832 | tf_op jit(solution)/shard_map/ppermute | solution.py:265
  31.4 4.7 %collective-permute-start.5 = (bf16[49,8,128]{2,1,0:T(8,128)(2,1)S(1)}, bf16[49,8,128]{2,1,0:T(8,128)(2,1)S(1)}, u32[]{:S(2)}, u32[]{:S(2)}) collective-permute-start(bf16[49,8,128]{2,1,0:T(8,128)(2,1)S(1)} %pad_maximum_fusion.3), channel_id=1, source_target_pairs={{0,4},{1,5},{2,6},{3,7},{4,0},{5,1},{6,2},{7,3},{8,12},{9,13},{10,... | collective-permute-start | bytes 301064 | tf_op jit(solution)/shard_map/ppermute | solution.py:265
  36.1 15.7 %copy-start = (bf16[9,128,128]{2,1,0:T(8,128)(2,1)S(1)}, bf16[9,128,128]{2,1,0:T(8,128)(2,1)}, u32[]{:S(2)}) copy-start(bf16[9,128,128]{2,1,0:T(8,128)(2,1)} %param.17) | copy-start | bytes 884740
  36.1 15.7 %copy-start.1 = (bf16[9,128,128]{2,1,0:T(8,128)(2,1)S(1)}, bf16[9,128,128]{2,1,0:T(8,128)(2,1)}, u32[]{:S(2)}) copy-start(bf16[9,128,128]{2,1,0:T(8,128)(2,1)} %param.18) | copy-start | bytes 884740
  36.2 15.7 %copy-start.2 = (bf16[128,512]{1,0:T(8,128)(2,1)S(1)}, bf16[128,512]{1,0:T(8,128)(2,1)}, u32[]{:S(2)}) copy-start(bf16[128,512]{1,0:T(8,128)(2,1)} %in_ref.1) | copy-start | bytes 393220
  36.2 15.7 %copy-start.3 = (bf16[512,128]{1,0:T(8,128)(2,1)S(1)}, bf16[512,128]{1,0:T(8,128)(2,1)}, u32[]{:S(2)}) copy-start(bf16[512,128]{1,0:T(8,128)(2,1)} %out_w_ref.1) | copy-start | bytes 393220
  36.2 15.6 %copy-start.4 = (f32[128]{0:T(128)S(1)}, f32[128]{0:T(128)}, u32[]{:S(2)}) copy-start(f32[128]{0:T(128)} %param.19) | copy-start | bytes 1540
  36.3 5.7 %collective-permute-start.6 = (bf16[49,8,128]{2,1,0:T(8,128)(2,1)S(1)}, bf16[49,8,128]{2,1,0:T(8,128)(2,1)S(1)}, u32[]{:S(2)}, u32[]{:S(2)}) collective-permute-start(bf16[49,8,128]{2,1,0:T(8,128)(2,1)S(1)} %pad_maximum_fusion.4), channel_id=1, source_target_pairs={{0,8},{1,9},{2,10},{3,11},{4,12},{5,13},{6,14},{7,15},{8,0},{9,1},... | collective-permute-start | bytes 301064 | tf_op jit(solution)/shard_map/ppermute | solution.py:265
  42.0 4.0 %collective-permute-start.7 = (bf16[16,8,128]{2,1,0:T(8,128)(2,1)S(1)}, bf16[16,8,128]{2,1,0:T(8,128)(2,1)S(1)}, u32[]{:S(2)}, u32[]{:S(2)}) collective-permute-start(bf16[16,8,128]{2,1,0:T(8,128)(2,1)S(1)} %divide_convert_fusion), channel_id=1, source_target_pairs={{0,4},{1,5},{2,6},{3,7},{4,0},{5,1},{6,2},{7,3},{8,12},{9,13},{10,... | collective-permute-start | bytes 98312 | tf_op jit(solution)/shard_map/ppermute | solution.py:265
  46.0 4.3 %collective-permute-start.8 = (bf16[33,8,128]{2,1,0:T(8,128)(2,1)S(1)}, bf16[33,8,128]{2,1,0:T(8,128)(2,1)S(1)}, u32[]{:S(2)}, u32[]{:S(2)}) collective-permute-start(bf16[33,8,128]{2,1,0:T(8,128)(2,1)S(1)} %pad_maximum_fusion.5), channel_id=1, source_target_pairs={{0,2},{1,3},{2,0},{3,1},{4,6},{5,7},{6,4},{7,5},{8,10},{9,11},{10,... | collective-permute-start | bytes 202760 | tf_op jit(solution)/shard_map/ppermute | solution.py:265
  50.3 1.4 %collective-permute-start.9 = (bf16[64,8,128]{2,1,0:T(8,128)(2,1)S(1)}, bf16[64,8,128]{2,1,0:T(8,128)(2,1)S(1)}, u32[]{:S(2)}, u32[]{:S(2)}) collective-permute-start(bf16[64,8,128]{2,1,0:T(8,128)(2,1)S(1)} %pad_maximum_fusion.2), channel_id=1, source_target_pairs={{0,1},{1,0},{2,3},{3,2},{4,5},{5,4},{6,7},{7,6},{8,9},{9,8},{10,11... | collective-permute-start | bytes 393224 | tf_op jit(solution)/shard_map/ppermute | solution.py:265

commit v4 on v3

--- a/solution.py
+++ b/solution.py
@@ -15,8 +15,16 @@
 UPPER = ({2: 2}, {2: 1, 3: 2})
 
 
+SLOPE = 0.7978845608028654
+BEND = SLOPE * 0.044715
+
+
+def twice_activate(values):
+    return values + values * jnp.tanh(values * (SLOPE + BEND * (values * values)))
+
+
 def activate(values):
-    return 0.5 * values * (1.0 + jnp.tanh(0.7978845608028654 * (values + 0.044715 * values**3)))
+    return 0.5 * twice_activate(values)
 
 
 def beside(blocks):
@@ -74,19 +82,34 @@
         rows_ref[row, length - width :] = blank
 
 
-def first_kernel(axis, own_ref, near_ref, w1_ref, w2_ref, edge_ref, part_ref, rows_ref, mid_ref):
-    across = own_ref.shape[1]
-    side = lax.rem(lax.axis_index(axis), 2)
+def cut_kernel(axis, own_ref, first_ref, second_ref, sems):
+    half = own_ref.shape[1] // 2
+    kept = lax.rem(lax.axis_index(axis) // 2, 2)
+    fetches = []
+    for k, (at, target) in enumerate(((kept, first_ref), (1 - kept, second_ref))):
+        place = pl.ds(at * (half - 2), half + 2)
+        fetches.append(pltpu.make_async_copy(own_ref.at[:, place], target, sems.at[k]))
+    for fetch in fetches:
+        fetch.start()
+    for fetch in fetches:
+        fetch.wait()
+
+
+def first_kernel(axis, cut0_ref, cut1_ref, near_ref, w1_ref, w2_ref, edge_ref, part_ref, rows_ref, mid_ref):
+    across = near_ref.shape[1]
+    span = across // 2
+    index = lax.axis_index(axis)
+    side = lax.rem(index, 2)
+    kept = lax.rem(index // 2, 2)
     clear_ends(rows_ref, 1)
     clear_ends(mid_ref, 1)
     clear_ends(edge_ref, 1)
-    for row, (source, at) in enumerate(
-        ((own_ref, side), (own_ref, 1 - side), (near_ref, side), (near_ref, 1 - side))
-    ):
-        rows_ref[row, 1 : across + 1] = source[at]
+    for row, at in enumerate((side, 1 - side)):
+        rows_ref[row, pl.ds(1 + kept * (span - 2), span + 2)] = cut0_ref[at]
+        rows_ref[row, pl.ds(1 + (1 - kept) * (span - 2), span + 2)] = cut1_ref[at]
+        rows_ref[2 + row, 1 : across + 1] = near_ref[at]
     taps = (2 * side, 1, 2 - 2 * side)
     back = (2 - 2 * side, 1, 2 * side)
-    span = across // 2
     for step in range(2):
         start = step * span
         low, high = conv_rows(rows_ref, w1_ref, taps, start, span, PAIR)
@@ -109,7 +132,7 @@
         state_ref, feature_ref, message_ref, keep_ref, strip_ref, rows_ref, mid_ref = refs[8:]
     else:
         feature_ref, message_ref, keep_ref, state_ref, rows_ref, mid_ref = refs[8:]
-    across, depth, channels = far_ref.shape[1:]
+    across, depth, channels = part_ref.shape[1:]
     devices = lax.axis_size(axis)
     index = lax.axis_index(axis)
     side = lax.rem(index, 2)
@@ -117,13 +140,14 @@
     kept = lax.rem(index // 2, 2)
     half = kept if second else 1 - kept
     clear_ends(rows_ref, 2)
-    inner = pl.ds(half * (span - 2), span + 2)
     local = pl.ds(2 - 2 * half, span + 2)
-    rows_ref[0, local] = far_ref[1 - side, inner]
-    rows_ref[1, local] = far_ref[side, inner]
+    border = jnp.logical_or(index == 0, index == devices - 1)
+    blank = jnp.zeros((span + 2, depth, channels), BF)
+    rows_ref[0, local] = jnp.where(border, blank, far_ref[1 - side])
+    rows_ref[1, local] = jnp.where(border, blank, far_ref[side])
     back = (2 - 2 * side, 1, 2 * side)
     low, high = conv_rows(rows_ref, w1_ref, back, 0, span + 2, UPPER, {2: 0, 3: 1})
-    inside = jnp.where(jnp.logical_or(index == 0, index == devices - 1), 0.0, 1.0)
+    inside = jnp.where(border, 0.0, 1.0)
     around = pl.ds(half * span, span + 2)
     mid_ref[1] = activate(low + edge_ref[0, around]).astype(BF)
     mid_ref[0] = (activate(high + edge_ref[1, around]) * inside).astype(BF)
@@ -139,7 +163,8 @@
         feature = (outs[u] + part_ref[u, place]).astype(BF)
         feature_ref[at] = feature
         both = jnp.dot(feature.reshape(-1, channels), score, preferred_element_type=F32)
-        columns = prior_ref[at, half]
+        columns = prior_ref[at]
+        columns = jnp.where(half == 0, columns[:, :span], columns[:, span:])
         prior = jnp.stack(
             [jnp.broadcast_to(columns[:, y : y + 1], (depth, channels)) for y in range(span)]
         )
@@ -253,8 +278,9 @@
             joined = (feature * (plane + mix_ref[row])).reshape(-1, channels)
             mean = jnp.mean(joined * joined, axis=-1, keepdims=True)
             normed = (joined * lax.rsqrt(mean + 1e-06) * gain).astype(BF)
-            hidden = activate(jnp.dot(normed, in_ref[...], preferred_element_type=F32)).astype(BF)
-            update = jnp.dot(hidden, out_w_ref[...], preferred_element_type=F32)
+            hidden = jnp.dot(normed, in_ref[...], preferred_element_type=F32)
+            hidden = twice_activate(hidden).astype(BF)
+            update = 0.5 * jnp.dot(hidden, out_w_ref[...], preferred_element_type=F32)
             out_ref[row, pl.ds(start, span)] = (
                 (joined + update).astype(BF).reshape(span, depth, channels)
             )
@@ -282,20 +308,21 @@
     return [message[k * size : (k + 1) * size] for k in range(3)]
 
 
-def kernel_call(body, outs, scratch, flops, *operands):
+def kernel_call(body, outs, scratch, flops, *operands, spaces=None):
     moved = sum(o.size * o.dtype.itemsize for o in operands)
     return pl.pallas_call(
         body,
         out_shape=outs,
-        in_specs=[IN_VMEM] * len(operands),
+        in_specs=[pl.BlockSpec(memory_space=m) for m in spaces or [pltpu.VMEM] * len(operands)],
         out_specs=jax.tree.map(lambda _: IN_VMEM, outs),
         scratch_shapes=scratch,
-        compiler_params=pltpu.CompilerParams(vmem_limit_bytes=12 * 1024 * 1024),
+        compiler_params=pltpu.CompilerParams(vmem_limit_bytes=14 * 1024 * 1024),
         cost_estimate=pl.CostEstimate(flops=flops, bytes_accessed=moved, transcendentals=0),
     )(*operands)
 
 
 def on_device(
+    others,
     axis,
     voxels,
     prior,
@@ -322,9 +349,26 @@
     def beyond_edge(at):
         return at + 2 * (at % 2) - 1
 
-    pairs = [(i, i + 1) for i in range(1, devices - 1, 2)]
-    far = lax.ppermute(voxels, axis, pairs + [(j, i) for i, j in pairs])
+    parts = lax.axis_size(others)
+    pairs = []
+    for base in range(0, parts * devices, devices):
+        twin = base ^ devices if (base ^ devices) < parts * devices else base
+        pairs += [(base, twin), (base + devices - 1, twin + devices - 1)]
+        for i in range(base + 1, base + devices - 1, 2):
+            pairs += [(i, i + 1), (i + 1, i)]
+    cut = jax.ShapeDtypeStruct((rows, half + 2, depth, channels), BF)
+    cuts = kernel_call(
+        functools.partial(cut_kernel, axis),
+        (cut, cut),
+        [pltpu.SemaphoreType.DMA((2,))],
+        flops,
+        voxels,
+        spaces=(pltpu.HBM,),
+    )
+    far0 = lax.ppermute(cuts[0], (others, axis), pairs)
+    far1 = lax.ppermute(cuts[1], (others, axis), pairs)
     near = swap(voxels, axis, 1)
+    prior = prior.swapaxes(1, 2)
     edge, part = kernel_call(
         functools.partial(first_kernel, axis),
         (
@@ -336,14 +380,13 @@
             pltpu.VMEM((2, across + 2, depth, channels), BF),
         ],
         2 * flops,
-        voxels,
+        *cuts,
         near,
         w_first,
         w_second,
     )
-    prior = prior.reshape(rows, 2, half, depth).swapaxes(2, 3)
-
-    def half_call(second, *state):
+
+    def half_call(second, far, *state):
         feature = jax.ShapeDtypeStruct((rows, half, depth, channels), BF)
         message = jax.ShapeDtypeStruct((3 * quarter + 2 * second, depth, channels), BF)
         keep = jax.ShapeDtypeStruct((3, quarter, depth, channels), F32)
@@ -372,12 +415,12 @@
         )
 
     masks = [1 << bit for bit in range(devices.bit_length() - 1)]
-    early, message, keep, state = half_call(False)
+    early, message, keep, state = half_call(False, far0)
     got = swap(message, axis, masks[0])
     sent = jnp.concatenate([p.astype(BF) for p in merge(keep, thirds(got))])
     sent, state = lax.optimization_barrier((sent, state))
     arriving = swap(sent, axis, masks[1])
-    late, message, keep, strip = half_call(True, state)
+    late, message, keep, strip = half_call(True, far1, state)
     got = swap(message, axis, masks[0])
     beyond = got[3 * quarter]
     carried = [got[3 * quarter + 1]]
@@ -432,7 +475,7 @@
 def solution(mesh):
     spread = ("scene", "gx")
     return jax.shard_map(
-        functools.partial(on_device, "gx"),
+        functools.partial(on_device, "scene", "gx"),
         mesh=mesh,
         in_specs=(P(spread, None, None, None), P(spread, None, None)) + (P(),) * 9,
         out_specs=P(spread, None, None, None),

time: 56.9 us -> 57.3 us (level)
  waiting for transfers between devices: 17.8 us -> 21.7 us
  local copies, waits for them, and re-layouts: 4.25 us -> 1.18 us
    ppermute x1 -> x2, waiting for transfers between devices: 0.01 us -> 4.82 us  [the longest x1 4.82 us: on_device(): far1 = lax.ppermute(cuts[1], (others, axis), pairs)]
    ppermute x9, starting transfers between devices: 19.3 us -> 15.8 us  [swap(): return lax.ppermute(values, axis, [(i, i ^ mask) for i in range(devices)])]
    ppermute x1 -> x2, starting transfers between devices: 0.68 us -> 4.13 us  [the longest x1 2.64 us: on_device(): far0 = lax.ppermute(cuts[0], (others, axis), pairs)]
    unnamed x24 -> x22, local copies, waits for them, and re-layouts: 3.42 us -> 1.13 us
    ppermute x9, waiting for transfers between devices: 17.8 us -> 16.9 us  [swap(): return lax.ppermute(values, axis, [(i, i ^ mask) for i in range(devices)])]
    reshape x2 -> x0, local copies, waits for them, and re-layouts: 0.78 us -> none  [on_device(): prior = prior.reshape(rows, 2, half, depth).swapaxes(2, 3)]
    pallas_call x4 -> x5, Pallas kernels: 13.7 us -> 13.5 us  [kernel_call(): pl.pallas_call(body, out_shape=outs, in_specs=[pl.BlockSpec(memory_space=...]
  transfers between devices with their start and end apart: 10 -> 11, of which waited for: 8 -> 7; matrix products, arithmetic and copies ran while one was open for 1% -> 0% of each run, Pallas kernels for 8% -> 8%
where the time goes in v4:
time: 57.3 us; the launch traced here: 57.1 us
  waiting for transfers between devices  21.7 us (38%)
  starting transfers between devices  19.9 us (35%)
  Pallas kernels  13.5 us (24%)
  local copies, waits for them, and re-layouts  1.18 us (2%)
    ppermute x9, waiting for transfers between devices, swap(): return lax.ppermute(values, axis, [(i, i ^ mask) for i in range(devices)])  16.9 us
    ppermute x9, starting transfers between devices, swap(): return lax.ppermute(values, axis, [(i, i ^ mask) for i in range(devices)])  15.8 us
    pallas_call x5, Pallas kernels, kernel_call(): pl.pallas_call(body, out_shape=outs, in_specs=[pl.BlockSpec(memory_space=...  13.5 us
    ppermute x1, waiting for transfers between devices, on_device(): far1 = lax.ppermute(cuts[1], (others, axis), pairs)  4.82 us
    ppermute x1, starting transfers between devices, on_device(): far0 = lax.ppermute(cuts[0], (others, axis), pairs)  2.64 us
    ppermute x1, starting transfers between devices, on_device(): far1 = lax.ppermute(cuts[1], (others, axis), pairs)  1.49 us
  transfers between devices with their start and end apart: 11, of which 7 were waited for; matrix products, arithmetic and copies ran while one was open for 0% of the time, Pallas kernels for 8%

profile of v4, /device:TPU:0, one launch (start us, length us, event | category | flops | bytes accessed | tf_op | source)
XLA Modules:
  0.0 57.1 jit_solution(16608193641963623483)
XLA Ops:
  0.0 0.5 collective-permute-start
  0.5 1.1 %copy-done.7 = bf16[2,128,8,128]{3,2,1,0:T(8,128)(2,1)S(1)} copy-done((bf16[2,128,8,128]{3,2,1,0:T(8,128)(2,1)S(1)}, bf16[2,128,8,128]{3,2,1,0:T(8,128)(2,1)}, u32[]{:S(2)}) %copy-start.7) | copy-done | bytes 524312
  1.6 0.1 shard_map.109
  1.6 2.6 %collective-permute-start.1 = (bf16[2,66,8,128]{3,2,1,0:T(8,128)(2,1)S(1)}, bf16[2,66,8,128]{3,2,1,0:T(8,128)(2,1)S(1)}, u32[]{:S(2)}, u32[]{:S(2)}) collective-permute-start(bf16[2,66,8,128]{3,2,1,0:T(8,128)(2,1)S(1)} %get-tuple-element.22.cut0_ref), channel_id=1, source_target_pairs={{0,16},{15,31},{1,2},{2,1},{3,4},{4,3},{5,6},{6,5},{7,8},{8,7},{9,... | collective-permute-start | bytes 811016 | tf_op jit(solution)/shard_map/ppermute | solution.py:368
  4.3 0.0 copy-start.8
  4.3 0.0 copy-start.9
  4.3 4.6 %shard_map.110 = (f32[2,130,8,128]{3,2,1,0:T(8,128)S(1)}, f32[2,128,8,128]{3,2,1,0:T(8,128)S(1)}) custom-call(bf16[2,66,8,128]{3,2,1,0:T(8,128)(2,1)S(1)} %get-tuple-element.22.cut0_ref, bf16[2,66,8,128]{3,2,1,0:T(8,128)(2,1)S(1)} %get-tuple-element.23.cut1_ref, bf16[2,128,8,128]{3,2,1,0:T(8,128)(2,1)S(1)} %collective-permute-done.near_ref, ...), custom_call_target="tpu_custom_call" | custom-call | flops 3623878656 | bytes 2834432 | tf_op jit(solution)/shard_map/pallas_call | solution.py:313
  9.0 2.2 %shard_map.111 = (bf16[2,64,8,128]{3,2,1,0:T(8,128)(2,1)S(1)}, bf16[96,8,128]{2,1,0:T(8,128)(2,1)S(1)}, f32[3,32,8,128]{3,2,1,0:T(8,128)S(1)}, f32[2,3,8,128]{3,2,1,0:T(8,128)S(1)}) custom-call(f32[2,130,8,128]{3,2,1,0:T(8,128)S(1)} %get-tuple-element.24.refs_0_, f32[2,128,8,128]{3,2,1,0:T(8,128)S(1)} %get-tuple-element.25.refs_1_, ...), custom_call_target="tpu_custom_call" | custom-call | flops 1358954496 | bytes 4227072 | tf_op jit(solution)/shard_map/pallas_call | solution.py:313
  11.2 1.8 %collective-permute-start.3 = (bf16[96,8,128]{2,1,0:T(8,128)(2,1)S(1)}, bf16[96,8,128]{2,1,0:T(8,128)(2,1)S(1)}, u32[]{:S(2)}, u32[]{:S(2)}) collective-permute-start(bf16[96,8,128]{2,1,0:T(8,128)(2,1)S(1)} %get-tuple-element.28), channel_id=1, source_target_pairs={{0,1},{1,0},{2,3},{3,2},{4,5},{5,4},{6,7},{7,6},{8,9},{9,8},{10,11... | collective-permute-start | bytes 589832 | tf_op jit(solution)/shard_map/ppermute | solution.py:291
  13.0 1.5 %collective-permute-start.2 = (bf16[2,66,8,128]{3,2,1,0:T(8,128)(2,1)S(1)}, bf16[2,66,8,128]{3,2,1,0:T(8,128)(2,1)S(1)}, u32[]{:S(2)}, u32[]{:S(2)}) collective-permute-start(bf16[2,66,8,128]{3,2,1,0:T(8,128)(2,1)S(1)} %get-tuple-element.23.cut1_ref), channel_id=1, source_target_pairs={{0,16},{15,31},{1,2},{2,1},{3,4},{4,3},{5,6},{6,5},{7,8},{8,7},{9,... | collective-permute-start | bytes 811016 | tf_op jit(solution)/shard_map/ppermute | solution.py:369
  14.5 0.1 fusion.16
  14.6 4.8 %collective-permute-done.2.refs_2_ = bf16[2,66,8,128]{3,2,1,0:T(8,128)(2,1)S(1)} collective-permute-done((bf16[2,66,8,128]{3,2,1,0:T(8,128)(2,1)S(1)}, bf16[2,66,8,128]{3,2,1,0:T(8,128)(2,1)S(1)}, u32[]{:S(2)}, u32[]{:S(2)}) %collective-permute-start.2) | collective-permute-done | bytes 270368 | tf_op jit(solution)/shard_map/ppermute | solution.py:369
  19.5 2.3 %shard_map.112 = (bf16[2,64,8,128]{3,2,1,0:T(8,128)(2,1)S(1)}, bf16[98,8,128]{2,1,0:T(8,128)(2,1)S(1)}, f32[3,32,8,128]{3,2,1,0:T(8,128)S(1)}, bf16[2,8,128]{2,1,0:T(8,128)(2,1)S(1)}) custom-call(f32[2,130,8,128]{3,2,1,0:T(8,128)S(1)} %get-tuple-element.24.refs_0_, f32[2,128,8,128]{3,2,1,0:T(8,128)S(1)} %get-tuple-element.25.refs_1_, ...), custom_call_target="tpu_custom_call" | custom-call | flops 1358954496 | bytes 4251648 | tf_op jit(solution)/shard_map/pallas_call | solution.py:313
  21.8 2.5 %collective-permute-start.4 = (bf16[98,8,128]{2,1,0:T(8,128)(2,1)S(1)}, bf16[98,8,128]{2,1,0:T(8,128)(2,1)S(1)}, u32[]{:S(2)}, u32[]{:S(2)}) collective-permute-start(bf16[98,8,128]{2,1,0:T(8,128)(2,1)S(1)} %get-tuple-element.33), channel_id=1, source_target_pairs={{0,1},{1,0},{2,3},{3,2},{4,5},{5,4},{6,7},{7,6},{8,9},{9,8},{10,11... | collective-permute-start | bytes 602120 | tf_op jit(solution)/shard_map/ppermute | solution.py:291
  24.3 2.4 %collective-permute-start.5 = (bf16[96,8,128]{2,1,0:T(8,128)(2,1)S(1)}, bf16[96,8,128]{2,1,0:T(8,128)(2,1)S(1)}, u32[]{:S(2)}, u32[]{:S(2)}) collective-permute-start(bf16[96,8,128]{2,1,0:T(8,128)(2,1)S(1)} %pad_maximum_fusion.1), channel_id=1, source_target_pairs={{0,2},{1,3},{2,0},{3,1},{4,6},{5,7},{6,4},{7,5},{8,10},{9,11},{10,... | collective-permute-start | bytes 589832 | tf_op jit(solution)/shard_map/ppermute | solution.py:291
  26.7 5.5 %collective-permute-done.5 = bf16[96,8,128]{2,1,0:T(8,128)(2,1)S(1)} collective-permute-done((bf16[96,8,128]{2,1,0:T(8,128)(2,1)S(1)}, bf16[96,8,128]{2,1,0:T(8,128)(2,1)S(1)}, u32[]{:S(2)}, u32[]{:S(2)}) %collective-permute-start.5) | collective-permute-done | bytes 196640 | tf_op jit(solution)/shard_map/ppermute | solution.py:291
  32.2 0.1 convert_maximum_fusion
  32.4 1.8 %collective-permute-start.6 = (bf16[49,8,128]{2,1,0:T(8,128)(2,1)S(1)}, bf16[49,8,128]{2,1,0:T(8,128)(2,1)S(1)}, u32[]{:S(2)}, u32[]{:S(2)}) collective-permute-start(bf16[49,8,128]{2,1,0:T(8,128)(2,1)S(1)} %pad_maximum_fusion.3), channel_id=1, source_target_pairs={{0,4},{1,5},{2,6},{3,7},{4,0},{5,1},{6,2},{7,3},{8,12},{9,13},{10,... | collective-permute-start | bytes 301064 | tf_op jit(solution)/shard_map/ppermute | solution.py:291
  34.3 2.9 %collective-permute-done.6 = bf16[49,8,128]{2,1,0:T(8,128)(2,1)S(1)} collective-permute-done((bf16[49,8,128]{2,1,0:T(8,128)(2,1)S(1)}, bf16[49,8,128]{2,1,0:T(8,128)(2,1)S(1)}, u32[]{:S(2)}, u32[]{:S(2)}) %collective-permute-start.6) | collective-permute-done | bytes 100384 | tf_op jit(solution)/shard_map/ppermute | solution.py:291
  37.2 0.0 copy-start
  37.2 0.0 copy-start.1
  37.2 0.0 copy-start.4
  37.3 2.9 %collective-permute-start.7 = (bf16[49,8,128]{2,1,0:T(8,128)(2,1)S(1)}, bf16[49,8,128]{2,1,0:T(8,128)(2,1)S(1)}, u32[]{:S(2)}, u32[]{:S(2)}) collective-permute-start(bf16[49,8,128]{2,1,0:T(8,128)(2,1)S(1)} %pad_maximum_fusion.4), channel_id=1, source_target_pairs={{0,8},{1,9},{2,10},{3,11},{4,12},{5,13},{6,14},{7,15},{8,0},{9,1},... | collective-permute-start | bytes 301064 | tf_op jit(solution)/shard_map/ppermute | solution.py:291
  40.2 2.8 %collective-permute-done.7 = bf16[49,8,128]{2,1,0:T(8,128)(2,1)S(1)} collective-permute-done((bf16[49,8,128]{2,1,0:T(8,128)(2,1)S(1)}, bf16[49,8,128]{2,1,0:T(8,128)(2,1)S(1)}, u32[]{:S(2)}, u32[]{:S(2)}) %collective-permute-start.7) | collective-permute-done | bytes 100384 | tf_op jit(solution)/shard_map/ppermute | solution.py:291
  42.9 0.1 divide_convert_fusion
  43.0 2.0 %collective-permute-start.8 = (bf16[16,8,128]{2,1,0:T(8,128)(2,1)S(1)}, bf16[16,8,128]{2,1,0:T(8,128)(2,1)S(1)}, u32[]{:S(2)}, u32[]{:S(2)}) collective-permute-start(bf16[16,8,128]{2,1,0:T(8,128)(2,1)S(1)} %divide_convert_fusion), channel_id=1, source_target_pairs={{0,4},{1,5},{2,6},{3,7},{4,0},{5,1},{6,2},{7,3},{8,12},{9,13},{10,... | collective-permute-start | bytes 98312 | tf_op jit(solution)/shard_map/ppermute | solution.py:291
  45.0 2.0 %collective-permute-done.8 = bf16[16,8,128]{2,1,0:T(8,128)(2,1)S(1)} collective-permute-done((bf16[16,8,128]{2,1,0:T(8,128)(2,1)S(1)}, bf16[16,8,128]{2,1,0:T(8,128)(2,1)S(1)}, u32[]{:S(2)}, u32[]{:S(2)}) %collective-permute-start.8) | collective-permute-done | bytes 32800 | tf_op jit(solution)/shard_map/ppermute | solution.py:291
  47.0 1.8 %collective-permute-start.9 = (bf16[33,8,128]{2,1,0:T(8,128)(2,1)S(1)}, bf16[33,8,128]{2,1,0:T(8,128)(2,1)S(1)}, u32[]{:S(2)}, u32[]{:S(2)}) collective-permute-start(bf16[33,8,128]{2,1,0:T(8,128)(2,1)S(1)} %pad_maximum_fusion.5), channel_id=1, source_target_pairs={{0,2},{1,3},{2,0},{3,1},{4,6},{5,7},{6,4},{7,5},{8,10},{9,11},{10,... | collective-permute-start | bytes 202760 | tf_op jit(solution)/shard_map/ppermute | solution.py:291
  48.7 2.5 %collective-permute-done.9 = bf16[33,8,128]{2,1,0:T(8,128)(2,1)S(1)} collective-permute-done((bf16[33,8,128]{2,1,0:T(8,128)(2,1)S(1)}, bf16[33,8,128]{2,1,0:T(8,128)(2,1)S(1)}, u32[]{:S(2)}, u32[]{:S(2)}) %collective-permute-start.9) | collective-permute-done | bytes 67616 | tf_op jit(solution)/shard_map/ppermute | solution.py:291
  51.3 0.1 collective-permute-start.10
  51.4 1.3 %collective-permute-done.10 = bf16[64,8,128]{2,1,0:T(8,128)(2,1)S(1)} collective-permute-done((bf16[64,8,128]{2,1,0:T(8,128)(2,1)S(1)}, bf16[64,8,128]{2,1,0:T(8,128)(2,1)S(1)}, u32[]{:S(2)}, u32[]{:S(2)}) %collective-permute-start.10) | collective-permute-done | bytes 131104 | tf_op jit(solution)/shard_map/ppermute | solution.py:291
  52.8 4.3 %shard_map.113 = bf16[2,128,8,128]{3,2,1,0:T(8,128)(2,1)} custom-call(bf16[2,64,8,128]{3,2,1,0:T(8,128)(2,1)S(1)} %get-tuple-element.26.early_ref, bf16[2,64,8,128]{3,2,1,0:T(8,128)(2,1)S(1)} %get-tuple-element.31.late_ref, bf16[128,8,128]{2,1,0:T(8,128)(2,1)S(1)} %pad_maximum_fusion.pooled_ref, bf16[4,8,128]{2,1,0:T(8,128)(2,1)S(1)} %pad_maximum_fusion.6.strip_ref, ...), custom_call_target="tpu_custom_call" | custom-call | flops 452984832 | bytes 1647104 | tf_op jit(solution)/shard_map/pallas_call | solution.py:313
  (39 shorter events, 0.3 us)
Async XLA Ops:
  0.0 4.3 %copy-start.5 = (bf16[27,128,128]{2,1,0:T(8,128)(2,1)S(1)}, bf16[27,128,128]{2,1,0:T(8,128)(2,1)}, u32[]{:S(2)}) copy-start(bf16[27,128,128]{2,1,0:T(8,128)(2,1)} %param.13) | copy-start | bytes 2654212
  0.0 4.3 %copy-start.6 = (bf16[27,128,128]{2,1,0:T(8,128)(2,1)S(1)}, bf16[27,128,128]{2,1,0:T(8,128)(2,1)}, u32[]{:S(2)}) copy-start(bf16[27,128,128]{2,1,0:T(8,128)(2,1)} %param.14) | copy-start | bytes 2654212
  0.0 4.3 %collective-permute-start = (bf16[2,128,8,128]{3,2,1,0:T(8,128)(2,1)}, bf16[2,128,8,128]{3,2,1,0:T(8,128)(2,1)S(1)}, u32[]{:S(2)}, u32[]{:S(2)}) collective-permute-start(bf16[2,128,8,128]{3,2,1,0:T(8,128)(2,1)} %own_ref.1), channel_id=1, source_target_pairs={{0,1},{1,0},{2,3},{3,2},{4,5},{5,4},{6,7},{7,6},{8,9},{9,8},{10,11... | collective-permute-start | bytes 1572872 | tf_op jit(solution)/shard_map/ppermute | solution.py:291
  0.5 1.1 %copy-start.7 = (bf16[2,128,8,128]{3,2,1,0:T(8,128)(2,1)S(1)}, bf16[2,128,8,128]{3,2,1,0:T(8,128)(2,1)}, u32[]{:S(2)}) copy-start(bf16[2,128,8,128]{3,2,1,0:T(8,128)(2,1)} %own_ref.1) | copy-start | bytes 1572868
  1.6 7.3 %collective-permute-start.1 = (bf16[2,66,8,128]{3,2,1,0:T(8,128)(2,1)S(1)}, bf16[2,66,8,128]{3,2,1,0:T(8,128)(2,1)S(1)}, u32[]{:S(2)}, u32[]{:S(2)}) collective-permute-start(bf16[2,66,8,128]{3,2,1,0:T(8,128)(2,1)S(1)} %get-tuple-element.22.cut0_ref), channel_id=1, source_target_pairs={{0,16},{15,31},{1,2},{2,1},{3,4},{4,3},{5,6},{6,5},{7,8},{8,7},{9,... | collective-permute-start | bytes 811016 | tf_op jit(solution)/shard_map/ppermute | solution.py:368
  4.3 4.7 %copy-start.8 = (bf16[128,128]{1,0:T(8,128)(2,1)S(1)}, bf16[128,128]{1,0:T(8,128)(2,1)}, u32[]{:S(2)}) copy-start(bf16[128,128]{1,0:T(8,128)(2,1)} %refs_5_.3) | copy-start | bytes 98308
  4.3 4.7 %copy-start.9 = (bf16[128,128]{1,0:T(8,128)(2,1)S(1)}, bf16[128,128]{1,0:T(8,128)(2,1)}, u32[]{:S(2)}) copy-start(bf16[128,128]{1,0:T(8,128)(2,1)} %refs_6_.3) | copy-start | bytes 98308
  4.3 4.7 %copy-start.10 = (f32[2,128,8]{1,2,0:T(8,128)S(1)}, f32[2,128,8]{1,2,0:T(8,128)}, u32[]{:S(2)}) copy-start(f32[2,128,8]{1,2,0:T(8,128)} %param.12) | copy-start | bytes 24580
  11.2 3.3 %collective-permute-start.3 = (bf16[96,8,128]{2,1,0:T(8,128)(2,1)S(1)}, bf16[96,8,128]{2,1,0:T(8,128)(2,1)S(1)}, u32[]{:S(2)}, u32[]{:S(2)}) collective-permute-start(bf16[96,8,128]{2,1,0:T(8,128)(2,1)S(1)} %get-tuple-element.28), channel_id=1, source_target_pairs={{0,1},{1,0},{2,3},{3,2},{4,5},{5,4},{6,7},{7,6},{8,9},{9,8},{10,11... | collective-permute-start | bytes 589832 | tf_op jit(solution)/shard_map/ppermute | solution.py:291
  13.0 6.5 %collective-permute-start.2 = (bf16[2,66,8,128]{3,2,1,0:T(8,128)(2,1)S(1)}, bf16[2,66,8,128]{3,2,1,0:T(8,128)(2,1)S(1)}, u32[]{:S(2)}, u32[]{:S(2)}) collective-permute-start(bf16[2,66,8,128]{3,2,1,0:T(8,128)(2,1)S(1)} %get-tuple-element.23.cut1_ref), channel_id=1, source_target_pairs={{0,16},{15,31},{1,2},{2,1},{3,4},{4,3},{5,6},{6,5},{7,8},{8,7},{9,... | collective-permute-start | bytes 811016 | tf_op jit(solution)/shard_map/ppermute | solution.py:369
  21.8 10.4 %collective-permute-start.4 = (bf16[98,8,128]{2,1,0:T(8,128)(2,1)S(1)}, bf16[98,8,128]{2,1,0:T(8,128)(2,1)S(1)}, u32[]{:S(2)}, u32[]{:S(2)}) collective-permute-start(bf16[98,8,128]{2,1,0:T(8,128)(2,1)S(1)} %get-tuple-element.33), channel_id=1, source_target_pairs={{0,1},{1,0},{2,3},{3,2},{4,5},{5,4},{6,7},{7,6},{8,9},{9,8},{10,11... | collective-permute-start | bytes 602120 | tf_op jit(solution)/shard_map/ppermute | solution.py:291
  24.3 7.9 %collective-permute-start.5 = (bf16[96,8,128]{2,1,0:T(8,128)(2,1)S(1)}, bf16[96,8,128]{2,1,0:T(8,128)(2,1)S(1)}, u32[]{:S(2)}, u32[]{:S(2)}) collective-permute-start(bf16[96,8,128]{2,1,0:T(8,128)(2,1)S(1)} %pad_maximum_fusion.1), channel_id=1, source_target_pairs={{0,2},{1,3},{2,0},{3,1},{4,6},{5,7},{6,4},{7,5},{8,10},{9,11},{10,... | collective-permute-start | bytes 589832 | tf_op jit(solution)/shard_map/ppermute | solution.py:291
  32.4 4.7 %collective-permute-start.6 = (bf16[49,8,128]{2,1,0:T(8,128)(2,1)S(1)}, bf16[49,8,128]{2,1,0:T(8,128)(2,1)S(1)}, u32[]{:S(2)}, u32[]{:S(2)}) collective-permute-start(bf16[49,8,128]{2,1,0:T(8,128)(2,1)S(1)} %pad_maximum_fusion.3), channel_id=1, source_target_pairs={{0,4},{1,5},{2,6},{3,7},{4,0},{5,1},{6,2},{7,3},{8,12},{9,13},{10,... | collective-permute-start | bytes 301064 | tf_op jit(solution)/shard_map/ppermute | solution.py:291
  37.2 15.5 %copy-start = (bf16[9,128,128]{2,1,0:T(8,128)(2,1)S(1)}, bf16[9,128,128]{2,1,0:T(8,128)(2,1)}, u32[]{:S(2)}) copy-start(bf16[9,128,128]{2,1,0:T(8,128)(2,1)} %param.17) | copy-start | bytes 884740
  37.2 15.5 %copy-start.1 = (bf16[9,128,128]{2,1,0:T(8,128)(2,1)S(1)}, bf16[9,128,128]{2,1,0:T(8,128)(2,1)}, u32[]{:S(2)}) copy-start(bf16[9,128,128]{2,1,0:T(8,128)(2,1)} %param.18) | copy-start | bytes 884740
  37.2 15.5 %copy-start.2 = (bf16[128,512]{1,0:T(8,128)(2,1)S(1)}, bf16[128,512]{1,0:T(8,128)(2,1)}, u32[]{:S(2)}) copy-start(bf16[128,512]{1,0:T(8,128)(2,1)} %in_ref.1) | copy-start | bytes 393220
  37.2 15.5 %copy-start.3 = (bf16[512,128]{1,0:T(8,128)(2,1)S(1)}, bf16[512,128]{1,0:T(8,128)(2,1)}, u32[]{:S(2)}) copy-start(bf16[512,128]{1,0:T(8,128)(2,1)} %out_w_ref.1) | copy-start | bytes 393220
  37.2 15.5 %copy-start.4 = (f32[128]{0:T(128)S(1)}, f32[128]{0:T(128)}, u32[]{:S(2)}) copy-start(f32[128]{0:T(128)} %param.19) | copy-start | bytes 1540
  37.3 5.6 %collective-permute-start.7 = (bf16[49,8,128]{2,1,0:T(8,128)(2,1)S(1)}, bf16[49,8,128]{2,1,0:T(8,128)(2,1)S(1)}, u32[]{:S(2)}, u32[]{:S(2)}) collective-permute-start(bf16[49,8,128]{2,1,0:T(8,128)(2,1)S(1)} %pad_maximum_fusion.4), channel_id=1, source_target_pairs={{0,8},{1,9},{2,10},{3,11},{4,12},{5,13},{6,14},{7,15},{8,0},{9,1},... | collective-permute-start | bytes 301064 | tf_op jit(solution)/shard_map/ppermute | solution.py:291
  43.0 4.0 %collective-permute-start.8 = (bf16[16,8,128]{2,1,0:T(8,128)(2,1)S(1)}, bf16[16,8,128]{2,1,0:T(8,128)(2,1)S(1)}, u32[]{:S(2)}, u32[]{:S(2)}) collective-permute-start(bf16[16,8,128]{2,1,0:T(8,128)(2,1)S(1)} %divide_convert_fusion), channel_id=1, source_target_pairs={{0,4},{1,5},{2,6},{3,7},{4,0},{5,1},{6,2},{7,3},{8,12},{9,13},{10,... | collective-permute-start | bytes 98312 | tf_op jit(solution)/shard_map/ppermute | solution.py:291
  47.0 4.3 %collective-permute-start.9 = (bf16[33,8,128]{2,1,0:T(8,128)(2,1)S(1)}, bf16[33,8,128]{2,1,0:T(8,128)(2,1)S(1)}, u32[]{:S(2)}, u32[]{:S(2)}) collective-permute-start(bf16[33,8,128]{2,1,0:T(8,128)(2,1)S(1)} %pad_maximum_fusion.5), channel_id=1, source_target_pairs={{0,2},{1,3},{2,0},{3,1},{4,6},{5,7},{6,4},{7,5},{8,10},{9,11},{10,... | collective-permute-start | bytes 202760 | tf_op jit(solution)/shard_map/ppermute | solution.py:291
  51.3 1.4 %collective-permute-start.10 = (bf16[64,8,128]{2,1,0:T(8,128)(2,1)S(1)}, bf16[64,8,128]{2,1,0:T(8,128)(2,1)S(1)}, u32[]{:S(2)}, u32[]{:S(2)}) collective-permute-start(bf16[64,8,128]{2,1,0:T(8,128)(2,1)S(1)} %pad_maximum_fusion.2), channel_id=1, source_target_pairs={{0,1},{1,0},{2,3},{3,2},{4,5},{5,4},{6,7},{7,6},{8,9},{9,8},{10,11... | collective-permute-start | bytes 393224 | tf_op jit(solution)/shard_map/ppermute | solution.py:291

commit v5 on v4

v5 whole, which is shorter than its diff:
```python
import functools

import jax
import jax.numpy as jnp
from jax import lax
from jax.experimental import pallas as pl
from jax.experimental.pallas import tpu as pltpu
from jax.sharding import PartitionSpec as P

BF = jnp.bfloat16
F32 = jnp.float32
PAIR = ({0: 0, 1: 1, 2: 2}, {1: 0, 2: 1, 3: 2})
LOWER = ({0: 0, 1: 1}, {1: 0})
UPPER = ({2: 2}, {2: 1, 3: 2})


SLOPE = 0.7978845608028654
BEND = SLOPE * 0.044715


def twice_activate(values):
    return values + values * jnp.tanh(values * (SLOPE + BEND * (values * values)))


def activate(values):
    return 0.5 * twice_activate(values)


def beside(blocks):
    return jnp.concatenate(blocks, axis=1)


def shift_depth(before, same, after, shape):
    depth = shape[1]
    place = lax.broadcasted_iota(jnp.int32, shape, 1)
    before = jnp.where(place == 0, 0.0, pltpu.roll(before.reshape(shape), 1, 1))
    after = jnp.where(place == depth - 1, 0.0, pltpu.roll(after.reshape(shape), depth - 1, 1))
    return before + same.reshape(shape) + after


def conv_rows(window, w_ref, taps, shape, uses):
    channels = shape[-1]
    zero = jnp.zeros((channels, channels), BF)
    windows = {r: [window(r, b) for b in range(3)] for r in sorted(set(uses[0]) | set(uses[1]))}

    def weight(out, row, b, c):
        return w_ref[taps[uses[out][row]], 3 * b + c] if row in uses[out] else zero

    def product(left, right):
        rows = sorted(set(uses[left[0]]) | set(uses[right[0]]))
        lhs = beside([windows[r][b] for r in rows for b in range(3)])
        rhs = jnp.concatenate(
            [
                beside([weight(left[0], r, b, left[1]), weight(right[0], r, b, right[1])])
                for r in rows
                for b in range(3)
            ],
            axis=0,
        )
        total = jnp.dot(lhs, rhs, preferred_element_type=F32)
        return total[:, :channels], total[:, channels:]

    low0, low1 = product((0, 0), (0, 1))
    low2, high0 = product((0, 2), (1, 0))
    high1, high2 = product((1, 1), (1, 2))
    return shift_depth(low0, low1, low2, shape), shift_depth(high0, high1, high2, shape)


def clear_ends(rows_ref, width):
    rows, length, depth, channels = rows_ref.shape
    blank = jnp.zeros((width, depth, channels), rows_ref.dtype)
    for row in range(rows):
        rows_ref[row, :width] = blank
        rows_ref[row, length - width :] = blank


def bit_of(index, bit):
    return lax.rem(index // (1 << bit), 2)


def pieces_of(index, second):
    flip = 0 if second else 1
    return [2 * jnp.bitwise_xor(bit_of(index, 1 + k), flip) + k for k in range(2)]


def clamp(start, across, length):
    return jnp.clip(start, 0, across - length)


def cut_kernel(axis, own_ref, early_ref, late_ref, sems):
    across = own_ref.shape[1]
    quarter, length = across // 4, early_ref.shape[2]
    devices = lax.axis_size(axis)
    index = lax.axis_index(axis)
    taker = lax.rem(index + 2 * lax.rem(index, 2) - 1 + devices, devices)
    fetches = []
    for k, target in enumerate((early_ref, late_ref)):
        for p, piece in enumerate(pieces_of(taker, k == 1)):
            place = pl.ds(clamp(piece * quarter - 2, across, length), length)
            fetches.append(
                pltpu.make_async_copy(own_ref.at[:, place], target.at[:, p], sems.at[k, p])
            )
    for fetch in fetches:
        fetch.start()
    for fetch in fetches:
        fetch.wait()


def first_kernel(axis, own_ref, near_ref, w1_ref, w2_ref, edge_ref, part_ref, rows_ref, mid_ref):
    across, depth, channels = own_ref.shape[1:]
    span = across // 2
    shape = (span, depth, channels)
    side = lax.rem(lax.axis_index(axis), 2)
    clear_ends(rows_ref, 1)
    clear_ends(mid_ref, 1)
    clear_ends(edge_ref, 1)
    for row, at in enumerate((side, 1 - side)):
        rows_ref[row, 1 : across + 1] = own_ref[at]
        rows_ref[2 + row, 1 : across + 1] = near_ref[at]
    taps = (2 * side, 1, 2 - 2 * side)
    back = (2 - 2 * side, 1, 2 * side)

    def windows(ref, names, start):
        def window(r, b):
            return ref[names[r], start + b : start + b + span].reshape(-1, channels)

        return window

    for step in range(2):
        start = step * span
        inner = slice(1 + start, 1 + start + span)
        low, high = conv_rows(windows(rows_ref, range(4), start), w1_ref, taps, shape, PAIR)
        mid_ref[0, inner] = activate(low).astype(BF)
        mid_ref[1, inner] = activate(high).astype(BF)
        low, high = conv_rows(windows(rows_ref, (1, 0), start), w1_ref, back, shape, LOWER)
        edge_ref[0, inner] = low
        edge_ref[1, inner] = high
    for step in range(2):
        start = step * span
        outs = conv_rows(windows(mid_ref, {2: 0, 3: 1}, start), w2_ref, taps, shape, UPPER)
        for u in range(2):
            own = rows_ref[u, 1 + start : 1 + start + span].astype(F32)
            part_ref[u, start : start + span] = outs[u] + own


def half_kernel(axis, second, *refs):
    edge_ref, part_ref, far_ref, w1_ref, w2_ref, x_ref, y_ref, prior_ref = refs[:8]
    if second:
        early_ref, feature_ref, message_ref, keep_ref, strip_ref, rows_ref, mid_ref = refs[8:]
    else:
        feature_ref, message_ref, keep_ref, rows_ref, mid_ref = refs[8:]
    across, depth, channels = part_ref.shape[1:]
    quarter, length = across // 4, far_ref.shape[2]
    span = 2 * quarter
    devices = lax.axis_size(axis)
    index = lax.axis_index(axis)
    side = lax.rem(index, 2)
    pieces = pieces_of(index, second)
    border = jnp.logical_or(index == 0, index == devices - 1)
    inside = jnp.where(border, 0.0, 1.0)
    blank = jnp.zeros((4, depth, channels), BF)
    absent = jnp.zeros((length, depth, channels), BF)
    for p, piece in enumerate(pieces):
        start = piece * quarter - 2
        place = pl.ds(2 + clamp(start, across, length) - start, length)
        for row, at in enumerate((1 - side, side)):
            rows_ref[row, p, :4] = blank
            rows_ref[row, p, length:] = blank
            rows_ref[row, p, place] = jnp.where(border, absent, far_ref[at, p])

    def windows(ref, names, start, rows):
        def window(r, b):
            return jnp.concatenate(
                [ref[names[r], p, start + b : start + b + rows].reshape(-1, channels) for p in range(2)]
            )

        return window

    around = quarter + 2
    back = (2 - 2 * side, 1, 2 * side)
    far_rows = windows(rows_ref, {2: 0, 3: 1}, 2, around)
    low, high = conv_rows(far_rows, w1_ref, back, (2 * around, depth, channels), UPPER)
    for p, piece in enumerate(pieces):
        cut = slice(p * around, (p + 1) * around)
        place = pl.ds(piece * quarter, around)
        mid_ref[1, p] = activate(low[cut] + edge_ref[0, place]).astype(BF)
        mid_ref[0, p] = (activate(high[cut] + edge_ref[1, place]) * inside).astype(BF)
        outside = 0 if p == 0 else around - 1

        @pl.when(piece == 3 * p)
        def _():
            mid_ref[0, p, outside] = blank[0]
            mid_ref[1, p, outside] = blank[0]

    taps = (2 * side, 1, 2 - 2 * side)
    mid_rows = windows(mid_ref, range(2), 0, quarter)
    outs = conv_rows(mid_rows, w2_ref, taps, (span, depth, channels), LOWER)
    across_score, along_score = x_ref[...], y_ref[...]

    def prior_of(at, pieces):
        table = prior_ref[at]
        columns = []
        for p, piece in enumerate(pieces):
            low, high = (table[:, k * quarter : (k + 1) * quarter] for k in (p, 2 + p))
            both = jnp.where(piece == p, low, high)
            columns += [
                jnp.broadcast_to(both[:, y : y + 1], (depth, channels)) for y in range(quarter)
            ]
        return jnp.stack(columns)

    logits, features = [], []
    for u in range(2):
        at = side if u == 0 else 1 - side
        part = jnp.concatenate([part_ref[u, pl.ds(piece * quarter, quarter)] for piece in pieces])
        feature = (outs[u] + part).astype(BF)
        feature_ref[at] = feature
        prior = prior_of(at, pieces)
        if not second:
            logit = jnp.dot(feature.reshape(-1, channels), across_score, preferred_element_type=F32)
        else:
            score = beside([across_score, along_score])
            both = jnp.dot(feature.reshape(-1, channels), score, preferred_element_type=F32)
            logit = both[:, :channels]
            logit_y = both[:, channels:].reshape(span, depth, channels) + prior
            other = early_ref[at]
            other_y = jnp.dot(other.reshape(-1, channels), along_score, preferred_element_type=F32)
            other_y = other_y.reshape(span, depth, channels) + prior_of(at, pieces_of(index, False))
            top = jnp.maximum(jnp.max(logit_y, axis=0), jnp.max(other_y, axis=0))
            weights, others = jnp.exp(logit_y - top), jnp.exp(other_y - top)
            norm_sum = jnp.sum(weights, axis=0) + jnp.sum(others, axis=0)
            weighted = jnp.sum(weights * feature.astype(F32), axis=0)
            weighted = weighted + jnp.sum(others * other.astype(F32), axis=0)
            pooled = (weighted / norm_sum).astype(BF)
            strip_ref[u] = pooled
            message_ref[3 * quarter + 1 - u] = pooled
        features.append(feature.astype(F32))
        logits.append(logit.reshape(span, depth, channels) + prior)
    peak = jnp.maximum(logits[0], logits[1])
    coarse = peak.astype(BF)
    shift = jnp.exp(jnp.clip(peak - coarse.astype(F32), -60.0, 60.0))
    low, high = jnp.exp(logits[0] - peak) * shift, jnp.exp(logits[1] - peak) * shift
    parts = (coarse.astype(F32), low + high, low * features[0] + high * features[1])
    for p in range(2):
        cut = slice(p * quarter, (p + 1) * quarter)

        @pl.when(side == p)
        def _():
            for k, part in enumerate(parts):
                keep_ref[k] = part[cut]

        @pl.when(side != p)
        def _():
            for k, part in enumerate(parts):
                message_ref[k * quarter : (k + 1) * quarter] = part[cut].astype(BF)


def last_kernel(
    axis,
    early_ref,
    late_ref,
    pooled_ref,
    strip_ref,
    yz_ref,
    xz_ref,
    gain_ref,
    in_ref,
    out_w_ref,
    out_hbm,
    plane_ref,
    mix_ref,
    out_ref,
    sems,
):
    rows, span, depth, channels = early_ref.shape
    across, quarter = 2 * span, span // 2
    index = lax.axis_index(axis)
    side = lax.rem(index, 2)
    bits = lax.axis_size(axis).bit_length() - 2
    block = across >> bits
    blank = jnp.zeros((depth, channels), BF)
    plane_ref[0] = blank
    plane_ref[across + 1] = blank
    for k in range(1 << bits):
        flips = [(k >> (bits - 1 - b)) % 2 for b in range(bits)]
        core = jnp.bitwise_xor(side, flips[0])
        ahead = jnp.where(core == 0, bit_of(index, 1), bit_of(index, 2))
        after = jnp.where(core == 0, bit_of(index, 2), bit_of(index, 1))
        place = 2 * jnp.bitwise_xor(ahead, flips[1]) + core
        place = 2 * place + jnp.bitwise_xor(after, flips[2])
        for b in range(3, bits):
            place = 2 * place + jnp.bitwise_xor(bit_of(index, b), flips[b])
        plane_ref[pl.ds(1 + place * block, block)] = pooled_ref[k * block : (k + 1) * block]

    def plane_product(windows, weights, shape):
        lhs = beside(windows)
        rhs = jnp.concatenate([beside(w) for w in weights], axis=0)
        total = jnp.dot(lhs, rhs, preferred_element_type=F32)
        parts = [total[:, c * channels : (c + 1) * channels] for c in range(3)]
        return shift_depth(*parts, shape).astype(BF).astype(F32)

    taps = (2 * side, 1, 2 - 2 * side)
    strip = strip_ref[...]
    mixed = plane_product(
        [strip[a : a + rows].reshape(-1, channels) for a in range(3)],
        [[xz_ref[taps[a], c] for c in range(3)] for a in range(3)],
        (rows, depth, channels),
    )
    mix_ref[side] = mixed[0]
    mix_ref[1 - side] = mixed[1]
    gain = gain_ref[...]
    copies = []
    for step, feature_ref in enumerate((early_ref, late_ref)):
        starts = [piece * quarter for piece in pieces_of(index, step == 1)]
        plane = plane_product(
            [
                jnp.concatenate(
                    [plane_ref[pl.ds(at + b, quarter)].reshape(-1, channels) for at in starts]
                )
                for b in range(3)
            ],
            [[yz_ref[b, c] for c in range(3)] for b in range(3)],
            (span, depth, channels),
        )
        mixing = plane[None] + jnp.stack([mix_ref[row] for row in range(rows)])[:, None]
        joined = (feature_ref[...].astype(F32) * mixing).reshape(-1, channels)
        mean = jnp.mean(joined * joined, axis=-1, keepdims=True)
        normed = (joined * lax.rsqrt(mean + 1e-06) * gain).astype(BF)
        hidden = jnp.dot(normed, in_ref[...], preferred_element_type=F32)
        hidden = twice_activate(hidden).astype(BF)
        update = 0.5 * jnp.dot(hidden, out_w_ref[...], preferred_element_type=F32)
        encoded = (joined + update).astype(BF).reshape(rows, 2, quarter, depth, channels)
        for row in range(rows):
            for p, at in enumerate(starts):
                slot = 2 * step + p
                out_ref[row, slot] = encoded[row, p]
                copies.append(
                    pltpu.make_async_copy(
                        out_ref.at[row, slot],
                        out_hbm.at[row, pl.ds(at, quarter)],
                        sems.at[row, slot],
                    )
                )
                copies[-1].start()
    for copy in copies:
        copy.wait()


def swap(values, axis, mask, odd_mask=None):
    masks = (mask, mask if odd_mask is None else odd_mask)
    devices = lax.axis_size(axis)
    return lax.ppermute(values, axis, [(i, i ^ masks[i % 2]) for i in range(devices)])


def merge(own, other):
    peak, other_peak = own[0], other[0].astype(F32)
    top = jnp.maximum(peak, other_peak)
    scale = jnp.exp(peak - top)
    other_scale = jnp.exp(other_peak - top)
    return [
        top,
        own[1] * scale + other[1].astype(F32) * other_scale,
        own[2] * scale + other[2].astype(F32) * other_scale,
    ]


def thirds(message):
    size = message.shape[0] // 3
    return [message[k * size : (k + 1) * size] for k in range(3)]


def kernel_call(body, outs, scratch, flops, *operands, spaces=None, results=pltpu.VMEM):
    moved = sum(o.size * o.dtype.itemsize for o in operands)
    return pl.pallas_call(
        body,
        out_shape=outs,
        in_specs=[pl.BlockSpec(memory_space=m) for m in spaces or [pltpu.VMEM] * len(operands)],
        out_specs=jax.tree.map(lambda _: pl.BlockSpec(memory_space=results), outs),
        scratch_shapes=scratch,
        compiler_params=pltpu.CompilerParams(vmem_limit_bytes=14 * 1024 * 1024),
        cost_estimate=pl.CostEstimate(flops=flops, bytes_accessed=moved, transcendentals=0),
    )(*operands)


def on_device(
    others,
    axis,
    voxels,
    prior,
    conv_first,
    conv_second,
    score_x,
    score_y,
    plane_yz_w,
    plane_xz_w,
    norm_gain,
    mlp_in,
    mlp_out,
):
    rows, across, depth, channels = voxels.shape
    devices = lax.axis_size(axis)
    if rows != 2 or devices & (devices - 1) or devices < 16 or across % 8:
        raise ValueError("unsupported mesh")
    index = lax.axis_index(axis)
    half, quarter = across // 2, across // 4
    w_first = conv_first.reshape(3, 9, channels, channels)
    w_second = conv_second.reshape(3, 9, channels, channels)
    flops = 2 * voxels.size * channels * 27

    def beyond_edge(at):
        return at + 2 * (at % 2) - 1

    parts = lax.axis_size(others)
    pairs = []
    for base in range(0, parts * devices, devices):
        twin = base ^ devices if (base ^ devices) < parts * devices else base
        pairs += [(base, twin), (base + devices - 1, twin + devices - 1)]
        for i in range(base + 1, base + devices - 1, 2):
            pairs += [(i, i + 1), (i + 1, i)]
    cut = jax.ShapeDtypeStruct((rows, 2, quarter + 4, depth, channels), BF)
    cuts = kernel_call(
        functools.partial(cut_kernel, axis),
        (cut, cut),
        [pltpu.SemaphoreType.DMA((2, 2))],
        flops,
        voxels,
        spaces=(pltpu.HBM,),
    )
    far0 = lax.ppermute(cuts[0], (others, axis), pairs)
    far1 = lax.ppermute(cuts[1], (others, axis), pairs)
    near = swap(voxels, axis, 1)
    prior = prior.swapaxes(1, 2)
    edge, part = kernel_call(
        functools.partial(first_kernel, axis),
        (
            jax.ShapeDtypeStruct((rows, across + 2, depth, channels), F32),
            jax.ShapeDtypeStruct(voxels.shape, F32),
        ),
        [
            pltpu.VMEM((4, across + 2, depth, channels), BF),
            pltpu.VMEM((2, across + 2, depth, channels), BF),
        ],
        2 * flops,
        voxels,
        near,
        w_first,
        w_second,
    )

    def half_call(second, far, *state):
        feature = jax.ShapeDtypeStruct((rows, half, depth, channels), BF)
        message = jax.ShapeDtypeStruct((3 * quarter + 2 * second, depth, channels), BF)
        keep = jax.ShapeDtypeStruct((3, quarter, depth, channels), F32)
        strip = (jax.ShapeDtypeStruct((rows, depth, channels), BF),) if second else ()
        return kernel_call(
            functools.partial(half_kernel, axis, second),
            (feature, message, keep) + strip,
            [
                pltpu.VMEM((2, 2, quarter + 8, depth, channels), BF),
                pltpu.VMEM((2, 2, quarter + 2, depth, channels), BF),
            ],
            3 * flops // 4,
            edge,
            part,
            far,
            w_first,
            w_second,
            score_x,
            score_y,
            prior,
            *state,
        )

    masks = [1 << bit for bit in range(devices.bit_length() - 1)]
    early, message, keep = half_call(False, far0)
    got = swap(message, axis, masks[0])
    sent = jnp.concatenate([p.astype(BF) for p in merge(keep, thirds(got))])
    sent, early_first = lax.optimization_barrier((sent, early))
    arriving = swap(sent, axis, masks[1], masks[2])
    late, message, keep, strip = half_call(True, far1, early_first)
    got = swap(message, axis, masks[0])
    beyond = got[3 * quarter]
    carried = [got[3 * quarter + 1]]
    parts = merge(merge(keep, thirds(got[: 3 * quarter])), thirds(arriving))
    side = index % 2
    ahead, after = jnp.where(side == 0, 2, 4), jnp.where(side == 0, 4, 2)
    for mask in masks[2:]:
        if mask != masks[-1]:
            size = parts[0].shape[0] // 2
            upper = (index // (after if mask == masks[2] else mask)) % 2
            sent = [lax.dynamic_slice_in_dim(p, (1 - upper) * size, size, 0) for p in parts]
            parts = [lax.dynamic_slice_in_dim(p, upper * size, size, 0) for p in parts]
        else:
            sent = parts
        message = jnp.concatenate([p.astype(BF) for p in sent] + [carried[-1][None]], axis=0)
        got = swap(message, axis, mask, masks[1] if mask == masks[2] else mask)
        carried.append(got[-1])
        last_row = carried[-1]
        parts = merge(parts, thirds(got[:-1]))
        parts[0], carried[-1] = lax.optimization_barrier((parts[0], last_row))
    pooled = (parts[2] / parts[1]).astype(BF)
    for mask in reversed(masks[2:-1]):
        other = swap(pooled, axis, mask, masks[1] if mask == masks[2] else mask)
        pooled = jnp.concatenate([pooled, other], axis=0)
    other = index ^ ahead
    path = other ^ beyond_edge(other)
    row = carried[0]
    for k, value in enumerate(carried[1:]):
        row = jnp.where(path == (1 << (k + 3)) - 1, value, row)
    got = swap(jnp.concatenate([pooled, row[None]], axis=0), axis, masks[1], masks[2])
    direct = (side == 1) & (index ^ beyond_edge(index) == 3)
    before = jnp.where(direct, carried[1], got[-1])
    before = jnp.where((index == 0) | (index == devices - 1), jnp.zeros_like(row), before)
    pooled = jnp.concatenate([pooled, got[:-1]], axis=0)
    pooled = jnp.concatenate([pooled, swap(pooled, axis, masks[0])], axis=0)
    strip = jnp.concatenate([before[None], strip, beyond[None]], axis=0)
    return kernel_call(
        functools.partial(last_kernel, axis),
        jax.ShapeDtypeStruct(voxels.shape, BF),
        [
            pltpu.VMEM((across + 2, depth, channels), BF),
            pltpu.VMEM((rows, depth, channels), F32),
            pltpu.VMEM((rows, 4, quarter, depth, channels), BF),
            pltpu.SemaphoreType.DMA((rows, 4)),
        ],
        flops // 4,
        early,
        late,
        pooled,
        strip,
        plane_yz_w.reshape(3, 3, channels, channels),
        plane_xz_w.reshape(3, 3, channels, channels),
        norm_gain.reshape(1, channels),
        mlp_in,
        mlp_out,
        results=pl.ANY,
    )


def solution(mesh):
    spread = ("scene", "gx")
    return jax.shard_map(
        functools.partial(on_device, "scene", "gx"),
        mesh=mesh,
        in_specs=(P(spread, None, None, None), P(spread, None, None)) + (P(),) * 9,
        out_specs=P(spread, None, None, None),
        check_vma=False,
    )
```

time: 57.3 us -> 56.8 us (level)
  waiting for transfers between devices: 21.7 us -> 20.1 us
  starting transfers between devices: 19.9 us -> 21.4 us
    ppermute x9, waiting for transfers between devices: 16.9 us -> 14.9 us  [swap(): lax.ppermute(values, axis, [(i, i ^ masks[i % 2]) for i in range(devices)])]
    ppermute x9, starting transfers between devices: 15.8 us -> 17.2 us  [swap(): lax.ppermute(values, axis, [(i, i ^ masks[i % 2]) for i in range(devices)])]
  transfers between devices with their start and end apart: 11 -> 11, of which waited for: 7 -> 7; matrix products, arithmetic and copies ran while one was open for 0% -> 0% of each run, Pallas kernels for 8% -> 9%
where the time goes in v5:
time: 56.8 us; the launch traced here: 56.6 us
  starting transfers between devices  21.4 us (38%)
  waiting for transfers between devices  20.1 us (35%)
  Pallas kernels  13.1 us (23%)
  local copies, waits for them, and re-layouts  1.18 us (2%)
    ppermute x9, starting transfers between devices, swap(): lax.ppermute(values, axis, [(i, i ^ masks[i % 2]) for i in range(devices)])  17.2 us
    ppermute x9, waiting for transfers between devices, swap(): lax.ppermute(values, axis, [(i, i ^ masks[i % 2]) for i in range(devices)])  14.9 us
    pallas_call x5, Pallas kernels, kernel_call(): pl.pallas_call(body, out_shape=outs, in_specs=[pl.BlockSpec(memory_space=...  13.1 us
    ppermute x1, waiting for transfers between devices, on_device(): far1 = lax.ppermute(cuts[1], (others, axis), pairs)  5.08 us
    ppermute x1, starting transfers between devices, on_device(): far0 = lax.ppermute(cuts[0], (others, axis), pairs)  2.64 us
    ppermute x1, starting transfers between devices, on_device(): far1 = lax.ppermute(cuts[1], (others, axis), pairs)  1.48 us
  transfers between devices with their start and end apart: 11, of which 7 were waited for; matrix products, arithmetic and copies ran while one was open for 0% of the time, Pallas kernels for 9%

profile of v5, /device:TPU:0, one launch (start us, length us, event | category | flops | bytes accessed | tf_op | source)
XLA Modules:
  0.0 56.6 jit_solution(12115159433142243035)
XLA Ops:
  0.0 0.5 collective-permute-start
  0.5 1.1 %copy-done.7 = bf16[2,128,8,128]{3,2,1,0:T(8,128)(2,1)S(1)} copy-done((bf16[2,128,8,128]{3,2,1,0:T(8,128)(2,1)S(1)}, bf16[2,128,8,128]{3,2,1,0:T(8,128)(2,1)}, u32[]{:S(2)}) %copy-start.7) | copy-done | bytes 524312
  1.6 0.4 shard_map.110
  2.0 2.6 %collective-permute-start.1 = (bf16[2,2,36,8,128]{4,3,2,1,0:T(8,128)(2,1)S(1)}, bf16[2,2,36,8,128]{4,3,2,1,0:T(8,128)(2,1)S(1)}, u32[]{:S(2)}, u32[]{:S(2)}) collective-permute-start(bf16[2,2,36,8,128]{4,3,2,1,0:T(8,128)(2,1)S(1)} %get-tuple-element.23), channel_id=1, source_target_pairs={{0,16},{15,31},{1,2},{2,1},{3,4},{4,3},{5,6},{6,5},{7,8},{8,7},{9,... | collective-permute-start | bytes 884744 | tf_op jit(solution)/shard_map/ppermute | solution.py:428
  4.6 0.0 copy-start.8
  4.7 0.0 copy-start.9
  4.7 4.6 %shard_map.109 = (f32[2,130,8,128]{3,2,1,0:T(8,128)S(1)}, f32[2,128,8,128]{3,2,1,0:T(8,128)S(1)}) custom-call(bf16[2,128,8,128]{3,2,1,0:T(8,128)(2,1)S(1)} %copy-done.7, bf16[2,128,8,128]{3,2,1,0:T(8,128)(2,1)S(1)} %collective-permute-done.near_ref, bf16[3,9,128,128]{3,2,1,0:T(8,128)(2,1)S(1)} %bitcast.89, bf16[3,9,128,128]{3,2,1,0:T(8,128)(2,1)S(1)} %bitcast.92), custom_call_target="tpu_custom_call" | custom-call | flops 3623878656 | bytes 2818048 | tf_op jit(solution)/shard_map/pallas_call | solution.py:373
  9.3 0.0 collective-permute-done.1.refs_2_
  9.3 2.2 %shard_map.111 = (bf16[2,64,8,128]{3,2,1,0:T(8,128)(2,1)S(1)}, bf16[96,8,128]{2,1,0:T(8,128)(2,1)S(1)}, f32[3,32,8,128]{3,2,1,0:T(8,128)S(1)}) custom-call(f32[2,130,8,128]{3,2,1,0:T(8,128)S(1)} %get-tuple-element.21.refs_0_, f32[2,128,8,128]{3,2,1,0:T(8,128)S(1)} %get-tuple-element.22.refs_1_, ...), custom_call_target="tpu_custom_call" | custom-call | flops 1358954496 | bytes 4251648 | tf_op jit(solution)/shard_map/pallas_call | solution.py:373
  11.5 2.3 %collective-permute-start.3 = (bf16[96,8,128]{2,1,0:T(8,128)(2,1)S(1)}, bf16[96,8,128]{2,1,0:T(8,128)(2,1)S(1)}, u32[]{:S(2)}, u32[]{:S(2)}) collective-permute-start(bf16[96,8,128]{2,1,0:T(8,128)(2,1)S(1)} %get-tuple-element.27), channel_id=1, source_target_pairs={{0,1},{1,0},{2,3},{3,2},{4,5},{5,4},{6,7},{7,6},{8,9},{9,8},{10,11... | collective-permute-start | bytes 589832 | tf_op jit(solution)/shard_map/ppermute | solution.py:351
  13.8 1.5 %collective-permute-start.2 = (bf16[2,2,36,8,128]{4,3,2,1,0:T(8,128)(2,1)S(1)}, bf16[2,2,36,8,128]{4,3,2,1,0:T(8,128)(2,1)S(1)}, u32[]{:S(2)}, u32[]{:S(2)}) collective-permute-start(bf16[2,2,36,8,128]{4,3,2,1,0:T(8,128)(2,1)S(1)} %get-tuple-element.25), channel_id=1, source_target_pairs={{0,16},{15,31},{1,2},{2,1},{3,4},{4,3},{5,6},{6,5},{7,8},{8,7},{9,... | collective-permute-start | bytes 884744 | tf_op jit(solution)/shard_map/ppermute | solution.py:429
  15.3 0.1 fusion.16
  15.5 5.1 %collective-permute-done.2.refs_2_ = bf16[2,2,36,8,128]{4,3,2,1,0:T(8,128)(2,1)S(1)} collective-permute-done((bf16[2,2,36,8,128]{4,3,2,1,0:T(8,128)(2,1)S(1)}, bf16[2,2,36,8,128]{4,3,2,1,0:T(8,128)(2,1)S(1)}, u32[]{:S(2)}, u32[]{:S(2)}) %collective-permute-start.2) | collective-permute-done | bytes 294944 | tf_op jit(solution)/shard_map/ppermute | solution.py:429
  20.6 2.7 %shard_map.112 = (bf16[2,64,8,128]{3,2,1,0:T(8,128)(2,1)S(1)}, bf16[98,8,128]{2,1,0:T(8,128)(2,1)S(1)}, f32[3,32,8,128]{3,2,1,0:T(8,128)S(1)}, bf16[2,8,128]{2,1,0:T(8,128)(2,1)S(1)}) custom-call(f32[2,130,8,128]{3,2,1,0:T(8,128)S(1)} %get-tuple-element.21.refs_0_, f32[2,128,8,128]{3,2,1,0:T(8,128)S(1)} %get-tuple-element.22.refs_1_, ...), custom_call_target="tpu_custom_call" | custom-call | flops 1358954496 | bytes 4513792 | tf_op jit(solution)/shard_map/pallas_call | solution.py:373
  23.3 2.7 %collective-permute-start.4 = (bf16[98,8,128]{2,1,0:T(8,128)(2,1)S(1)}, bf16[98,8,128]{2,1,0:T(8,128)(2,1)S(1)}, u32[]{:S(2)}, u32[]{:S(2)}) collective-permute-start(bf16[98,8,128]{2,1,0:T(8,128)(2,1)S(1)} %get-tuple-element.31), channel_id=1, source_target_pairs={{0,1},{1,0},{2,3},{3,2},{4,5},{5,4},{6,7},{7,6},{8,9},{9,8},{10,11... | collective-permute-start | bytes 602120 | tf_op jit(solution)/shard_map/ppermute | solution.py:351
  26.0 2.4 %collective-permute-start.5 = (bf16[96,8,128]{2,1,0:T(8,128)(2,1)S(1)}, bf16[96,8,128]{2,1,0:T(8,128)(2,1)S(1)}, u32[]{:S(2)}, u32[]{:S(2)}) collective-permute-start(bf16[96,8,128]{2,1,0:T(8,128)(2,1)S(1)} %pad_maximum_fusion.1), channel_id=1, source_target_pairs={{0,2},{1,5},{2,0},{3,7},{4,6},{5,1},{6,4},{7,3},{8,10},{9,13},{10,... | collective-permute-start | bytes 589832 | tf_op jit(solution)/shard_map/ppermute | solution.py:351
  28.4 3.6 %collective-permute-done.5 = bf16[96,8,128]{2,1,0:T(8,128)(2,1)S(1)} collective-permute-done((bf16[96,8,128]{2,1,0:T(8,128)(2,1)S(1)}, bf16[96,8,128]{2,1,0:T(8,128)(2,1)S(1)}, u32[]{:S(2)}, u32[]{:S(2)}) %collective-permute-start.5) | collective-permute-done | bytes 196640 | tf_op jit(solution)/shard_map/ppermute | solution.py:351
  32.1 0.1 convert_maximum_fusion
  32.3 2.5 %collective-permute-start.6 = (bf16[49,8,128]{2,1,0:T(8,128)(2,1)S(1)}, bf16[49,8,128]{2,1,0:T(8,128)(2,1)S(1)}, u32[]{:S(2)}, u32[]{:S(2)}) collective-permute-start(bf16[49,8,128]{2,1,0:T(8,128)(2,1)S(1)} %pad_maximum_fusion.3), channel_id=1, source_target_pairs={{0,4},{1,3},{2,6},{3,1},{4,0},{5,7},{6,2},{7,5},{8,12},{9,11},{10,... | collective-permute-start | bytes 301064 | tf_op jit(solution)/shard_map/ppermute | solution.py:351
  34.8 2.6 %collective-permute-done.6 = bf16[49,8,128]{2,1,0:T(8,128)(2,1)S(1)} collective-permute-done((bf16[49,8,128]{2,1,0:T(8,128)(2,1)S(1)}, bf16[49,8,128]{2,1,0:T(8,128)(2,1)S(1)}, u32[]{:S(2)}, u32[]{:S(2)}) %collective-permute-start.6) | collective-permute-done | bytes 100384 | tf_op jit(solution)/shard_map/ppermute | solution.py:351
  37.5 0.0 copy-start.2
  37.5 0.0 copy-start.3
  37.6 3.1 %collective-permute-start.7 = (bf16[49,8,128]{2,1,0:T(8,128)(2,1)S(1)}, bf16[49,8,128]{2,1,0:T(8,128)(2,1)S(1)}, u32[]{:S(2)}, u32[]{:S(2)}) collective-permute-start(bf16[49,8,128]{2,1,0:T(8,128)(2,1)S(1)} %pad_maximum_fusion.4), channel_id=1, source_target_pairs={{0,8},{1,9},{2,10},{3,11},{4,12},{5,13},{6,14},{7,15},{8,0},{9,1},... | collective-permute-start | bytes 301064 | tf_op jit(solution)/shard_map/ppermute | solution.py:351
  40.7 2.6 %collective-permute-done.7 = bf16[49,8,128]{2,1,0:T(8,128)(2,1)S(1)} collective-permute-done((bf16[49,8,128]{2,1,0:T(8,128)(2,1)S(1)}, bf16[49,8,128]{2,1,0:T(8,128)(2,1)S(1)}, u32[]{:S(2)}, u32[]{:S(2)}) %collective-permute-start.7) | collective-permute-done | bytes 100384 | tf_op jit(solution)/shard_map/ppermute | solution.py:351
  43.3 0.1 divide_convert_fusion
  43.3 2.1 %collective-permute-start.8 = (bf16[16,8,128]{2,1,0:T(8,128)(2,1)S(1)}, bf16[16,8,128]{2,1,0:T(8,128)(2,1)S(1)}, u32[]{:S(2)}, u32[]{:S(2)}) collective-permute-start(bf16[16,8,128]{2,1,0:T(8,128)(2,1)S(1)} %divide_convert_fusion), channel_id=1, source_target_pairs={{0,4},{1,3},{2,6},{3,1},{4,0},{5,7},{6,2},{7,5},{8,12},{9,11},{10,... | collective-permute-start | bytes 98312 | tf_op jit(solution)/shard_map/ppermute | solution.py:351
  45.5 1.9 %collective-permute-done.8 = bf16[16,8,128]{2,1,0:T(8,128)(2,1)S(1)} collective-permute-done((bf16[16,8,128]{2,1,0:T(8,128)(2,1)S(1)}, bf16[16,8,128]{2,1,0:T(8,128)(2,1)S(1)}, u32[]{:S(2)}, u32[]{:S(2)}) %collective-permute-start.8) | collective-permute-done | bytes 32800 | tf_op jit(solution)/shard_map/ppermute | solution.py:351
  47.4 1.5 %collective-permute-start.9 = (bf16[33,8,128]{2,1,0:T(8,128)(2,1)S(1)}, bf16[33,8,128]{2,1,0:T(8,128)(2,1)S(1)}, u32[]{:S(2)}, u32[]{:S(2)}) collective-permute-start(bf16[33,8,128]{2,1,0:T(8,128)(2,1)S(1)} %pad_maximum_fusion.5), channel_id=1, source_target_pairs={{0,2},{1,5},{2,0},{3,7},{4,6},{5,1},{6,4},{7,3},{8,10},{9,13},{10,... | collective-permute-start | bytes 202760 | tf_op jit(solution)/shard_map/ppermute | solution.py:351
  48.9 2.8 %collective-permute-done.9 = bf16[33,8,128]{2,1,0:T(8,128)(2,1)S(1)} collective-permute-done((bf16[33,8,128]{2,1,0:T(8,128)(2,1)S(1)}, bf16[33,8,128]{2,1,0:T(8,128)(2,1)S(1)}, u32[]{:S(2)}, u32[]{:S(2)}) %collective-permute-start.9) | collective-permute-done | bytes 67616 | tf_op jit(solution)/shard_map/ppermute | solution.py:351
  51.7 0.1 collective-permute-start.10
  51.8 1.3 %collective-permute-done.10 = bf16[64,8,128]{2,1,0:T(8,128)(2,1)S(1)} collective-permute-done((bf16[64,8,128]{2,1,0:T(8,128)(2,1)S(1)}, bf16[64,8,128]{2,1,0:T(8,128)(2,1)S(1)}, u32[]{:S(2)}, u32[]{:S(2)}) %collective-permute-start.10) | collective-permute-done | bytes 131104 | tf_op jit(solution)/shard_map/ppermute | solution.py:351
  53.2 3.2 %shard_map.113 = bf16[2,128,8,128]{3,2,1,0:T(8,128)(2,1)} custom-call(bf16[2,64,8,128]{3,2,1,0:T(8,128)(2,1)S(1)} %get-tuple-element.28.refs_8_.early_ref, bf16[2,64,8,128]{3,2,1,0:T(8,128)(2,1)S(1)} %get-tuple-element.29.late_ref, bf16[128,8,128]{2,1,0:T(8,128)(2,1)S(1)} %pad_maximum_fusion.pooled_ref, bf16[4,8,128]{2,1,0:T(8,128)(2,1)S(1)} %pad_maximum_fusion.6.strip_ref, ...), custom_call_target="tpu_custom_call" | custom-call | flops 452984832 | bytes 1647104 | tf_op jit(solution)/shard_map/pallas_call | solution.py:373
  (39 shorter events, 0.3 us)
Async XLA Ops:
  0.0 4.6 %copy-start.5 = (bf16[27,128,128]{2,1,0:T(8,128)(2,1)S(1)}, bf16[27,128,128]{2,1,0:T(8,128)(2,1)}, u32[]{:S(2)}) copy-start(bf16[27,128,128]{2,1,0:T(8,128)(2,1)} %param.13) | copy-start | bytes 2654212
  0.0 4.6 %copy-start.6 = (bf16[27,128,128]{2,1,0:T(8,128)(2,1)S(1)}, bf16[27,128,128]{2,1,0:T(8,128)(2,1)}, u32[]{:S(2)}) copy-start(bf16[27,128,128]{2,1,0:T(8,128)(2,1)} %param.14) | copy-start | bytes 2654212
  0.0 4.6 %collective-permute-start = (bf16[2,128,8,128]{3,2,1,0:T(8,128)(2,1)}, bf16[2,128,8,128]{3,2,1,0:T(8,128)(2,1)S(1)}, u32[]{:S(2)}, u32[]{:S(2)}) collective-permute-start(bf16[2,128,8,128]{3,2,1,0:T(8,128)(2,1)} %own_ref.3), channel_id=1, source_target_pairs={{0,1},{1,0},{2,3},{3,2},{4,5},{5,4},{6,7},{7,6},{8,9},{9,8},{10,11... | collective-permute-start | bytes 1572872 | tf_op jit(solution)/shard_map/ppermute | solution.py:351
  0.5 1.1 %copy-start.7 = (bf16[2,128,8,128]{3,2,1,0:T(8,128)(2,1)S(1)}, bf16[2,128,8,128]{3,2,1,0:T(8,128)(2,1)}, u32[]{:S(2)}) copy-start(bf16[2,128,8,128]{3,2,1,0:T(8,128)(2,1)} %own_ref.3) | copy-start | bytes 1572868
  2.0 7.3 %collective-permute-start.1 = (bf16[2,2,36,8,128]{4,3,2,1,0:T(8,128)(2,1)S(1)}, bf16[2,2,36,8,128]{4,3,2,1,0:T(8,128)(2,1)S(1)}, u32[]{:S(2)}, u32[]{:S(2)}) collective-permute-start(bf16[2,2,36,8,128]{4,3,2,1,0:T(8,128)(2,1)S(1)} %get-tuple-element.23), channel_id=1, source_target_pairs={{0,16},{15,31},{1,2},{2,1},{3,4},{4,3},{5,6},{6,5},{7,8},{8,7},{9,... | collective-permute-start | bytes 884744 | tf_op jit(solution)/shard_map/ppermute | solution.py:428
  4.6 4.7 %copy-start.8 = (bf16[128,128]{1,0:T(8,128)(2,1)S(1)}, bf16[128,128]{1,0:T(8,128)(2,1)}, u32[]{:S(2)}) copy-start(bf16[128,128]{1,0:T(8,128)(2,1)} %refs_5_.3) | copy-start | bytes 98308
  4.7 4.7 %copy-start.9 = (bf16[128,128]{1,0:T(8,128)(2,1)S(1)}, bf16[128,128]{1,0:T(8,128)(2,1)}, u32[]{:S(2)}) copy-start(bf16[128,128]{1,0:T(8,128)(2,1)} %refs_6_.3) | copy-start | bytes 98308
  4.7 4.7 %copy-start.10 = (f32[2,128,8]{1,2,0:T(8,128)S(1)}, f32[2,128,8]{1,2,0:T(8,128)}, u32[]{:S(2)}) copy-start(f32[2,128,8]{1,2,0:T(8,128)} %param.12) | copy-start | bytes 24580
  11.5 3.8 %collective-permute-start.3 = (bf16[96,8,128]{2,1,0:T(8,128)(2,1)S(1)}, bf16[96,8,128]{2,1,0:T(8,128)(2,1)S(1)}, u32[]{:S(2)}, u32[]{:S(2)}) collective-permute-start(bf16[96,8,128]{2,1,0:T(8,128)(2,1)S(1)} %get-tuple-element.27), channel_id=1, source_target_pairs={{0,1},{1,0},{2,3},{3,2},{4,5},{5,4},{6,7},{7,6},{8,9},{9,8},{10,11... | collective-permute-start | bytes 589832 | tf_op jit(solution)/shard_map/ppermute | solution.py:351
  13.8 6.7 %collective-permute-start.2 = (bf16[2,2,36,8,128]{4,3,2,1,0:T(8,128)(2,1)S(1)}, bf16[2,2,36,8,128]{4,3,2,1,0:T(8,128)(2,1)S(1)}, u32[]{:S(2)}, u32[]{:S(2)}) collective-permute-start(bf16[2,2,36,8,128]{4,3,2,1,0:T(8,128)(2,1)S(1)} %get-tuple-element.25), channel_id=1, source_target_pairs={{0,16},{15,31},{1,2},{2,1},{3,4},{4,3},{5,6},{6,5},{7,8},{8,7},{9,... | collective-permute-start | bytes 884744 | tf_op jit(solution)/shard_map/ppermute | solution.py:429
  23.3 8.8 %collective-permute-start.4 = (bf16[98,8,128]{2,1,0:T(8,128)(2,1)S(1)}, bf16[98,8,128]{2,1,0:T(8,128)(2,1)S(1)}, u32[]{:S(2)}, u32[]{:S(2)}) collective-permute-start(bf16[98,8,128]{2,1,0:T(8,128)(2,1)S(1)} %get-tuple-element.31), channel_id=1, source_target_pairs={{0,1},{1,0},{2,3},{3,2},{4,5},{5,4},{6,7},{7,6},{8,9},{9,8},{10,11... | collective-permute-start | bytes 602120 | tf_op jit(solution)/shard_map/ppermute | solution.py:351
  26.0 6.1 %collective-permute-start.5 = (bf16[96,8,128]{2,1,0:T(8,128)(2,1)S(1)}, bf16[96,8,128]{2,1,0:T(8,128)(2,1)S(1)}, u32[]{:S(2)}, u32[]{:S(2)}) collective-permute-start(bf16[96,8,128]{2,1,0:T(8,128)(2,1)S(1)} %pad_maximum_fusion.1), channel_id=1, source_target_pairs={{0,2},{1,5},{2,0},{3,7},{4,6},{5,1},{6,4},{7,3},{8,10},{9,13},{10,... | collective-permute-start | bytes 589832 | tf_op jit(solution)/shard_map/ppermute | solution.py:351
  32.3 5.1 %collective-permute-start.6 = (bf16[49,8,128]{2,1,0:T(8,128)(2,1)S(1)}, bf16[49,8,128]{2,1,0:T(8,128)(2,1)S(1)}, u32[]{:S(2)}, u32[]{:S(2)}) collective-permute-start(bf16[49,8,128]{2,1,0:T(8,128)(2,1)S(1)} %pad_maximum_fusion.3), channel_id=1, source_target_pairs={{0,4},{1,3},{2,6},{3,1},{4,0},{5,7},{6,2},{7,5},{8,12},{9,11},{10,... | collective-permute-start | bytes 301064 | tf_op jit(solution)/shard_map/ppermute | solution.py:351
  37.4 15.7 %copy-start = (bf16[9,128,128]{2,1,0:T(8,128)(2,1)S(1)}, bf16[9,128,128]{2,1,0:T(8,128)(2,1)}, u32[]{:S(2)}) copy-start(bf16[9,128,128]{2,1,0:T(8,128)(2,1)} %param.17) | copy-start | bytes 884740
  37.4 15.7 %copy-start.1 = (bf16[9,128,128]{2,1,0:T(8,128)(2,1)S(1)}, bf16[9,128,128]{2,1,0:T(8,128)(2,1)}, u32[]{:S(2)}) copy-start(bf16[9,128,128]{2,1,0:T(8,128)(2,1)} %param.18) | copy-start | bytes 884740
  37.5 15.7 %copy-start.2 = (bf16[128,512]{1,0:T(8,128)(2,1)S(1)}, bf16[128,512]{1,0:T(8,128)(2,1)}, u32[]{:S(2)}) copy-start(bf16[128,512]{1,0:T(8,128)(2,1)} %in_ref.1) | copy-start | bytes 393220
  37.5 15.7 %copy-start.3 = (bf16[512,128]{1,0:T(8,128)(2,1)S(1)}, bf16[512,128]{1,0:T(8,128)(2,1)}, u32[]{:S(2)}) copy-start(bf16[512,128]{1,0:T(8,128)(2,1)} %out_w_ref.1) | copy-start | bytes 393220
  37.5 15.7 %copy-start.4 = (f32[128]{0:T(128)S(1)}, f32[128]{0:T(128)}, u32[]{:S(2)}) copy-start(f32[128]{0:T(128)} %param.19) | copy-start | bytes 1540
  37.6 5.7 %collective-permute-start.7 = (bf16[49,8,128]{2,1,0:T(8,128)(2,1)S(1)}, bf16[49,8,128]{2,1,0:T(8,128)(2,1)S(1)}, u32[]{:S(2)}, u32[]{:S(2)}) collective-permute-start(bf16[49,8,128]{2,1,0:T(8,128)(2,1)S(1)} %pad_maximum_fusion.4), channel_id=1, source_target_pairs={{0,8},{1,9},{2,10},{3,11},{4,12},{5,13},{6,14},{7,15},{8,0},{9,1},... | collective-permute-start | bytes 301064 | tf_op jit(solution)/shard_map/ppermute | solution.py:351
  43.3 4.1 %collective-permute-start.8 = (bf16[16,8,128]{2,1,0:T(8,128)(2,1)S(1)}, bf16[16,8,128]{2,1,0:T(8,128)(2,1)S(1)}, u32[]{:S(2)}, u32[]{:S(2)}) collective-permute-start(bf16[16,8,128]{2,1,0:T(8,128)(2,1)S(1)} %divide_convert_fusion), channel_id=1, source_target_pairs={{0,4},{1,3},{2,6},{3,1},{4,0},{5,7},{6,2},{7,5},{8,12},{9,11},{10,... | collective-permute-start | bytes 98312 | tf_op jit(solution)/shard_map/ppermute | solution.py:351
  47.4 4.3 %collective-permute-start.9 = (bf16[33,8,128]{2,1,0:T(8,128)(2,1)S(1)}, bf16[33,8,128]{2,1,0:T(8,128)(2,1)S(1)}, u32[]{:S(2)}, u32[]{:S(2)}) collective-permute-start(bf16[33,8,128]{2,1,0:T(8,128)(2,1)S(1)} %pad_maximum_fusion.5), channel_id=1, source_target_pairs={{0,2},{1,5},{2,0},{3,7},{4,6},{5,1},{6,4},{7,3},{8,10},{9,13},{10,... | collective-permute-start | bytes 202760 | tf_op jit(solution)/shard_map/ppermute | solution.py:351
  51.7 1.4 %collective-permute-start.10 = (bf16[64,8,128]{2,1,0:T(8,128)(2,1)S(1)}, bf16[64,8,128]{2,1,0:T(8,128)(2,1)S(1)}, u32[]{:S(2)}, u32[]{:S(2)}) collective-permute-start(bf16[64,8,128]{2,1,0:T(8,128)(2,1)S(1)} %pad_maximum_fusion.2), channel_id=1, source_target_pairs={{0,1},{1,0},{2,3},{3,2},{4,5},{5,4},{6,7},{7,6},{8,9},{9,8},{10,11... | collective-permute-start | bytes 393224 | tf_op jit(solution)/shard_map/ppermute | solution.py:351

commit v6 on v4

--- a/solution.py
+++ b/solution.py
@@ -9,7 +9,6 @@
 
 BF = jnp.bfloat16
 F32 = jnp.float32
-IN_VMEM = pl.BlockSpec(memory_space=pltpu.VMEM)
 PAIR = ({0: 0, 1: 1, 2: 2}, {1: 0, 2: 1, 3: 2})
 LOWER = ({0: 0, 1: 1}, {1: 0})
 UPPER = ({2: 2}, {2: 1, 3: 2})
@@ -129,9 +128,9 @@
 def half_kernel(axis, second, *refs):
     edge_ref, part_ref, far_ref, w1_ref, w2_ref, x_ref, y_ref, prior_ref = refs[:8]
     if second:
-        state_ref, feature_ref, message_ref, keep_ref, strip_ref, rows_ref, mid_ref = refs[8:]
+        early_ref, feature_ref, message_ref, keep_ref, strip_ref, rows_ref, mid_ref = refs[8:]
     else:
-        feature_ref, message_ref, keep_ref, state_ref, rows_ref, mid_ref = refs[8:]
+        feature_ref, message_ref, keep_ref, rows_ref, mid_ref = refs[8:]
     across, depth, channels = part_ref.shape[1:]
     devices = lax.axis_size(axis)
     index = lax.axis_index(axis)
@@ -156,39 +155,41 @@
     mid_ref[1, half * (span + 1)] = blank
     outs = conv_rows(mid_ref, w2_ref, (2 * side, 1, 2 - 2 * side), 0, span, LOWER)
     place = pl.ds(half * span, span)
-    score = beside([x_ref[...], y_ref[...]])
+    across_score, along_score = x_ref[...], y_ref[...]
+
+    def prior_of(at, half):
+        columns = prior_ref[at]
+        columns = jnp.where(half == 0, columns[:, :span], columns[:, span:])
+        return jnp.stack(
+            [jnp.broadcast_to(columns[:, y : y + 1], (depth, channels)) for y in range(span)]
+        )
+
     logits, features = [], []
     for u in range(2):
         at = side if u == 0 else 1 - side
         feature = (outs[u] + part_ref[u, place]).astype(BF)
         feature_ref[at] = feature
-        both = jnp.dot(feature.reshape(-1, channels), score, preferred_element_type=F32)
-        columns = prior_ref[at]
-        columns = jnp.where(half == 0, columns[:, :span], columns[:, span:])
-        prior = jnp.stack(
-            [jnp.broadcast_to(columns[:, y : y + 1], (depth, channels)) for y in range(span)]
-        )
-        feature = feature.astype(F32)
-        features.append(feature)
-        logits.append(both[:, :channels].reshape(span, depth, channels) + prior)
-        logit_y = both[:, channels:].reshape(span, depth, channels) + prior
-        top = jnp.max(logit_y, axis=0)
-        if second:
-            top = jnp.maximum(top, state_ref[u, 0])
-        weights = jnp.exp(logit_y - top)
-        norm_sum = jnp.sum(weights, axis=0)
-        weighted = jnp.sum(weights * feature, axis=0)
-        if second:
-            scale = jnp.exp(state_ref[u, 0] - top)
-            norm_sum = norm_sum + state_ref[u, 1] * scale
-            weighted = weighted + state_ref[u, 2] * scale
+        prior = prior_of(at, half)
+        if not second:
+            logit = jnp.dot(feature.reshape(-1, channels), across_score, preferred_element_type=F32)
+        else:
+            score = beside([across_score, along_score])
+            both = jnp.dot(feature.reshape(-1, channels), score, preferred_element_type=F32)
+            logit = both[:, :channels]
+            logit_y = both[:, channels:].reshape(span, depth, channels) + prior
+            other = early_ref[at]
+            other_y = jnp.dot(other.reshape(-1, channels), along_score, preferred_element_type=F32)
+            other_y = other_y.reshape(span, depth, channels) + prior_of(at, 1 - half)
+            top = jnp.maximum(jnp.max(logit_y, axis=0), jnp.max(other_y, axis=0))
+            weights, others = jnp.exp(logit_y - top), jnp.exp(other_y - top)
+            norm_sum = jnp.sum(weights, axis=0) + jnp.sum(others, axis=0)
+            weighted = jnp.sum(weights * feature.astype(F32), axis=0)
+            weighted = weighted + jnp.sum(others * other.astype(F32), axis=0)
             pooled = (weighted / norm_sum).astype(BF)
             strip_ref[u] = pooled
             message_ref[3 * (span // 2) + 1 - u] = pooled
-        else:
-            state_ref[u, 0] = top
-            state_ref[u, 1] = norm_sum
-            state_ref[u, 2] = weighted
+        features.append(feature.astype(F32))
+        logits.append(logit.reshape(span, depth, channels) + prior)
     peak = jnp.maximum(logits[0], logits[1])
     coarse = peak.astype(BF)
     shift = jnp.exp(jnp.clip(peak - coarse.astype(F32), -60.0, 60.0))
@@ -220,9 +221,11 @@
     gain_ref,
     in_ref,
     out_w_ref,
-    out_ref,
+    out_hbm,
     plane_ref,
     mix_ref,
+    out_ref,
+    sems,
 ):
     rows, half, depth, channels = early_ref.shape
     across = 2 * half
@@ -262,7 +265,8 @@
     mix_ref[side] = mixed[0]
     mix_ref[1 - side] = mixed[1]
     gain = gain_ref[...]
-    span = min(32, half)
+    span = out_ref.shape[2]
+    copies = []
     for step in range(across // span):
         early = step * span < half
         feature_ref = early_ref if early else late_ref
@@ -273,17 +277,25 @@
             [[yz_ref[b, c] for c in range(3)] for b in range(3)],
             (span, depth, channels),
         )
+        feature = feature_ref[:, at : at + span].astype(F32)
+        mixing = plane[None] + jnp.stack([mix_ref[row] for row in range(rows)])[:, None]
+        joined = (feature * mixing).reshape(-1, channels)
+        mean = jnp.mean(joined * joined, axis=-1, keepdims=True)
+        normed = (joined * lax.rsqrt(mean + 1e-06) * gain).astype(BF)
+        hidden = jnp.dot(normed, in_ref[...], preferred_element_type=F32)
+        hidden = twice_activate(hidden).astype(BF)
+        update = 0.5 * jnp.dot(hidden, out_w_ref[...], preferred_element_type=F32)
+        encoded = (joined + update).astype(BF).reshape(rows, span, depth, channels)
         for row in range(rows):
-            feature = feature_ref[row, at : at + span].astype(F32)
-            joined = (feature * (plane + mix_ref[row])).reshape(-1, channels)
-            mean = jnp.mean(joined * joined, axis=-1, keepdims=True)
-            normed = (joined * lax.rsqrt(mean + 1e-06) * gain).astype(BF)
-            hidden = jnp.dot(normed, in_ref[...], preferred_element_type=F32)
-            hidden = twice_activate(hidden).astype(BF)
-            update = 0.5 * jnp.dot(hidden, out_w_ref[...], preferred_element_type=F32)
-            out_ref[row, pl.ds(start, span)] = (
-                (joined + update).astype(BF).reshape(span, depth, channels)
+            out_ref[row, step] = encoded[row]
+            copies.append(
+                pltpu.make_async_copy(
+                    out_ref.at[row, step], out_hbm.at[row, pl.ds(start, span)], sems.at[row, step]
+                )
             )
+            copies[-1].start()
+    for copy in copies:
+        copy.wait()
 
 
 def swap(values, axis, mask):
@@ -308,13 +320,13 @@
     return [message[k * size : (k + 1) * size] for k in range(3)]
 
 
-def kernel_call(body, outs, scratch, flops, *operands, spaces=None):
+def kernel_call(body, outs, scratch, flops, *operands, spaces=None, results=pltpu.VMEM):
     moved = sum(o.size * o.dtype.itemsize for o in operands)
     return pl.pallas_call(
         body,
         out_shape=outs,
         in_specs=[pl.BlockSpec(memory_space=m) for m in spaces or [pltpu.VMEM] * len(operands)],
-        out_specs=jax.tree.map(lambda _: IN_VMEM, outs),
+        out_specs=jax.tree.map(lambda _: pl.BlockSpec(memory_space=results), outs),
         scratch_shapes=scratch,
         compiler_params=pltpu.CompilerParams(vmem_limit_bytes=14 * 1024 * 1024),
         cost_estimate=pl.CostEstimate(flops=flops, bytes_accessed=moved, transcendentals=0),
@@ -390,14 +402,10 @@
         feature = jax.ShapeDtypeStruct((rows, half, depth, channels), BF)
         message = jax.ShapeDtypeStruct((3 * quarter + 2 * second, depth, channels), BF)
         keep = jax.ShapeDtypeStruct((3, quarter, depth, channels), F32)
-        last = (
-            jax.ShapeDtypeStruct((rows, depth, channels), BF)
-            if second
-            else jax.ShapeDtypeStruct((rows, 3, depth, channels), F32)
-        )
+        strip = (jax.ShapeDtypeStruct((rows, depth, channels), BF),) if second else ()
         return kernel_call(
             functools.partial(half_kernel, axis, second),
-            (feature, message, keep, last),
+            (feature, message, keep) + strip,
             [
                 pltpu.VMEM((2, half + 4, depth, channels), BF),
                 pltpu.VMEM((2, half + 2, depth, channels), BF),
@@ -415,12 +423,12 @@
         )
 
     masks = [1 << bit for bit in range(devices.bit_length() - 1)]
-    early, message, keep, state = half_call(False, far0)
+    early, message, keep = half_call(False, far0)
     got = swap(message, axis, masks[0])
     sent = jnp.concatenate([p.astype(BF) for p in merge(keep, thirds(got))])
-    sent, state = lax.optimization_barrier((sent, state))
+    sent, early_first = lax.optimization_barrier((sent, early))
     arriving = swap(sent, axis, masks[1])
-    late, message, keep, strip = half_call(True, far1, state)
+    late, message, keep, strip = half_call(True, far1, early_first)
     got = swap(message, axis, masks[0])
     beyond = got[3 * quarter]
     carried = [got[3 * quarter + 1]]
@@ -452,12 +460,15 @@
     pooled = jnp.concatenate([pooled, got[:-1]], axis=0)
     pooled = jnp.concatenate([pooled, swap(pooled, axis, masks[0])], axis=0)
     strip = jnp.concatenate([before[None], strip, beyond[None]], axis=0)
+    span = min(64, half)
     return kernel_call(
         functools.partial(last_kernel, axis),
         jax.ShapeDtypeStruct(voxels.shape, BF),
         [
             pltpu.VMEM((across + 2, depth, channels), BF),
             pltpu.VMEM((rows, depth, channels), F32),
+            pltpu.VMEM((rows, across // span, span, depth, channels), BF),
+            pltpu.SemaphoreType.DMA((rows, across // span)),
         ],
         flops // 4,
         early,
@@ -469,6 +480,7 @@
         norm_gain.reshape(1, channels),
         mlp_in,
         mlp_out,
+        results=pl.ANY,
     )
 
 

time: 57.3 us -> 55.9 us (0.976)
  Pallas kernels: 13.5 us -> 12.1 us
    pallas_call x5, Pallas kernels: 13.5 us -> 12.1 us  [kernel_call(): pl.pallas_call(body, out_shape=outs, in_specs=[pl.BlockSpec(memory_space=...]
where the time goes in v6:
time: 55.9 us; the launch traced here: 55.8 us
  waiting for transfers between devices  21.8 us (39%)
  starting transfers between devices  19.9 us (36%)
  Pallas kernels  12.1 us (22%)
  local copies, waits for them, and re-layouts  1.18 us (2%)
    ppermute x9, waiting for transfers between devices, swap(): return lax.ppermute(values, axis, [(i, i ^ mask) for i in range(devices)])  17 us
    ppermute x9, starting transfers between devices, swap(): return lax.ppermute(values, axis, [(i, i ^ mask) for i in range(devices)])  15.8 us
    pallas_call x5, Pallas kernels, kernel_call(): pl.pallas_call(body, out_shape=outs, in_specs=[pl.BlockSpec(memory_space=...  12.1 us
    ppermute x1, waiting for transfers between devices, on_device(): far1 = lax.ppermute(cuts[1], (others, axis), pairs)  4.82 us
    ppermute x1, starting transfers between devices, on_device(): far0 = lax.ppermute(cuts[0], (others, axis), pairs)  2.64 us
    ppermute x1, starting transfers between devices, on_device(): far1 = lax.ppermute(cuts[1], (others, axis), pairs)  1.49 us
    unnamed x22, local copies, waits for them, and re-layouts  1.13 us
  transfers between devices with their start and end apart: 11, of which 7 were waited for; matrix products, arithmetic and copies ran while one was open for 0% of the time, Pallas kernels for 8%

profile of v6, /device:TPU:0, one launch (start us, length us, event | category | flops | bytes accessed | tf_op | source)
XLA Modules:
  0.0 55.8 jit_solution(7874119888576565024)
XLA Ops:
  0.0 0.5 collective-permute-start
  0.5 1.1 %copy-done.7 = bf16[2,128,8,128]{3,2,1,0:T(8,128)(2,1)S(1)} copy-done((bf16[2,128,8,128]{3,2,1,0:T(8,128)(2,1)S(1)}, bf16[2,128,8,128]{3,2,1,0:T(8,128)(2,1)}, u32[]{:S(2)}) %copy-start.7) | copy-done | bytes 524312
  1.6 0.1 shard_map.109
  1.6 2.6 %collective-permute-start.1 = (bf16[2,66,8,128]{3,2,1,0:T(8,128)(2,1)S(1)}, bf16[2,66,8,128]{3,2,1,0:T(8,128)(2,1)S(1)}, u32[]{:S(2)}, u32[]{:S(2)}) collective-permute-start(bf16[2,66,8,128]{3,2,1,0:T(8,128)(2,1)S(1)} %get-tuple-element.21.cut0_ref), channel_id=1, source_target_pairs={{0,16},{15,31},{1,2},{2,1},{3,4},{4,3},{5,6},{6,5},{7,8},{8,7},{9,... | collective-permute-start | bytes 811016 | tf_op jit(solution)/shard_map/ppermute | solution.py:380
  4.3 0.0 copy-start.8
  4.3 0.0 copy-start.10
  4.3 4.5 %shard_map.110 = (f32[2,130,8,128]{3,2,1,0:T(8,128)S(1)}, f32[2,128,8,128]{3,2,1,0:T(8,128)S(1)}) custom-call(bf16[2,66,8,128]{3,2,1,0:T(8,128)(2,1)S(1)} %get-tuple-element.21.cut0_ref, bf16[2,66,8,128]{3,2,1,0:T(8,128)(2,1)S(1)} %get-tuple-element.22.cut1_ref, bf16[2,128,8,128]{3,2,1,0:T(8,128)(2,1)S(1)} %collective-permute-done.near_ref, ...), custom_call_target="tpu_custom_call" | custom-call | flops 3623878656 | bytes 2834432 | tf_op jit(solution)/shard_map/pallas_call | solution.py:325
  8.9 2.0 %shard_map.111 = (bf16[2,64,8,128]{3,2,1,0:T(8,128)(2,1)S(1)}, bf16[96,8,128]{2,1,0:T(8,128)(2,1)S(1)}, f32[3,32,8,128]{3,2,1,0:T(8,128)S(1)}) custom-call(f32[2,130,8,128]{3,2,1,0:T(8,128)S(1)} %get-tuple-element.23.refs_0_, f32[2,128,8,128]{3,2,1,0:T(8,128)S(1)} %get-tuple-element.24.refs_1_, bf16[2,66,8,128]{3,2,1,0:T(8,128)(2,1)S(1)} %collective-permute-done.1.refs_2_, ...), custom_call_target="tpu_custom_call" | custom-call | flops 1358954496 | bytes 4227072 | tf_op jit(solution)/shard_map/pallas_call | solution.py:325
  10.9 1.9 %collective-permute-start.3 = (bf16[96,8,128]{2,1,0:T(8,128)(2,1)S(1)}, bf16[96,8,128]{2,1,0:T(8,128)(2,1)S(1)}, u32[]{:S(2)}, u32[]{:S(2)}) collective-permute-start(bf16[96,8,128]{2,1,0:T(8,128)(2,1)S(1)} %get-tuple-element.27), channel_id=1, source_target_pairs={{0,1},{1,0},{2,3},{3,2},{4,5},{5,4},{6,7},{7,6},{8,9},{9,8},{10,11... | collective-permute-start | bytes 589832 | tf_op jit(solution)/shard_map/ppermute | solution.py:303
  12.8 1.5 %collective-permute-start.2 = (bf16[2,66,8,128]{3,2,1,0:T(8,128)(2,1)S(1)}, bf16[2,66,8,128]{3,2,1,0:T(8,128)(2,1)S(1)}, u32[]{:S(2)}, u32[]{:S(2)}) collective-permute-start(bf16[2,66,8,128]{3,2,1,0:T(8,128)(2,1)S(1)} %get-tuple-element.22.cut1_ref), channel_id=1, source_target_pairs={{0,16},{15,31},{1,2},{2,1},{3,4},{4,3},{5,6},{6,5},{7,8},{8,7},{9,... | collective-permute-start | bytes 811016 | tf_op jit(solution)/shard_map/ppermute | solution.py:381
  14.3 0.1 fusion.16
  14.4 4.8 %collective-permute-done.2.refs_2_ = bf16[2,66,8,128]{3,2,1,0:T(8,128)(2,1)S(1)} collective-permute-done((bf16[2,66,8,128]{3,2,1,0:T(8,128)(2,1)S(1)}, bf16[2,66,8,128]{3,2,1,0:T(8,128)(2,1)S(1)}, u32[]{:S(2)}, u32[]{:S(2)}) %collective-permute-start.2) | collective-permute-done | bytes 270368 | tf_op jit(solution)/shard_map/ppermute | solution.py:381
  19.3 2.3 %shard_map.112 = (bf16[2,64,8,128]{3,2,1,0:T(8,128)(2,1)S(1)}, bf16[98,8,128]{2,1,0:T(8,128)(2,1)S(1)}, f32[3,32,8,128]{3,2,1,0:T(8,128)S(1)}, bf16[2,8,128]{2,1,0:T(8,128)(2,1)S(1)}) custom-call(f32[2,130,8,128]{3,2,1,0:T(8,128)S(1)} %get-tuple-element.23.refs_0_, f32[2,128,8,128]{3,2,1,0:T(8,128)S(1)} %get-tuple-element.24.refs_1_, ...), custom_call_target="tpu_custom_call" | custom-call | flops 1358954496 | bytes 4489216 | tf_op jit(solution)/shard_map/pallas_call | solution.py:325
  21.6 2.5 %collective-permute-start.4 = (bf16[98,8,128]{2,1,0:T(8,128)(2,1)S(1)}, bf16[98,8,128]{2,1,0:T(8,128)(2,1)S(1)}, u32[]{:S(2)}, u32[]{:S(2)}) collective-permute-start(bf16[98,8,128]{2,1,0:T(8,128)(2,1)S(1)} %get-tuple-element.31), channel_id=1, source_target_pairs={{0,1},{1,0},{2,3},{3,2},{4,5},{5,4},{6,7},{7,6},{8,9},{9,8},{10,11... | collective-permute-start | bytes 602120 | tf_op jit(solution)/shard_map/ppermute | solution.py:303
  24.1 2.4 %collective-permute-start.5 = (bf16[96,8,128]{2,1,0:T(8,128)(2,1)S(1)}, bf16[96,8,128]{2,1,0:T(8,128)(2,1)S(1)}, u32[]{:S(2)}, u32[]{:S(2)}) collective-permute-start(bf16[96,8,128]{2,1,0:T(8,128)(2,1)S(1)} %pad_maximum_fusion.1), channel_id=1, source_target_pairs={{0,2},{1,3},{2,0},{3,1},{4,6},{5,7},{6,4},{7,5},{8,10},{9,11},{10,... | collective-permute-start | bytes 589832 | tf_op jit(solution)/shard_map/ppermute | solution.py:303
  26.5 5.5 %collective-permute-done.5 = bf16[96,8,128]{2,1,0:T(8,128)(2,1)S(1)} collective-permute-done((bf16[96,8,128]{2,1,0:T(8,128)(2,1)S(1)}, bf16[96,8,128]{2,1,0:T(8,128)(2,1)S(1)}, u32[]{:S(2)}, u32[]{:S(2)}) %collective-permute-start.5) | collective-permute-done | bytes 196640 | tf_op jit(solution)/shard_map/ppermute | solution.py:303
  32.0 0.1 convert_maximum_fusion
  32.2 1.8 %collective-permute-start.6 = (bf16[49,8,128]{2,1,0:T(8,128)(2,1)S(1)}, bf16[49,8,128]{2,1,0:T(8,128)(2,1)S(1)}, u32[]{:S(2)}, u32[]{:S(2)}) collective-permute-start(bf16[49,8,128]{2,1,0:T(8,128)(2,1)S(1)} %pad_maximum_fusion.3), channel_id=1, source_target_pairs={{0,4},{1,5},{2,6},{3,7},{4,0},{5,1},{6,2},{7,3},{8,12},{9,13},{10,... | collective-permute-start | bytes 301064 | tf_op jit(solution)/shard_map/ppermute | solution.py:303
  34.0 2.9 %collective-permute-done.6 = bf16[49,8,128]{2,1,0:T(8,128)(2,1)S(1)} collective-permute-done((bf16[49,8,128]{2,1,0:T(8,128)(2,1)S(1)}, bf16[49,8,128]{2,1,0:T(8,128)(2,1)S(1)}, u32[]{:S(2)}, u32[]{:S(2)}) %collective-permute-start.6) | collective-permute-done | bytes 100384 | tf_op jit(solution)/shard_map/ppermute | solution.py:303
  37.0 0.0 copy-start
  37.0 0.0 copy-start.3
  37.0 0.0 copy-start.4
  37.1 2.8 %collective-permute-start.7 = (bf16[49,8,128]{2,1,0:T(8,128)(2,1)S(1)}, bf16[49,8,128]{2,1,0:T(8,128)(2,1)S(1)}, u32[]{:S(2)}, u32[]{:S(2)}) collective-permute-start(bf16[49,8,128]{2,1,0:T(8,128)(2,1)S(1)} %pad_maximum_fusion.4), channel_id=1, source_target_pairs={{0,8},{1,9},{2,10},{3,11},{4,12},{5,13},{6,14},{7,15},{8,0},{9,1},... | collective-permute-start | bytes 301064 | tf_op jit(solution)/shard_map/ppermute | solution.py:303
  39.9 2.8 %collective-permute-done.7 = bf16[49,8,128]{2,1,0:T(8,128)(2,1)S(1)} collective-permute-done((bf16[49,8,128]{2,1,0:T(8,128)(2,1)S(1)}, bf16[49,8,128]{2,1,0:T(8,128)(2,1)S(1)}, u32[]{:S(2)}, u32[]{:S(2)}) %collective-permute-start.7) | collective-permute-done | bytes 100384 | tf_op jit(solution)/shard_map/ppermute | solution.py:303
  42.7 0.1 divide_convert_fusion
  42.8 2.0 %collective-permute-start.8 = (bf16[16,8,128]{2,1,0:T(8,128)(2,1)S(1)}, bf16[16,8,128]{2,1,0:T(8,128)(2,1)S(1)}, u32[]{:S(2)}, u32[]{:S(2)}) collective-permute-start(bf16[16,8,128]{2,1,0:T(8,128)(2,1)S(1)} %divide_convert_fusion), channel_id=1, source_target_pairs={{0,4},{1,5},{2,6},{3,7},{4,0},{5,1},{6,2},{7,3},{8,12},{9,13},{10,... | collective-permute-start | bytes 98312 | tf_op jit(solution)/shard_map/ppermute | solution.py:303
  44.8 2.0 %collective-permute-done.8 = bf16[16,8,128]{2,1,0:T(8,128)(2,1)S(1)} collective-permute-done((bf16[16,8,128]{2,1,0:T(8,128)(2,1)S(1)}, bf16[16,8,128]{2,1,0:T(8,128)(2,1)S(1)}, u32[]{:S(2)}, u32[]{:S(2)}) %collective-permute-start.8) | collective-permute-done | bytes 32800 | tf_op jit(solution)/shard_map/ppermute | solution.py:303
  46.8 1.8 %collective-permute-start.9 = (bf16[33,8,128]{2,1,0:T(8,128)(2,1)S(1)}, bf16[33,8,128]{2,1,0:T(8,128)(2,1)S(1)}, u32[]{:S(2)}, u32[]{:S(2)}) collective-permute-start(bf16[33,8,128]{2,1,0:T(8,128)(2,1)S(1)} %pad_maximum_fusion.5), channel_id=1, source_target_pairs={{0,2},{1,3},{2,0},{3,1},{4,6},{5,7},{6,4},{7,5},{8,10},{9,11},{10,... | collective-permute-start | bytes 202760 | tf_op jit(solution)/shard_map/ppermute | solution.py:303
  48.5 2.5 %collective-permute-done.9 = bf16[33,8,128]{2,1,0:T(8,128)(2,1)S(1)} collective-permute-done((bf16[33,8,128]{2,1,0:T(8,128)(2,1)S(1)}, bf16[33,8,128]{2,1,0:T(8,128)(2,1)S(1)}, u32[]{:S(2)}, u32[]{:S(2)}) %collective-permute-start.9) | collective-permute-done | bytes 67616 | tf_op jit(solution)/shard_map/ppermute | solution.py:303
  51.1 0.1 collective-permute-start.10
  51.2 1.3 %collective-permute-done.10 = bf16[64,8,128]{2,1,0:T(8,128)(2,1)S(1)} collective-permute-done((bf16[64,8,128]{2,1,0:T(8,128)(2,1)S(1)}, bf16[64,8,128]{2,1,0:T(8,128)(2,1)S(1)}, u32[]{:S(2)}, u32[]{:S(2)}) %collective-permute-start.10) | collective-permute-done | bytes 131104 | tf_op jit(solution)/shard_map/ppermute | solution.py:303
  52.6 3.2 %shard_map.113 = bf16[2,128,8,128]{3,2,1,0:T(8,128)(2,1)} custom-call(bf16[2,64,8,128]{3,2,1,0:T(8,128)(2,1)S(1)} %get-tuple-element.28.refs_8_.early_ref, bf16[2,64,8,128]{3,2,1,0:T(8,128)(2,1)S(1)} %get-tuple-element.29.late_ref, bf16[128,8,128]{2,1,0:T(8,128)(2,1)S(1)} %pad_maximum_fusion.pooled_ref, bf16[4,8,128]{2,1,0:T(8,128)(2,1)S(1)} %pad_maximum_fusion.6.strip_ref, ...), custom_call_target="tpu_custom_call" | custom-call | flops 452984832 | bytes 1647104 | tf_op jit(solution)/shard_map/pallas_call | solution.py:325
  (39 shorter events, 0.3 us)
Async XLA Ops:
  0.0 4.3 %copy-start.5 = (bf16[27,128,128]{2,1,0:T(8,128)(2,1)S(1)}, bf16[27,128,128]{2,1,0:T(8,128)(2,1)}, u32[]{:S(2)}) copy-start(bf16[27,128,128]{2,1,0:T(8,128)(2,1)} %param.13) | copy-start | bytes 2654212
  0.0 4.3 %copy-start.6 = (bf16[27,128,128]{2,1,0:T(8,128)(2,1)S(1)}, bf16[27,128,128]{2,1,0:T(8,128)(2,1)}, u32[]{:S(2)}) copy-start(bf16[27,128,128]{2,1,0:T(8,128)(2,1)} %param.14) | copy-start | bytes 2654212
  0.0 4.3 %collective-permute-start = (bf16[2,128,8,128]{3,2,1,0:T(8,128)(2,1)}, bf16[2,128,8,128]{3,2,1,0:T(8,128)(2,1)S(1)}, u32[]{:S(2)}, u32[]{:S(2)}) collective-permute-start(bf16[2,128,8,128]{3,2,1,0:T(8,128)(2,1)} %own_ref.1), channel_id=1, source_target_pairs={{0,1},{1,0},{2,3},{3,2},{4,5},{5,4},{6,7},{7,6},{8,9},{9,8},{10,11... | collective-permute-start | bytes 1572872 | tf_op jit(solution)/shard_map/ppermute | solution.py:303
  0.5 1.1 %copy-start.7 = (bf16[2,128,8,128]{3,2,1,0:T(8,128)(2,1)S(1)}, bf16[2,128,8,128]{3,2,1,0:T(8,128)(2,1)}, u32[]{:S(2)}) copy-start(bf16[2,128,8,128]{3,2,1,0:T(8,128)(2,1)} %own_ref.1) | copy-start | bytes 1572868
  1.6 7.2 %collective-permute-start.1 = (bf16[2,66,8,128]{3,2,1,0:T(8,128)(2,1)S(1)}, bf16[2,66,8,128]{3,2,1,0:T(8,128)(2,1)S(1)}, u32[]{:S(2)}, u32[]{:S(2)}) collective-permute-start(bf16[2,66,8,128]{3,2,1,0:T(8,128)(2,1)S(1)} %get-tuple-element.21.cut0_ref), channel_id=1, source_target_pairs={{0,16},{15,31},{1,2},{2,1},{3,4},{4,3},{5,6},{6,5},{7,8},{8,7},{9,... | collective-permute-start | bytes 811016 | tf_op jit(solution)/shard_map/ppermute | solution.py:380
  4.3 4.6 %copy-start.8 = (bf16[128,128]{1,0:T(8,128)(2,1)S(1)}, bf16[128,128]{1,0:T(8,128)(2,1)}, u32[]{:S(2)}) copy-start(bf16[128,128]{1,0:T(8,128)(2,1)} %refs_5_.3) | copy-start | bytes 98308
  4.3 4.6 %copy-start.9 = (bf16[128,128]{1,0:T(8,128)(2,1)S(1)}, bf16[128,128]{1,0:T(8,128)(2,1)}, u32[]{:S(2)}) copy-start(bf16[128,128]{1,0:T(8,128)(2,1)} %refs_6_.3) | copy-start | bytes 98308
  4.3 4.6 %copy-start.10 = (f32[2,128,8]{1,2,0:T(8,128)S(1)}, f32[2,128,8]{1,2,0:T(8,128)}, u32[]{:S(2)}) copy-start(f32[2,128,8]{1,2,0:T(8,128)} %param.12) | copy-start | bytes 24580
  10.9 3.4 %collective-permute-start.3 = (bf16[96,8,128]{2,1,0:T(8,128)(2,1)S(1)}, bf16[96,8,128]{2,1,0:T(8,128)(2,1)S(1)}, u32[]{:S(2)}, u32[]{:S(2)}) collective-permute-start(bf16[96,8,128]{2,1,0:T(8,128)(2,1)S(1)} %get-tuple-element.27), channel_id=1, source_target_pairs={{0,1},{1,0},{2,3},{3,2},{4,5},{5,4},{6,7},{7,6},{8,9},{9,8},{10,11... | collective-permute-start | bytes 589832 | tf_op jit(solution)/shard_map/ppermute | solution.py:303
  12.8 6.5 %collective-permute-start.2 = (bf16[2,66,8,128]{3,2,1,0:T(8,128)(2,1)S(1)}, bf16[2,66,8,128]{3,2,1,0:T(8,128)(2,1)S(1)}, u32[]{:S(2)}, u32[]{:S(2)}) collective-permute-start(bf16[2,66,8,128]{3,2,1,0:T(8,128)(2,1)S(1)} %get-tuple-element.22.cut1_ref), channel_id=1, source_target_pairs={{0,16},{15,31},{1,2},{2,1},{3,4},{4,3},{5,6},{6,5},{7,8},{8,7},{9,... | collective-permute-start | bytes 811016 | tf_op jit(solution)/shard_map/ppermute | solution.py:381
  21.6 10.4 %collective-permute-start.4 = (bf16[98,8,128]{2,1,0:T(8,128)(2,1)S(1)}, bf16[98,8,128]{2,1,0:T(8,128)(2,1)S(1)}, u32[]{:S(2)}, u32[]{:S(2)}) collective-permute-start(bf16[98,8,128]{2,1,0:T(8,128)(2,1)S(1)} %get-tuple-element.31), channel_id=1, source_target_pairs={{0,1},{1,0},{2,3},{3,2},{4,5},{5,4},{6,7},{7,6},{8,9},{9,8},{10,11... | collective-permute-start | bytes 602120 | tf_op jit(solution)/shard_map/ppermute | solution.py:303
  24.1 7.9 %collective-permute-start.5 = (bf16[96,8,128]{2,1,0:T(8,128)(2,1)S(1)}, bf16[96,8,128]{2,1,0:T(8,128)(2,1)S(1)}, u32[]{:S(2)}, u32[]{:S(2)}) collective-permute-start(bf16[96,8,128]{2,1,0:T(8,128)(2,1)S(1)} %pad_maximum_fusion.1), channel_id=1, source_target_pairs={{0,2},{1,3},{2,0},{3,1},{4,6},{5,7},{6,4},{7,5},{8,10},{9,11},{10,... | collective-permute-start | bytes 589832 | tf_op jit(solution)/shard_map/ppermute | solution.py:303
  32.2 4.7 %collective-permute-start.6 = (bf16[49,8,128]{2,1,0:T(8,128)(2,1)S(1)}, bf16[49,8,128]{2,1,0:T(8,128)(2,1)S(1)}, u32[]{:S(2)}, u32[]{:S(2)}) collective-permute-start(bf16[49,8,128]{2,1,0:T(8,128)(2,1)S(1)} %pad_maximum_fusion.3), channel_id=1, source_target_pairs={{0,4},{1,5},{2,6},{3,7},{4,0},{5,1},{6,2},{7,3},{8,12},{9,13},{10,... | collective-permute-start | bytes 301064 | tf_op jit(solution)/shard_map/ppermute | solution.py:303
  37.0 15.5 %copy-start = (bf16[9,128,128]{2,1,0:T(8,128)(2,1)S(1)}, bf16[9,128,128]{2,1,0:T(8,128)(2,1)}, u32[]{:S(2)}) copy-start(bf16[9,128,128]{2,1,0:T(8,128)(2,1)} %param.17) | copy-start | bytes 884740
  37.0 15.5 %copy-start.1 = (bf16[9,128,128]{2,1,0:T(8,128)(2,1)S(1)}, bf16[9,128,128]{2,1,0:T(8,128)(2,1)}, u32[]{:S(2)}) copy-start(bf16[9,128,128]{2,1,0:T(8,128)(2,1)} %param.18) | copy-start | bytes 884740
  37.0 15.5 %copy-start.2 = (bf16[128,512]{1,0:T(8,128)(2,1)S(1)}, bf16[128,512]{1,0:T(8,128)(2,1)}, u32[]{:S(2)}) copy-start(bf16[128,512]{1,0:T(8,128)(2,1)} %in_ref.1) | copy-start | bytes 393220
  37.0 15.5 %copy-start.3 = (bf16[512,128]{1,0:T(8,128)(2,1)S(1)}, bf16[512,128]{1,0:T(8,128)(2,1)}, u32[]{:S(2)}) copy-start(bf16[512,128]{1,0:T(8,128)(2,1)} %out_w_ref.1) | copy-start | bytes 393220
  37.0 15.5 %copy-start.4 = (f32[128]{0:T(128)S(1)}, f32[128]{0:T(128)}, u32[]{:S(2)}) copy-start(f32[128]{0:T(128)} %param.19) | copy-start | bytes 1540
  37.1 5.6 %collective-permute-start.7 = (bf16[49,8,128]{2,1,0:T(8,128)(2,1)S(1)}, bf16[49,8,128]{2,1,0:T(8,128)(2,1)S(1)}, u32[]{:S(2)}, u32[]{:S(2)}) collective-permute-start(bf16[49,8,128]{2,1,0:T(8,128)(2,1)S(1)} %pad_maximum_fusion.4), channel_id=1, source_target_pairs={{0,8},{1,9},{2,10},{3,11},{4,12},{5,13},{6,14},{7,15},{8,0},{9,1},... | collective-permute-start | bytes 301064 | tf_op jit(solution)/shard_map/ppermute | solution.py:303
  42.8 4.0 %collective-permute-start.8 = (bf16[16,8,128]{2,1,0:T(8,128)(2,1)S(1)}, bf16[16,8,128]{2,1,0:T(8,128)(2,1)S(1)}, u32[]{:S(2)}, u32[]{:S(2)}) collective-permute-start(bf16[16,8,128]{2,1,0:T(8,128)(2,1)S(1)} %divide_convert_fusion), channel_id=1, source_target_pairs={{0,4},{1,5},{2,6},{3,7},{4,0},{5,1},{6,2},{7,3},{8,12},{9,13},{10,... | collective-permute-start | bytes 98312 | tf_op jit(solution)/shard_map/ppermute | solution.py:303
  46.8 4.3 %collective-permute-start.9 = (bf16[33,8,128]{2,1,0:T(8,128)(2,1)S(1)}, bf16[33,8,128]{2,1,0:T(8,128)(2,1)S(1)}, u32[]{:S(2)}, u32[]{:S(2)}) collective-permute-start(bf16[33,8,128]{2,1,0:T(8,128)(2,1)S(1)} %pad_maximum_fusion.5), channel_id=1, source_target_pairs={{0,2},{1,3},{2,0},{3,1},{4,6},{5,7},{6,4},{7,5},{8,10},{9,11},{10,... | collective-permute-start | bytes 202760 | tf_op jit(solution)/shard_map/ppermute | solution.py:303
  51.1 1.4 %collective-permute-start.10 = (bf16[64,8,128]{2,1,0:T(8,128)(2,1)S(1)}, bf16[64,8,128]{2,1,0:T(8,128)(2,1)S(1)}, u32[]{:S(2)}, u32[]{:S(2)}) collective-permute-start(bf16[64,8,128]{2,1,0:T(8,128)(2,1)S(1)} %pad_maximum_fusion.2), channel_id=1, source_target_pairs={{0,1},{1,0},{2,3},{3,2},{4,5},{5,4},{6,7},{7,6},{8,9},{9,8},{10,11... | collective-permute-start | bytes 393224 | tf_op jit(solution)/shard_map/ppermute | solution.py:303

commit v7 on v6

--- a/solution.py
+++ b/solution.py
@@ -210,25 +210,17 @@
                 message_ref[k * quarter : (k + 1) * quarter] = part[cut].astype(BF)
 
 
-def last_kernel(
-    axis,
-    early_ref,
-    late_ref,
-    pooled_ref,
-    strip_ref,
-    yz_ref,
-    xz_ref,
-    gain_ref,
-    in_ref,
-    out_w_ref,
-    out_hbm,
-    plane_ref,
-    mix_ref,
-    out_ref,
-    sems,
-):
-    rows, half, depth, channels = early_ref.shape
-    across = 2 * half
+def last_kernel(axis, second, *refs):
+    if second:
+        feature_ref, done_ref, mix_ref, pooled_ref, yz_ref, gain_ref, in_ref, out_w_ref = refs[:8]
+        out_hbm, plane_ref, out_ref, sems = refs[8:]
+        across = feature_ref.shape[1]
+    else:
+        early_ref, late_ref, strip_ref, xz_ref, pooled_ref, yz_ref, gain_ref, in_ref, out_w_ref = refs[:9]
+        feature_ref, out_ref, mix_ref, plane_ref = refs[9:]
+        across = 2 * early_ref.shape[1]
+    rows, (depth, channels) = feature_ref.shape[0], feature_ref.shape[2:]
+    half, quarter, span = across // 2, across // 4, out_ref.shape[2]
     index = lax.axis_index(axis)
     side = lax.rem(index, 2)
     kept = lax.rem(index // 2, 2)
@@ -238,10 +230,25 @@
     mine = 0
     for bit in order:
         mine = mine * 2 + lax.rem(index // (1 << bit), 2)
-    blank = jnp.zeros((depth, channels), BF)
-    plane_ref[0] = blank
-    plane_ref[across + 1] = blank
-    for k in range(1 << bits):
+    copies = []
+    if second:
+        for row in range(rows):
+            for h in range(2):
+                place = pl.ds(h * half + side * quarter, quarter)
+                copies.append(
+                    pltpu.make_async_copy(
+                        done_ref.at[row, h], out_hbm.at[row, place], sems.at[0, row, h]
+                    )
+                )
+                copies[-1].start()
+        blank = jnp.zeros((depth, channels), BF)
+        plane_ref[0] = blank
+        plane_ref[across + 1] = blank
+    else:
+        plane_ref[...] = jnp.zeros_like(plane_ref)
+        feature_ref[:, pl.ds((1 - kept) * half, half)] = early_ref[...]
+        feature_ref[:, pl.ds(kept * half, half)] = late_ref[...]
+    for k in range(pooled_ref.shape[0] // block):
         other = 0
         for bit in order:
             other = other * 2 + (k >> (bits - 1 - bit)) % 2
@@ -255,47 +262,56 @@
         parts = [total[:, c * channels : (c + 1) * channels] for c in range(3)]
         return shift_depth(*parts, shape).astype(BF).astype(F32)
 
-    taps = (2 * side, 1, 2 - 2 * side)
-    strip = strip_ref[...]
-    mixed = plane_product(
-        [strip[a : a + rows].reshape(-1, channels) for a in range(3)],
-        [[xz_ref[taps[a], c] for c in range(3)] for a in range(3)],
-        (rows, depth, channels),
-    )
-    mix_ref[side] = mixed[0]
-    mix_ref[1 - side] = mixed[1]
-    gain = gain_ref[...]
-    span = out_ref.shape[2]
-    copies = []
-    for step in range(across // span):
-        early = step * span < half
-        feature_ref = early_ref if early else late_ref
-        at = step * span % half
-        start = (1 - kept if early else kept) * half + at
-        plane = plane_product(
-            [plane_ref[pl.ds(start + b, span)].reshape(-1, channels) for b in range(3)],
-            [[yz_ref[b, c] for c in range(3)] for b in range(3)],
-            (span, depth, channels),
+    if not second:
+        taps = (2 * side, 1, 2 - 2 * side)
+        strip = strip_ref[...]
+        mixed = plane_product(
+            [strip[a : a + rows].reshape(-1, channels) for a in range(3)],
+            [[xz_ref[taps[a], c] for c in range(3)] for a in range(3)],
+            (rows, depth, channels),
         )
-        feature = feature_ref[:, at : at + span].astype(F32)
-        mixing = plane[None] + jnp.stack([mix_ref[row] for row in range(rows)])[:, None]
-        joined = (feature * mixing).reshape(-1, channels)
-        mean = jnp.mean(joined * joined, axis=-1, keepdims=True)
-        normed = (joined * lax.rsqrt(mean + 1e-06) * gain).astype(BF)
-        hidden = jnp.dot(normed, in_ref[...], preferred_element_type=F32)
-        hidden = twice_activate(hidden).astype(BF)
-        update = 0.5 * jnp.dot(hidden, out_w_ref[...], preferred_element_type=F32)
-        encoded = (joined + update).astype(BF).reshape(rows, span, depth, channels)
+        mix_ref[side] = mixed[0]
+        mix_ref[1 - side] = mixed[1]
+    if second:
+        starts = [
+            jnp.clip(h * half + (1 - side) * quarter - 1, 0, across - span) for h in range(2)
+        ]
+    else:
+        starts = [h * half + side * quarter for h in range(2)]
+    plane = plane_product(
+        [
+            jnp.concatenate([plane_ref[pl.ds(at + b, span)].reshape(-1, channels) for at in starts])
+            for b in range(3)
+        ],
+        [[yz_ref[b, c] for c in range(3)] for b in range(3)],
+        (2 * span, depth, channels),
+    )
+    feature = jnp.concatenate([feature_ref[:, pl.ds(at, span)] for at in starts], axis=1)
+    mixing = plane[None] + jnp.stack([mix_ref[row] for row in range(rows)])[:, None]
+    joined = (feature.astype(F32) * mixing).reshape(-1, channels)
+    mean = jnp.mean(joined * joined, axis=-1, keepdims=True)
+    normed = (joined * lax.rsqrt(mean + 1e-06) * gain_ref[...]).astype(BF)
+    hidden = jnp.dot(normed, in_ref[...], preferred_element_type=F32)
+    hidden = twice_activate(hidden).astype(BF)
+    update = 0.5 * jnp.dot(hidden, out_w_ref[...], preferred_element_type=F32)
+    encoded = (joined + update).astype(BF).reshape(rows, 2, span, depth, channels)
+    for row in range(rows):
+        for h in range(2):
+            out_ref[row, h] = encoded[row, h]
+    if second:
+        for copy in copies:
+            copy.wait()
+        copies = []
         for row in range(rows):
-            out_ref[row, step] = encoded[row]
-            copies.append(
-                pltpu.make_async_copy(
-                    out_ref.at[row, step], out_hbm.at[row, pl.ds(start, span)], sems.at[row, step]
+            for h, at in enumerate(starts):
+                copies.append(
+                    pltpu.make_async_copy(
+                        out_ref.at[row, h], out_hbm.at[row, pl.ds(at, span)], sems.at[1, row, h]
+                    )
                 )
-            )
-            copies[-1].start()
-    for copy in copies:
-        copy.wait()
+                copies[-1].start()
+        for copy in copies:
+            copy.wait()
 
 
 def swap(values, axis, mask):
@@ -320,13 +336,17 @@
     return [message[k * size : (k + 1) * size] for k in range(3)]
 
 
-def kernel_call(body, outs, scratch, flops, *operands, spaces=None, results=pltpu.VMEM):
+def kernel_call(body, outs, scratch, flops, *operands, spaces=None, results=None):
     moved = sum(o.size * o.dtype.itemsize for o in operands)
     return pl.pallas_call(
         body,
         out_shape=outs,
         in_specs=[pl.BlockSpec(memory_space=m) for m in spaces or [pltpu.VMEM] * len(operands)],
-        out_specs=jax.tree.map(lambda _: pl.BlockSpec(memory_space=results), outs),
+        out_specs=jax.tree.map(
+            lambda _, space: pl.BlockSpec(memory_space=space),
+            outs,
+            results or jax.tree.map(lambda _: pltpu.VMEM, outs),
+        ),
         scratch_shapes=scratch,
         compiler_params=pltpu.CompilerParams(vmem_limit_bytes=14 * 1024 * 1024),
         cost_estimate=pl.CostEstimate(flops=flops, bytes_accessed=moved, transcendentals=0),
@@ -458,29 +478,47 @@
     got = swap(jnp.concatenate([pooled, row[None]], axis=0), axis, masks[1])
     before = jnp.where((index == 0) | (index == devices - 1), jnp.zeros_like(row), got[-1])
     pooled = jnp.concatenate([pooled, got[:-1]], axis=0)
-    pooled = jnp.concatenate([pooled, swap(pooled, axis, masks[0])], axis=0)
     strip = jnp.concatenate([before[None], strip, beyond[None]], axis=0)
-    span = min(64, half)
-    return kernel_call(
-        functools.partial(last_kernel, axis),
-        jax.ShapeDtypeStruct(voxels.shape, BF),
-        [
-            pltpu.VMEM((across + 2, depth, channels), BF),
-            pltpu.VMEM((rows, depth, channels), F32),
-            pltpu.VMEM((rows, across // span, span, depth, channels), BF),
-            pltpu.SemaphoreType.DMA((rows, across // span)),
-        ],
-        flops // 4,
-        early,
-        late,
-        pooled,
-        strip,
+    weights = (
         plane_yz_w.reshape(3, 3, channels, channels),
-        plane_xz_w.reshape(3, 3, channels, channels),
         norm_gain.reshape(1, channels),
         mlp_in,
         mlp_out,
-        results=pl.ANY,
+    )
+    whole = jax.ShapeDtypeStruct(voxels.shape, BF)
+    plane = pltpu.VMEM((across + 2, depth, channels), BF)
+    other = swap(pooled, axis, masks[0])
+    feature, done, mix = kernel_call(
+        functools.partial(last_kernel, axis, False),
+        (
+            whole,
+            jax.ShapeDtypeStruct((rows, 2, quarter, depth, channels), BF),
+            jax.ShapeDtypeStruct((rows, depth, channels), F32),
+        ),
+        [plane],
+        flops // 8,
+        early,
+        late,
+        strip,
+        plane_xz_w.reshape(3, 3, channels, channels),
+        pooled,
+        *weights,
+    )
+    return kernel_call(
+        functools.partial(last_kernel, axis, True),
+        whole,
+        [
+            plane,
+            pltpu.VMEM((rows, 2, quarter + 2, depth, channels), BF),
+            pltpu.SemaphoreType.DMA((2, rows, 2)),
+        ],
+        flops // 8,
+        feature,
+        done,
+        mix,
+        jnp.concatenate([pooled, other], axis=0),
+        *weights,
+        results=pltpu.HBM,
     )
 
 

time: 55.9 us -> 55.5 us (level)
  waiting for transfers between devices: 21.8 us -> 20.5 us
    ppermute x9, waiting for transfers between devices: 17 us -> 15.7 us  [swap(): return lax.ppermute(values, axis, [(i, i ^ mask) for i in range(devices)])]
    pallas_call x5 -> x6, Pallas kernels: 12.1 us -> 12.6 us  [kernel_call(): pl.pallas_call(body, out_shape=outs, in_specs=[pl.BlockSpec(memory_space=...]
  transfers between devices with their start and end apart: 11 -> 11, of which waited for: 7 -> 6; matrix products, arithmetic and copies ran while one was open for 0% -> 0% of each run, Pallas kernels for 8% -> 11%
where the time goes in v7:
time: 55.5 us; the launch traced here: 55 us
  waiting for transfers between devices  20.5 us (37%)
  starting transfers between devices  19.9 us (36%)
  Pallas kernels  12.6 us (23%)
  local copies, waits for them, and re-layouts  1.18 us (2%)
    ppermute x9, starting transfers between devices, swap(): return lax.ppermute(values, axis, [(i, i ^ mask) for i in range(devices)])  15.8 us
    ppermute x9, waiting for transfers between devices, swap(): return lax.ppermute(values, axis, [(i, i ^ mask) for i in range(devices)])  15.7 us
    pallas_call x6, Pallas kernels, kernel_call(): pl.pallas_call(body, out_shape=outs, in_specs=[pl.BlockSpec(memory_space=...  12.6 us
    ppermute x1, waiting for transfers between devices, on_device(): far1 = lax.ppermute(cuts[1], (others, axis), pairs)  4.82 us
    ppermute x1, starting transfers between devices, on_device(): far0 = lax.ppermute(cuts[0], (others, axis), pairs)  2.64 us
    ppermute x1, starting transfers between devices, on_device(): far1 = lax.ppermute(cuts[1], (others, axis), pairs)  1.49 us
    unnamed x22, local copies, waits for them, and re-layouts  1.13 us
  transfers between devices with their start and end apart: 11, of which 6 were waited for; matrix products, arithmetic and copies ran while one was open for 0% of the time, Pallas kernels for 11%

profile of v7, /device:TPU:0, one launch (start us, length us, event | category | flops | bytes accessed | tf_op | source)
XLA Modules:
  0.0 55.0 jit_solution(8947834747810909367)
XLA Ops:
  0.0 0.5 collective-permute-start
  0.5 1.1 %copy-done.7 = bf16[2,128,8,128]{3,2,1,0:T(8,128)(2,1)S(1)} copy-done((bf16[2,128,8,128]{3,2,1,0:T(8,128)(2,1)S(1)}, bf16[2,128,8,128]{3,2,1,0:T(8,128)(2,1)}, u32[]{:S(2)}) %copy-start.7) | copy-done | bytes 524312
  1.6 0.1 shard_map.109
  1.6 2.6 %collective-permute-start.1 = (bf16[2,66,8,128]{3,2,1,0:T(8,128)(2,1)S(1)}, bf16[2,66,8,128]{3,2,1,0:T(8,128)(2,1)S(1)}, u32[]{:S(2)}, u32[]{:S(2)}) collective-permute-start(bf16[2,66,8,128]{3,2,1,0:T(8,128)(2,1)S(1)} %get-tuple-element.24.cut0_ref), channel_id=1, source_target_pairs={{0,16},{15,31},{1,2},{2,1},{3,4},{4,3},{5,6},{6,5},{7,8},{8,7},{9,... | collective-permute-start | bytes 811016 | tf_op jit(solution)/shard_map/ppermute | solution.py:400
  4.3 0.0 copy-start.8
  4.3 0.0 copy-start.10
  4.3 4.5 %shard_map.110 = (f32[2,130,8,128]{3,2,1,0:T(8,128)S(1)}, f32[2,128,8,128]{3,2,1,0:T(8,128)S(1)}) custom-call(bf16[2,66,8,128]{3,2,1,0:T(8,128)(2,1)S(1)} %get-tuple-element.24.cut0_ref, bf16[2,66,8,128]{3,2,1,0:T(8,128)(2,1)S(1)} %get-tuple-element.25.cut1_ref, bf16[2,128,8,128]{3,2,1,0:T(8,128)(2,1)S(1)} %collective-permute-done.near_ref, ...), custom_call_target="tpu_custom_call" | custom-call | flops 3623878656 | bytes 2834432 | tf_op jit(solution)/shard_map/pallas_call | solution.py:341
  8.9 2.0 %shard_map.111 = (bf16[2,64,8,128]{3,2,1,0:T(8,128)(2,1)S(1)}, bf16[96,8,128]{2,1,0:T(8,128)(2,1)S(1)}, f32[3,32,8,128]{3,2,1,0:T(8,128)S(1)}) custom-call(f32[2,130,8,128]{3,2,1,0:T(8,128)S(1)} %get-tuple-element.26.refs_0_, f32[2,128,8,128]{3,2,1,0:T(8,128)S(1)} %get-tuple-element.27.refs_1_, bf16[2,66,8,128]{3,2,1,0:T(8,128)(2,1)S(1)} %collective-permute-done.1.refs_2_, ...), custom_call_target="tpu_custom_call" | custom-call | flops 1358954496 | bytes 4227072 | tf_op jit(solution)/shard_map/pallas_call | solution.py:341
  10.9 1.9 %collective-permute-start.3 = (bf16[96,8,128]{2,1,0:T(8,128)(2,1)S(1)}, bf16[96,8,128]{2,1,0:T(8,128)(2,1)S(1)}, u32[]{:S(2)}, u32[]{:S(2)}) collective-permute-start(bf16[96,8,128]{2,1,0:T(8,128)(2,1)S(1)} %get-tuple-element.30), channel_id=1, source_target_pairs={{0,1},{1,0},{2,3},{3,2},{4,5},{5,4},{6,7},{7,6},{8,9},{9,8},{10,11... | collective-permute-start | bytes 589832 | tf_op jit(solution)/shard_map/ppermute | solution.py:319
  12.8 1.5 %collective-permute-start.2 = (bf16[2,66,8,128]{3,2,1,0:T(8,128)(2,1)S(1)}, bf16[2,66,8,128]{3,2,1,0:T(8,128)(2,1)S(1)}, u32[]{:S(2)}, u32[]{:S(2)}) collective-permute-start(bf16[2,66,8,128]{3,2,1,0:T(8,128)(2,1)S(1)} %get-tuple-element.25.cut1_ref), channel_id=1, source_target_pairs={{0,16},{15,31},{1,2},{2,1},{3,4},{4,3},{5,6},{6,5},{7,8},{8,7},{9,... | collective-permute-start | bytes 811016 | tf_op jit(solution)/shard_map/ppermute | solution.py:401
  14.3 0.1 fusion.16
  14.4 4.8 %collective-permute-done.2.refs_2_ = bf16[2,66,8,128]{3,2,1,0:T(8,128)(2,1)S(1)} collective-permute-done((bf16[2,66,8,128]{3,2,1,0:T(8,128)(2,1)S(1)}, bf16[2,66,8,128]{3,2,1,0:T(8,128)(2,1)S(1)}, u32[]{:S(2)}, u32[]{:S(2)}) %collective-permute-start.2) | collective-permute-done | bytes 270368 | tf_op jit(solution)/shard_map/ppermute | solution.py:401
  19.3 2.3 %shard_map.112 = (bf16[2,64,8,128]{3,2,1,0:T(8,128)(2,1)S(1)}, bf16[98,8,128]{2,1,0:T(8,128)(2,1)S(1)}, f32[3,32,8,128]{3,2,1,0:T(8,128)S(1)}, bf16[2,8,128]{2,1,0:T(8,128)(2,1)S(1)}) custom-call(f32[2,130,8,128]{3,2,1,0:T(8,128)S(1)} %get-tuple-element.26.refs_0_, f32[2,128,8,128]{3,2,1,0:T(8,128)S(1)} %get-tuple-element.27.refs_1_, ...), custom_call_target="tpu_custom_call" | custom-call | flops 1358954496 | bytes 4489216 | tf_op jit(solution)/shard_map/pallas_call | solution.py:341
  21.6 2.5 %collective-permute-start.4 = (bf16[98,8,128]{2,1,0:T(8,128)(2,1)S(1)}, bf16[98,8,128]{2,1,0:T(8,128)(2,1)S(1)}, u32[]{:S(2)}, u32[]{:S(2)}) collective-permute-start(bf16[98,8,128]{2,1,0:T(8,128)(2,1)S(1)} %get-tuple-element.34), channel_id=1, source_target_pairs={{0,1},{1,0},{2,3},{3,2},{4,5},{5,4},{6,7},{7,6},{8,9},{9,8},{10,11... | collective-permute-start | bytes 602120 | tf_op jit(solution)/shard_map/ppermute | solution.py:319
  24.1 2.4 %collective-permute-start.5 = (bf16[96,8,128]{2,1,0:T(8,128)(2,1)S(1)}, bf16[96,8,128]{2,1,0:T(8,128)(2,1)S(1)}, u32[]{:S(2)}, u32[]{:S(2)}) collective-permute-start(bf16[96,8,128]{2,1,0:T(8,128)(2,1)S(1)} %pad_maximum_fusion.1), channel_id=1, source_target_pairs={{0,2},{1,3},{2,0},{3,1},{4,6},{5,7},{6,4},{7,5},{8,10},{9,11},{10,... | collective-permute-start | bytes 589832 | tf_op jit(solution)/shard_map/ppermute | solution.py:319
  26.5 5.5 %collective-permute-done.5 = bf16[96,8,128]{2,1,0:T(8,128)(2,1)S(1)} collective-permute-done((bf16[96,8,128]{2,1,0:T(8,128)(2,1)S(1)}, bf16[96,8,128]{2,1,0:T(8,128)(2,1)S(1)}, u32[]{:S(2)}, u32[]{:S(2)}) %collective-permute-start.5) | collective-permute-done | bytes 196640 | tf_op jit(solution)/shard_map/ppermute | solution.py:319
  32.0 0.1 convert_maximum_fusion
  32.2 0.0 copy-start
  32.2 0.0 copy-start.3
  32.3 0.0 copy-start.4
  32.3 1.8 %collective-permute-start.6 = (bf16[49,8,128]{2,1,0:T(8,128)(2,1)S(1)}, bf16[49,8,128]{2,1,0:T(8,128)(2,1)S(1)}, u32[]{:S(2)}, u32[]{:S(2)}) collective-permute-start(bf16[49,8,128]{2,1,0:T(8,128)(2,1)S(1)} %pad_maximum_fusion.3), channel_id=1, source_target_pairs={{0,4},{1,5},{2,6},{3,7},{4,0},{5,1},{6,2},{7,3},{8,12},{9,13},{10,... | collective-permute-start | bytes 301064 | tf_op jit(solution)/shard_map/ppermute | solution.py:319
  34.1 2.9 %collective-permute-done.6 = bf16[49,8,128]{2,1,0:T(8,128)(2,1)S(1)} collective-permute-done((bf16[49,8,128]{2,1,0:T(8,128)(2,1)S(1)}, bf16[49,8,128]{2,1,0:T(8,128)(2,1)S(1)}, u32[]{:S(2)}, u32[]{:S(2)}) %collective-permute-start.6) | collective-permute-done | bytes 100384 | tf_op jit(solution)/shard_map/ppermute | solution.py:319
  37.1 2.8 %collective-permute-start.7 = (bf16[49,8,128]{2,1,0:T(8,128)(2,1)S(1)}, bf16[49,8,128]{2,1,0:T(8,128)(2,1)S(1)}, u32[]{:S(2)}, u32[]{:S(2)}) collective-permute-start(bf16[49,8,128]{2,1,0:T(8,128)(2,1)S(1)} %pad_maximum_fusion.4), channel_id=1, source_target_pairs={{0,8},{1,9},{2,10},{3,11},{4,12},{5,13},{6,14},{7,15},{8,0},{9,1},... | collective-permute-start | bytes 301064 | tf_op jit(solution)/shard_map/ppermute | solution.py:319
  39.9 2.8 %collective-permute-done.7 = bf16[49,8,128]{2,1,0:T(8,128)(2,1)S(1)} collective-permute-done((bf16[49,8,128]{2,1,0:T(8,128)(2,1)S(1)}, bf16[49,8,128]{2,1,0:T(8,128)(2,1)S(1)}, u32[]{:S(2)}, u32[]{:S(2)}) %collective-permute-start.7) | collective-permute-done | bytes 100384 | tf_op jit(solution)/shard_map/ppermute | solution.py:319
  42.7 0.1 divide_convert_fusion
  42.8 2.0 %collective-permute-start.8 = (bf16[16,8,128]{2,1,0:T(8,128)(2,1)S(1)}, bf16[16,8,128]{2,1,0:T(8,128)(2,1)S(1)}, u32[]{:S(2)}, u32[]{:S(2)}) collective-permute-start(bf16[16,8,128]{2,1,0:T(8,128)(2,1)S(1)} %divide_convert_fusion), channel_id=1, source_target_pairs={{0,4},{1,5},{2,6},{3,7},{4,0},{5,1},{6,2},{7,3},{8,12},{9,13},{10,... | collective-permute-start | bytes 98312 | tf_op jit(solution)/shard_map/ppermute | solution.py:319
  44.8 2.0 %collective-permute-done.8 = bf16[16,8,128]{2,1,0:T(8,128)(2,1)S(1)} collective-permute-done((bf16[16,8,128]{2,1,0:T(8,128)(2,1)S(1)}, bf16[16,8,128]{2,1,0:T(8,128)(2,1)S(1)}, u32[]{:S(2)}, u32[]{:S(2)}) %collective-permute-start.8) | collective-permute-done | bytes 32800 | tf_op jit(solution)/shard_map/ppermute | solution.py:319
  46.8 1.8 %collective-permute-start.9 = (bf16[33,8,128]{2,1,0:T(8,128)(2,1)S(1)}, bf16[33,8,128]{2,1,0:T(8,128)(2,1)S(1)}, u32[]{:S(2)}, u32[]{:S(2)}) collective-permute-start(bf16[33,8,128]{2,1,0:T(8,128)(2,1)S(1)} %pad_maximum_fusion.5), channel_id=1, source_target_pairs={{0,2},{1,3},{2,0},{3,1},{4,6},{5,7},{6,4},{7,5},{8,10},{9,11},{10,... | collective-permute-start | bytes 202760 | tf_op jit(solution)/shard_map/ppermute | solution.py:319
  48.5 2.5 %collective-permute-done.9 = bf16[33,8,128]{2,1,0:T(8,128)(2,1)S(1)} collective-permute-done((bf16[33,8,128]{2,1,0:T(8,128)(2,1)S(1)}, bf16[33,8,128]{2,1,0:T(8,128)(2,1)S(1)}, u32[]{:S(2)}, u32[]{:S(2)}) %collective-permute-start.9) | collective-permute-done | bytes 67616 | tf_op jit(solution)/shard_map/ppermute | solution.py:319
  51.1 0.1 collective-permute-start.10
  51.2 1.4 %shard_map.113 = (bf16[2,128,8,128]{3,2,1,0:T(8,128)(2,1)S(1)}, bf16[2,2,32,8,128]{4,3,2,1,0:T(8,128)(2,1)S(1)}, f32[2,8,128]{2,1,0:T(8,128)S(1)}) custom-call(bf16[2,64,8,128]{3,2,1,0:T(8,128)(2,1)S(1)} %get-tuple-element.31.refs_8_.refs_0_, bf16[2,64,8,128]{3,2,1,0:T(8,128)(2,1)S(1)} %get-tuple-element.32.refs_1_, ...), custom_call_target="tpu_custom_call" | custom-call | flops 226492416 | bytes 1516032 | tf_op jit(solution)/shard_map/pallas_call | solution.py:341
  52.7 2.3 %shard_map.114 = bf16[2,128,8,128]{3,2,1,0:T(8,128)(2,1)} custom-call(bf16[2,128,8,128]{3,2,1,0:T(8,128)(2,1)S(1)} %get-tuple-element.40.refs_0_, bf16[2,2,32,8,128]{4,3,2,1,0:T(8,128)(2,1)S(1)} %get-tuple-element.41.refs_1_, f32[2,8,128]{2,1,0:T(8,128)S(1)} %get-tuple-element.42.refs_2_, bf16[128,8,128]{2,1,0:T(8,128)(2,1)S(1)} %pad_maximum_fusion.refs_3_, ...), custom_call_target="tpu_custom_call" | custom-call | flops 226492416 | bytes 1614336 | tf_op jit(solution)/shard_map/pallas_call | solution.py:341
  (40 shorter events, 0.3 us)
Async XLA Ops:
  0.0 4.3 %copy-start.5 = (bf16[27,128,128]{2,1,0:T(8,128)(2,1)S(1)}, bf16[27,128,128]{2,1,0:T(8,128)(2,1)}, u32[]{:S(2)}) copy-start(bf16[27,128,128]{2,1,0:T(8,128)(2,1)} %param.13) | copy-start | bytes 2654212
  0.0 4.3 %copy-start.6 = (bf16[27,128,128]{2,1,0:T(8,128)(2,1)S(1)}, bf16[27,128,128]{2,1,0:T(8,128)(2,1)}, u32[]{:S(2)}) copy-start(bf16[27,128,128]{2,1,0:T(8,128)(2,1)} %param.14) | copy-start | bytes 2654212
  0.0 4.3 %collective-permute-start = (bf16[2,128,8,128]{3,2,1,0:T(8,128)(2,1)}, bf16[2,128,8,128]{3,2,1,0:T(8,128)(2,1)S(1)}, u32[]{:S(2)}, u32[]{:S(2)}) collective-permute-start(bf16[2,128,8,128]{3,2,1,0:T(8,128)(2,1)} %own_ref.1), channel_id=1, source_target_pairs={{0,1},{1,0},{2,3},{3,2},{4,5},{5,4},{6,7},{7,6},{8,9},{9,8},{10,11... | collective-permute-start | bytes 1572872 | tf_op jit(solution)/shard_map/ppermute | solution.py:319
  0.5 1.1 %copy-start.7 = (bf16[2,128,8,128]{3,2,1,0:T(8,128)(2,1)S(1)}, bf16[2,128,8,128]{3,2,1,0:T(8,128)(2,1)}, u32[]{:S(2)}) copy-start(bf16[2,128,8,128]{3,2,1,0:T(8,128)(2,1)} %own_ref.1) | copy-start | bytes 1572868
  1.6 7.2 %collective-permute-start.1 = (bf16[2,66,8,128]{3,2,1,0:T(8,128)(2,1)S(1)}, bf16[2,66,8,128]{3,2,1,0:T(8,128)(2,1)S(1)}, u32[]{:S(2)}, u32[]{:S(2)}) collective-permute-start(bf16[2,66,8,128]{3,2,1,0:T(8,128)(2,1)S(1)} %get-tuple-element.24.cut0_ref), channel_id=1, source_target_pairs={{0,16},{15,31},{1,2},{2,1},{3,4},{4,3},{5,6},{6,5},{7,8},{8,7},{9,... | collective-permute-start | bytes 811016 | tf_op jit(solution)/shard_map/ppermute | solution.py:400
  4.3 4.6 %copy-start.8 = (bf16[128,128]{1,0:T(8,128)(2,1)S(1)}, bf16[128,128]{1,0:T(8,128)(2,1)}, u32[]{:S(2)}) copy-start(bf16[128,128]{1,0:T(8,128)(2,1)} %refs_5_.3) | copy-start | bytes 98308
  4.3 4.6 %copy-start.9 = (bf16[128,128]{1,0:T(8,128)(2,1)S(1)}, bf16[128,128]{1,0:T(8,128)(2,1)}, u32[]{:S(2)}) copy-start(bf16[128,128]{1,0:T(8,128)(2,1)} %refs_6_.4) | copy-start | bytes 98308
  4.3 4.6 %copy-start.10 = (f32[2,128,8]{1,2,0:T(8,128)S(1)}, f32[2,128,8]{1,2,0:T(8,128)}, u32[]{:S(2)}) copy-start(f32[2,128,8]{1,2,0:T(8,128)} %param.12) | copy-start | bytes 24580
  10.9 3.4 %collective-permute-start.3 = (bf16[96,8,128]{2,1,0:T(8,128)(2,1)S(1)}, bf16[96,8,128]{2,1,0:T(8,128)(2,1)S(1)}, u32[]{:S(2)}, u32[]{:S(2)}) collective-permute-start(bf16[96,8,128]{2,1,0:T(8,128)(2,1)S(1)} %get-tuple-element.30), channel_id=1, source_target_pairs={{0,1},{1,0},{2,3},{3,2},{4,5},{5,4},{6,7},{7,6},{8,9},{9,8},{10,11... | collective-permute-start | bytes 589832 | tf_op jit(solution)/shard_map/ppermute | solution.py:319
  12.8 6.5 %collective-permute-start.2 = (bf16[2,66,8,128]{3,2,1,0:T(8,128)(2,1)S(1)}, bf16[2,66,8,128]{3,2,1,0:T(8,128)(2,1)S(1)}, u32[]{:S(2)}, u32[]{:S(2)}) collective-permute-start(bf16[2,66,8,128]{3,2,1,0:T(8,128)(2,1)S(1)} %get-tuple-element.25.cut1_ref), channel_id=1, source_target_pairs={{0,16},{15,31},{1,2},{2,1},{3,4},{4,3},{5,6},{6,5},{7,8},{8,7},{9,... | collective-permute-start | bytes 811016 | tf_op jit(solution)/shard_map/ppermute | solution.py:401
  21.6 10.4 %collective-permute-start.4 = (bf16[98,8,128]{2,1,0:T(8,128)(2,1)S(1)}, bf16[98,8,128]{2,1,0:T(8,128)(2,1)S(1)}, u32[]{:S(2)}, u32[]{:S(2)}) collective-permute-start(bf16[98,8,128]{2,1,0:T(8,128)(2,1)S(1)} %get-tuple-element.34), channel_id=1, source_target_pairs={{0,1},{1,0},{2,3},{3,2},{4,5},{5,4},{6,7},{7,6},{8,9},{9,8},{10,11... | collective-permute-start | bytes 602120 | tf_op jit(solution)/shard_map/ppermute | solution.py:319
  24.1 7.9 %collective-permute-start.5 = (bf16[96,8,128]{2,1,0:T(8,128)(2,1)S(1)}, bf16[96,8,128]{2,1,0:T(8,128)(2,1)S(1)}, u32[]{:S(2)}, u32[]{:S(2)}) collective-permute-start(bf16[96,8,128]{2,1,0:T(8,128)(2,1)S(1)} %pad_maximum_fusion.1), channel_id=1, source_target_pairs={{0,2},{1,3},{2,0},{3,1},{4,6},{5,7},{6,4},{7,5},{8,10},{9,11},{10,... | collective-permute-start | bytes 589832 | tf_op jit(solution)/shard_map/ppermute | solution.py:319
  32.2 19.0 %copy-start = (bf16[9,128,128]{2,1,0:T(8,128)(2,1)S(1)}, bf16[9,128,128]{2,1,0:T(8,128)(2,1)}, u32[]{:S(2)}) copy-start(bf16[9,128,128]{2,1,0:T(8,128)(2,1)} %param.17) | copy-start | bytes 884740
  32.2 19.0 %copy-start.1 = (bf16[128,512]{1,0:T(8,128)(2,1)S(1)}, bf16[128,512]{1,0:T(8,128)(2,1)}, u32[]{:S(2)}) copy-start(bf16[128,512]{1,0:T(8,128)(2,1)} %refs_6_.5) | copy-start | bytes 393220
  32.2 19.0 %copy-start.2 = (bf16[512,128]{1,0:T(8,128)(2,1)S(1)}, bf16[512,128]{1,0:T(8,128)(2,1)}, u32[]{:S(2)}) copy-start(bf16[512,128]{1,0:T(8,128)(2,1)} %refs_7_.3) | copy-start | bytes 393220
  32.2 19.0 %copy-start.3 = (bf16[9,128,128]{2,1,0:T(8,128)(2,1)S(1)}, bf16[9,128,128]{2,1,0:T(8,128)(2,1)}, u32[]{:S(2)}) copy-start(bf16[9,128,128]{2,1,0:T(8,128)(2,1)} %param.18) | copy-start | bytes 884740
  32.3 19.0 %copy-start.4 = (f32[128]{0:T(128)S(1)}, f32[128]{0:T(128)}, u32[]{:S(2)}) copy-start(f32[128]{0:T(128)} %param.19) | copy-start | bytes 1540
  32.3 4.7 %collective-permute-start.6 = (bf16[49,8,128]{2,1,0:T(8,128)(2,1)S(1)}, bf16[49,8,128]{2,1,0:T(8,128)(2,1)S(1)}, u32[]{:S(2)}, u32[]{:S(2)}) collective-permute-start(bf16[49,8,128]{2,1,0:T(8,128)(2,1)S(1)} %pad_maximum_fusion.3), channel_id=1, source_target_pairs={{0,4},{1,5},{2,6},{3,7},{4,0},{5,1},{6,2},{7,3},{8,12},{9,13},{10,... | collective-permute-start | bytes 301064 | tf_op jit(solution)/shard_map/ppermute | solution.py:319
  37.1 5.6 %collective-permute-start.7 = (bf16[49,8,128]{2,1,0:T(8,128)(2,1)S(1)}, bf16[49,8,128]{2,1,0:T(8,128)(2,1)S(1)}, u32[]{:S(2)}, u32[]{:S(2)}) collective-permute-start(bf16[49,8,128]{2,1,0:T(8,128)(2,1)S(1)} %pad_maximum_fusion.4), channel_id=1, source_target_pairs={{0,8},{1,9},{2,10},{3,11},{4,12},{5,13},{6,14},{7,15},{8,0},{9,1},... | collective-permute-start | bytes 301064 | tf_op jit(solution)/shard_map/ppermute | solution.py:319
  42.8 4.0 %collective-permute-start.8 = (bf16[16,8,128]{2,1,0:T(8,128)(2,1)S(1)}, bf16[16,8,128]{2,1,0:T(8,128)(2,1)S(1)}, u32[]{:S(2)}, u32[]{:S(2)}) collective-permute-start(bf16[16,8,128]{2,1,0:T(8,128)(2,1)S(1)} %divide_convert_fusion), channel_id=1, source_target_pairs={{0,4},{1,5},{2,6},{3,7},{4,0},{5,1},{6,2},{7,3},{8,12},{9,13},{10,... | collective-permute-start | bytes 98312 | tf_op jit(solution)/shard_map/ppermute | solution.py:319
  46.8 4.3 %collective-permute-start.9 = (bf16[33,8,128]{2,1,0:T(8,128)(2,1)S(1)}, bf16[33,8,128]{2,1,0:T(8,128)(2,1)S(1)}, u32[]{:S(2)}, u32[]{:S(2)}) collective-permute-start(bf16[33,8,128]{2,1,0:T(8,128)(2,1)S(1)} %pad_maximum_fusion.5), channel_id=1, source_target_pairs={{0,2},{1,3},{2,0},{3,1},{4,6},{5,7},{6,4},{7,5},{8,10},{9,11},{10,... | collective-permute-start | bytes 202760 | tf_op jit(solution)/shard_map/ppermute | solution.py:319
  51.1 1.6 %collective-permute-start.10 = (bf16[64,8,128]{2,1,0:T(8,128)(2,1)S(1)}, bf16[64,8,128]{2,1,0:T(8,128)(2,1)S(1)}, u32[]{:S(2)}, u32[]{:S(2)}) collective-permute-start(bf16[64,8,128]{2,1,0:T(8,128)(2,1)S(1)} %pad_maximum_fusion.2.refs_4_), channel_id=1, source_target_pairs={{0,1},{1,0},{2,3},{3,2},{4,5},{5,4},{6,7},{7,6},{8,9},{9,8},{10,11... | collective-permute-start | bytes 393224 | tf_op jit(solution)/shard_map/ppermute | solution.py:319

commit v8 on v7

--- a/solution.py
+++ b/solution.py
@@ -81,48 +81,44 @@
         rows_ref[row, length - width :] = blank
 
 
-def cut_kernel(axis, own_ref, first_ref, second_ref, sems):
+def cut_kernel(axis, second, own_ref, cut_ref, sem):
     half = own_ref.shape[1] // 2
     kept = lax.rem(lax.axis_index(axis) // 2, 2)
-    fetches = []
-    for k, (at, target) in enumerate(((kept, first_ref), (1 - kept, second_ref))):
-        place = pl.ds(at * (half - 2), half + 2)
-        fetches.append(pltpu.make_async_copy(own_ref.at[:, place], target, sems.at[k]))
-    for fetch in fetches:
-        fetch.start()
-    for fetch in fetches:
-        fetch.wait()
-
-
-def first_kernel(axis, cut0_ref, cut1_ref, near_ref, w1_ref, w2_ref, edge_ref, part_ref, rows_ref, mid_ref):
-    across = near_ref.shape[1]
-    span = across // 2
-    index = lax.axis_index(axis)
-    side = lax.rem(index, 2)
-    kept = lax.rem(index // 2, 2)
-    clear_ends(rows_ref, 1)
-    clear_ends(mid_ref, 1)
-    clear_ends(edge_ref, 1)
+    at = 1 - kept if second else kept
+    fetch = pltpu.make_async_copy(own_ref.at[:, pl.ds(at * (half - 2), half + 2)], cut_ref, sem)
+    fetch.start()
+    fetch.wait()
+
+
+def half_of(axis, second):
+    kept = lax.rem(lax.axis_index(axis) // 2, 2)
+    return kept if second else 1 - kept
+
+
+def first_kernel(axis, second, own_ref, near_ref, w1_ref, w2_ref, edge_ref, part_ref, rows_ref, mid_ref):
+    span, (depth, channels) = part_ref.shape[1], part_ref.shape[2:]
+    side = lax.rem(lax.axis_index(axis), 2)
+    half = half_of(axis, second)
+    clear_ends(rows_ref, 2)
+    inner = pl.ds(half * (span - 2), span + 2)
+    local = pl.ds(2 - 2 * half, span + 2)
     for row, at in enumerate((side, 1 - side)):
-        rows_ref[row, pl.ds(1 + kept * (span - 2), span + 2)] = cut0_ref[at]
-        rows_ref[row, pl.ds(1 + (1 - kept) * (span - 2), span + 2)] = cut1_ref[at]
-        rows_ref[2 + row, 1 : across + 1] = near_ref[at]
+        rows_ref[row, local] = own_ref[at]
+        rows_ref[2 + row, local] = near_ref[at, inner]
     taps = (2 * side, 1, 2 - 2 * side)
     back = (2 - 2 * side, 1, 2 * side)
-    for step in range(2):
-        start = step * span
-        low, high = conv_rows(rows_ref, w1_ref, taps, start, span, PAIR)
-        mid_ref[0, 1 + start : 1 + start + span] = activate(low).astype(BF)
-        mid_ref[1, 1 + start : 1 + start + span] = activate(high).astype(BF)
-        low, high = conv_rows(rows_ref, w1_ref, back, start, span, LOWER, {0: 1, 1: 0})
-        edge_ref[0, 1 + start : 1 + start + span] = low
-        edge_ref[1, 1 + start : 1 + start + span] = high
-    for step in range(2):
-        start = step * span
-        low, high = conv_rows(mid_ref, w2_ref, taps, start, span, UPPER, {2: 0, 3: 1})
-        for u, part in enumerate((low, high)):
-            own = rows_ref[u, 1 + start : 1 + start + span].astype(F32)
-            part_ref[u, start : start + span] = part + own
+    low, high = conv_rows(rows_ref, w1_ref, taps, 0, span + 2, PAIR)
+    mid_ref[0] = activate(low).astype(BF)
+    mid_ref[1] = activate(high).astype(BF)
+    blank = jnp.zeros((depth, channels), BF)
+    mid_ref[0, half * (span + 1)] = blank
+    mid_ref[1, half * (span + 1)] = blank
+    low, high = conv_rows(rows_ref, w1_ref, back, 0, span + 2, LOWER, {0: 1, 1: 0})
+    edge_ref[0] = low
+    edge_ref[1] = high
+    outs = conv_rows(mid_ref, w2_ref, taps, 0, span, UPPER, {2: 0, 3: 1})
+    for u in range(2):
+        part_ref[u] = outs[u] + rows_ref[u, 2 : 2 + span].astype(F32)
 
 
 def half_kernel(axis, second, *refs):
@@ -131,13 +127,11 @@
         early_ref, feature_ref, message_ref, keep_ref, strip_ref, rows_ref, mid_ref = refs[8:]
     else:
         feature_ref, message_ref, keep_ref, rows_ref, mid_ref = refs[8:]
-    across, depth, channels = part_ref.shape[1:]
+    span, depth, channels = part_ref.shape[1:]
     devices = lax.axis_size(axis)
     index = lax.axis_index(axis)
     side = lax.rem(index, 2)
-    span = across // 2
-    kept = lax.rem(index // 2, 2)
-    half = kept if second else 1 - kept
+    half = half_of(axis, second)
     clear_ends(rows_ref, 2)
     local = pl.ds(2 - 2 * half, span + 2)
     border = jnp.logical_or(index == 0, index == devices - 1)
@@ -147,14 +141,12 @@
     back = (2 - 2 * side, 1, 2 * side)
     low, high = conv_rows(rows_ref, w1_ref, back, 0, span + 2, UPPER, {2: 0, 3: 1})
     inside = jnp.where(border, 0.0, 1.0)
-    around = pl.ds(half * span, span + 2)
-    mid_ref[1] = activate(low + edge_ref[0, around]).astype(BF)
-    mid_ref[0] = (activate(high + edge_ref[1, around]) * inside).astype(BF)
+    mid_ref[1] = activate(low + edge_ref[0]).astype(BF)
+    mid_ref[0] = (activate(high + edge_ref[1]) * inside).astype(BF)
     blank = jnp.zeros((depth, channels), BF)
     mid_ref[0, half * (span + 1)] = blank
     mid_ref[1, half * (span + 1)] = blank
     outs = conv_rows(mid_ref, w2_ref, (2 * side, 1, 2 - 2 * side), 0, span, LOWER)
-    place = pl.ds(half * span, span)
     across_score, along_score = x_ref[...], y_ref[...]
 
     def prior_of(at, half):
@@ -167,7 +159,7 @@
     logits, features = [], []
     for u in range(2):
         at = side if u == 0 else 1 - side
-        feature = (outs[u] + part_ref[u, place]).astype(BF)
+        feature = (outs[u] + part_ref[u]).astype(BF)
         feature_ref[at] = feature
         prior = prior_of(at, half)
         if not second:
@@ -389,36 +381,41 @@
         for i in range(base + 1, base + devices - 1, 2):
             pairs += [(i, i + 1), (i + 1, i)]
     cut = jax.ShapeDtypeStruct((rows, half + 2, depth, channels), BF)
-    cuts = kernel_call(
-        functools.partial(cut_kernel, axis),
-        (cut, cut),
-        [pltpu.SemaphoreType.DMA((2,))],
-        flops,
-        voxels,
-        spaces=(pltpu.HBM,),
-    )
+    cuts = [
+        kernel_call(
+            functools.partial(cut_kernel, axis, second),
+            cut,
+            [pltpu.SemaphoreType.DMA],
+            flops * second,
+            voxels,
+            spaces=(pltpu.HBM,),
+        )
+        for second in (False, True)
+    ]
     far0 = lax.ppermute(cuts[0], (others, axis), pairs)
     far1 = lax.ppermute(cuts[1], (others, axis), pairs)
     near = swap(voxels, axis, 1)
     prior = prior.swapaxes(1, 2)
-    edge, part = kernel_call(
-        functools.partial(first_kernel, axis),
-        (
-            jax.ShapeDtypeStruct((rows, across + 2, depth, channels), F32),
-            jax.ShapeDtypeStruct(voxels.shape, F32),
-        ),
-        [
-            pltpu.VMEM((4, across + 2, depth, channels), BF),
-            pltpu.VMEM((2, across + 2, depth, channels), BF),
-        ],
-        2 * flops,
-        *cuts,
-        near,
-        w_first,
-        w_second,
-    )
-
-    def half_call(second, far, *state):
+
+    def base_call(second, own):
+        return kernel_call(
+            functools.partial(first_kernel, axis, second),
+            (
+                jax.ShapeDtypeStruct((rows, half + 2, depth, channels), F32),
+                jax.ShapeDtypeStruct((rows, half, depth, channels), F32),
+            ),
+            [
+                pltpu.VMEM((4, half + 4, depth, channels), BF),
+                pltpu.VMEM((2, half + 2, depth, channels), BF),
+            ],
+            flops,
+            own,
+            near,
+            w_first,
+            w_second,
+        )
+
+    def half_call(second, base, far, *state):
         feature = jax.ShapeDtypeStruct((rows, half, depth, channels), BF)
         message = jax.ShapeDtypeStruct((3 * quarter + 2 * second, depth, channels), BF)
         keep = jax.ShapeDtypeStruct((3, quarter, depth, channels), F32)
@@ -431,8 +428,7 @@
                 pltpu.VMEM((2, half + 2, depth, channels), BF),
             ],
             3 * flops // 4,
-            edge,
-            part,
+            *base,
             far,
             w_first,
             w_second,
@@ -443,12 +439,14 @@
         )
 
     masks = [1 << bit for bit in range(devices.bit_length() - 1)]
-    early, message, keep = half_call(False, far0)
+    base = base_call(False, cuts[1])
+    early, message, keep = half_call(False, base, far0)
     got = swap(message, axis, masks[0])
     sent = jnp.concatenate([p.astype(BF) for p in merge(keep, thirds(got))])
     sent, early_first = lax.optimization_barrier((sent, early))
     arriving = swap(sent, axis, masks[1])
-    late, message, keep, strip = half_call(True, far1, early_first)
+    base = base_call(True, cuts[0])
+    late, message, keep, strip = half_call(True, base, far1, early_first)
     got = swap(message, axis, masks[0])
     beyond = got[3 * quarter]
     carried = [got[3 * quarter + 1]]

time: 55.5 us -> 56.5 us (1.018)
  waiting for transfers between devices: 20.5 us -> 19.6 us
  local copies, waits for them, and re-layouts: 1.18 us -> 1.93 us
  Pallas kernels: 12.6 us -> 13.2 us
    ppermute x1, waiting for transfers between devices: 4.82 us -> 2.37 us  [on_device(): far1 = lax.ppermute(cuts[1], (others, axis), pairs)]
    ppermute x1, waiting for transfers between devices: 0.01 us -> 1.88 us  [on_device(): far0 = lax.ppermute(cuts[0], (others, axis), pairs)]
    unnamed x22, local copies, waits for them, and re-layouts: 1.13 us -> 1.88 us
    ppermute x9, starting transfers between devices: 15.8 us -> 16.3 us  [swap(): return lax.ppermute(values, axis, [(i, i ^ mask) for i in range(devices)])]
    pallas_call x6 -> x8, Pallas kernels: 12.6 us -> 13.2 us  [kernel_call(): pl.pallas_call(body, out_shape=outs, in_specs=[pl.BlockSpec(memory_space=...]
  transfers between devices with their start and end apart: 11 -> 11, of which waited for: 6 -> 7; matrix products, arithmetic and copies ran while one was open for 0% -> 0% of each run, Pallas kernels for 11% -> 11%
where the time goes in v8:
time: 56.5 us; the launch traced here: 56 us
  starting transfers between devices  20.4 us (36%)
  waiting for transfers between devices  19.6 us (35%)
  Pallas kernels  13.2 us (23%)
  local copies, waits for them, and re-layouts  1.93 us (3%)
    ppermute x9, starting transfers between devices, swap(): return lax.ppermute(values, axis, [(i, i ^ mask) for i in range(devices)])  16.3 us
    ppermute x9, waiting for transfers between devices, swap(): return lax.ppermute(values, axis, [(i, i ^ mask) for i in range(devices)])  15.3 us
    pallas_call x8, Pallas kernels, kernel_call(): pl.pallas_call(body, out_shape=outs, in_specs=[pl.BlockSpec(memory_space=...  13.2 us
    ppermute x1, starting transfers between devices, on_device(): far0 = lax.ppermute(cuts[0], (others, axis), pairs)  2.54 us
    ppermute x1, waiting for transfers between devices, on_device(): far1 = lax.ppermute(cuts[1], (others, axis), pairs)  2.37 us
    unnamed x22, local copies, waits for them, and re-layouts  1.88 us
    ppermute x1, waiting for transfers between devices, on_device(): far0 = lax.ppermute(cuts[0], (others, axis), pairs)  1.88 us
    ppermute x1, starting transfers between devices, on_device(): far1 = lax.ppermute(cuts[1], (others, axis), pairs)  1.49 us
  transfers between devices with their start and end apart: 11, of which 7 were waited for; matrix products, arithmetic and copies ran while one was open for 0% of the time, Pallas kernels for 11%

profile of v8, /device:TPU:0, one launch (start us, length us, event | category | flops | bytes accessed | tf_op | source)
XLA Modules:
  0.0 56.0 jit_solution(228440822837003991)
XLA Ops:
  0.0 0.5 collective-permute-start
  0.5 1.0 %copy-done.1 = bf16[2,128,8,128]{3,2,1,0:T(8,128)(2,1)S(1)} copy-done((bf16[2,128,8,128]{3,2,1,0:T(8,128)(2,1)S(1)}, bf16[2,128,8,128]{3,2,1,0:T(8,128)(2,1)}, u32[]{:S(2)}) %copy-start.1) | copy-done | bytes 524312
  1.6 0.0 copy-start.6
  1.6 2.5 %collective-permute-start.1 = (bf16[2,66,8,128]{3,2,1,0:T(8,128)(2,1)S(1)}, bf16[2,66,8,128]{3,2,1,0:T(8,128)(2,1)S(1)}, u32[]{:S(2)}, u32[]{:S(2)}) collective-permute-start(bf16[2,66,8,128]{3,2,1,0:T(8,128)(2,1)S(1)} %shard_map.111.own_ref), channel_id=1, source_target_pairs={{0,16},{15,31},{1,2},{2,1},{3,4},{4,3},{5,6},{6,5},{7,8},{8,7},{9,... | collective-permute-start | bytes 811016 | tf_op jit(solution)/shard_map/ppermute | solution.py:395
  4.2 0.0 copy-start.8
  4.2 2.4 %shard_map.110 = (f32[2,66,8,128]{3,2,1,0:T(8,128)S(1)}, f32[2,64,8,128]{3,2,1,0:T(8,128)S(1)}) custom-call(bf16[2,66,8,128]{3,2,1,0:T(8,128)(2,1)S(1)} %shard_map.109.own_ref, bf16[2,128,8,128]{3,2,1,0:T(8,128)(2,1)S(1)} %collective-permute-done.near_ref, bf16[3,9,128,128]{3,2,1,0:T(8,128)(2,1)S(1)} %bitcast.81, bf16[3,9,128,128]{3,2,1,0:T(8,128)(2,1)S(1)} %bitcast.85), custom_call_target="tpu_custom_call" | custom-call | flops 1811939328 | bytes 2564096 | tf_op jit(solution)/shard_map/pallas_call | solution.py:333
  6.7 1.9 %collective-permute-done.1.refs_2_ = bf16[2,66,8,128]{3,2,1,0:T(8,128)(2,1)S(1)} collective-permute-done((bf16[2,66,8,128]{3,2,1,0:T(8,128)(2,1)S(1)}, bf16[2,66,8,128]{3,2,1,0:T(8,128)(2,1)S(1)}, u32[]{:S(2)}, u32[]{:S(2)}) %collective-permute-start.1) | collective-permute-done | bytes 270368 | tf_op jit(solution)/shard_map/ppermute | solution.py:395
  8.6 2.0 %shard_map.112 = (bf16[2,64,8,128]{3,2,1,0:T(8,128)(2,1)S(1)}, bf16[96,8,128]{2,1,0:T(8,128)(2,1)S(1)}, f32[3,32,8,128]{3,2,1,0:T(8,128)S(1)}) custom-call(f32[2,66,8,128]{3,2,1,0:T(8,128)S(1)} %get-tuple-element.24.refs_0_, f32[2,64,8,128]{3,2,1,0:T(8,128)S(1)} %get-tuple-element.25.refs_1_, bf16[2,66,8,128]{3,2,1,0:T(8,128)(2,1)S(1)} %collective-permute-done.1.refs_2_, ...), custom_call_target="tpu_custom_call" | custom-call | flops 1358954496 | bytes 3178496 | tf_op jit(solution)/shard_map/pallas_call | solution.py:333
  10.6 2.1 %collective-permute-start.3 = (bf16[96,8,128]{2,1,0:T(8,128)(2,1)S(1)}, bf16[96,8,128]{2,1,0:T(8,128)(2,1)S(1)}, u32[]{:S(2)}, u32[]{:S(2)}) collective-permute-start(bf16[96,8,128]{2,1,0:T(8,128)(2,1)S(1)} %get-tuple-element.30), channel_id=1, source_target_pairs={{0,1},{1,0},{2,3},{3,2},{4,5},{5,4},{6,7},{7,6},{8,9},{9,8},{10,11... | collective-permute-start | bytes 589832 | tf_op jit(solution)/shard_map/ppermute | solution.py:311
  12.7 1.5 %collective-permute-start.2 = (bf16[2,66,8,128]{3,2,1,0:T(8,128)(2,1)S(1)}, bf16[2,66,8,128]{3,2,1,0:T(8,128)(2,1)S(1)}, u32[]{:S(2)}, u32[]{:S(2)}) collective-permute-start(bf16[2,66,8,128]{3,2,1,0:T(8,128)(2,1)S(1)} %shard_map.109.own_ref), channel_id=1, source_target_pairs={{0,16},{15,31},{1,2},{2,1},{3,4},{4,3},{5,6},{6,5},{7,8},{8,7},{9,... | collective-permute-start | bytes 811016 | tf_op jit(solution)/shard_map/ppermute | solution.py:396
  14.2 2.4 %shard_map.113 = (f32[2,66,8,128]{3,2,1,0:T(8,128)S(1)}, f32[2,64,8,128]{3,2,1,0:T(8,128)S(1)}) custom-call(bf16[2,66,8,128]{3,2,1,0:T(8,128)(2,1)S(1)} %shard_map.111.own_ref, bf16[2,128,8,128]{3,2,1,0:T(8,128)(2,1)S(1)} %collective-permute-done.near_ref, bf16[3,9,128,128]{3,2,1,0:T(8,128)(2,1)S(1)} %bitcast.83, bf16[3,9,128,128]{3,2,1,0:T(8,128)(2,1)S(1)} %bitcast.87), custom_call_target="tpu_custom_call" | custom-call | flops 1811939328 | bytes 2564096 | tf_op jit(solution)/shard_map/pallas_call | solution.py:333
  16.6 0.1 fusion.16
  16.7 2.4 %collective-permute-done.2.refs_2_ = bf16[2,66,8,128]{3,2,1,0:T(8,128)(2,1)S(1)} collective-permute-done((bf16[2,66,8,128]{3,2,1,0:T(8,128)(2,1)S(1)}, bf16[2,66,8,128]{3,2,1,0:T(8,128)(2,1)S(1)}, u32[]{:S(2)}, u32[]{:S(2)}) %collective-permute-start.2) | collective-permute-done | bytes 270368 | tf_op jit(solution)/shard_map/ppermute | solution.py:396
  19.1 2.5 %shard_map.114 = (bf16[2,64,8,128]{3,2,1,0:T(8,128)(2,1)S(1)}, bf16[98,8,128]{2,1,0:T(8,128)(2,1)S(1)}, f32[3,32,8,128]{3,2,1,0:T(8,128)S(1)}, bf16[2,8,128]{2,1,0:T(8,128)(2,1)S(1)}) custom-call(f32[2,66,8,128]{3,2,1,0:T(8,128)S(1)} %get-tuple-element.27.refs_0_, f32[2,64,8,128]{3,2,1,0:T(8,128)S(1)} %get-tuple-element.28.refs_1_, ...), custom_call_target="tpu_custom_call" | custom-call | flops 1358954496 | bytes 3440640 | tf_op jit(solution)/shard_map/pallas_call | solution.py:333
  21.6 2.5 %collective-permute-start.4 = (bf16[98,8,128]{2,1,0:T(8,128)(2,1)S(1)}, bf16[98,8,128]{2,1,0:T(8,128)(2,1)S(1)}, u32[]{:S(2)}, u32[]{:S(2)}) collective-permute-start(bf16[98,8,128]{2,1,0:T(8,128)(2,1)S(1)} %get-tuple-element.34), channel_id=1, source_target_pairs={{0,1},{1,0},{2,3},{3,2},{4,5},{5,4},{6,7},{7,6},{8,9},{9,8},{10,11... | collective-permute-start | bytes 602120 | tf_op jit(solution)/shard_map/ppermute | solution.py:311
  24.1 2.4 %collective-permute-start.5 = (bf16[96,8,128]{2,1,0:T(8,128)(2,1)S(1)}, bf16[96,8,128]{2,1,0:T(8,128)(2,1)S(1)}, u32[]{:S(2)}, u32[]{:S(2)}) collective-permute-start(bf16[96,8,128]{2,1,0:T(8,128)(2,1)S(1)} %pad_maximum_fusion.1), channel_id=1, source_target_pairs={{0,2},{1,3},{2,0},{3,1},{4,6},{5,7},{6,4},{7,5},{8,10},{9,11},{10,... | collective-permute-start | bytes 589832 | tf_op jit(solution)/shard_map/ppermute | solution.py:311
  26.5 5.5 %collective-permute-done.5 = bf16[96,8,128]{2,1,0:T(8,128)(2,1)S(1)} collective-permute-done((bf16[96,8,128]{2,1,0:T(8,128)(2,1)S(1)}, bf16[96,8,128]{2,1,0:T(8,128)(2,1)S(1)}, u32[]{:S(2)}, u32[]{:S(2)}) %collective-permute-start.5) | collective-permute-done | bytes 196640 | tf_op jit(solution)/shard_map/ppermute | solution.py:311
  32.0 0.1 convert_maximum_fusion
  32.3 2.0 %collective-permute-start.6 = (bf16[49,8,128]{2,1,0:T(8,128)(2,1)S(1)}, bf16[49,8,128]{2,1,0:T(8,128)(2,1)S(1)}, u32[]{:S(2)}, u32[]{:S(2)}) collective-permute-start(bf16[49,8,128]{2,1,0:T(8,128)(2,1)S(1)} %pad_maximum_fusion.3), channel_id=1, source_target_pairs={{0,4},{1,5},{2,6},{3,7},{4,0},{5,1},{6,2},{7,3},{8,12},{9,13},{10,... | collective-permute-start | bytes 301064 | tf_op jit(solution)/shard_map/ppermute | solution.py:311
  34.2 2.7 %collective-permute-done.6 = bf16[49,8,128]{2,1,0:T(8,128)(2,1)S(1)} collective-permute-done((bf16[49,8,128]{2,1,0:T(8,128)(2,1)S(1)}, bf16[49,8,128]{2,1,0:T(8,128)(2,1)S(1)}, u32[]{:S(2)}, u32[]{:S(2)}) %collective-permute-start.6) | collective-permute-done | bytes 100384 | tf_op jit(solution)/shard_map/ppermute | solution.py:311
  37.1 3.0 %collective-permute-start.7 = (bf16[49,8,128]{2,1,0:T(8,128)(2,1)S(1)}, bf16[49,8,128]{2,1,0:T(8,128)(2,1)S(1)}, u32[]{:S(2)}, u32[]{:S(2)}) collective-permute-start(bf16[49,8,128]{2,1,0:T(8,128)(2,1)S(1)} %pad_maximum_fusion.4), channel_id=1, source_target_pairs={{0,8},{1,9},{2,10},{3,11},{4,12},{5,13},{6,14},{7,15},{8,0},{9,1},... | collective-permute-start | bytes 301064 | tf_op jit(solution)/shard_map/ppermute | solution.py:311
  40.1 2.6 %collective-permute-done.7 = bf16[49,8,128]{2,1,0:T(8,128)(2,1)S(1)} collective-permute-done((bf16[49,8,128]{2,1,0:T(8,128)(2,1)S(1)}, bf16[49,8,128]{2,1,0:T(8,128)(2,1)S(1)}, u32[]{:S(2)}, u32[]{:S(2)}) %collective-permute-start.7) | collective-permute-done | bytes 100384 | tf_op jit(solution)/shard_map/ppermute | solution.py:311
  42.7 0.1 divide_convert_fusion
  42.8 2.1 %collective-permute-start.8 = (bf16[16,8,128]{2,1,0:T(8,128)(2,1)S(1)}, bf16[16,8,128]{2,1,0:T(8,128)(2,1)S(1)}, u32[]{:S(2)}, u32[]{:S(2)}) collective-permute-start(bf16[16,8,128]{2,1,0:T(8,128)(2,1)S(1)} %divide_convert_fusion), channel_id=1, source_target_pairs={{0,4},{1,5},{2,6},{3,7},{4,0},{5,1},{6,2},{7,3},{8,12},{9,13},{10,... | collective-permute-start | bytes 98312 | tf_op jit(solution)/shard_map/ppermute | solution.py:311
  44.9 1.9 %collective-permute-done.8 = bf16[16,8,128]{2,1,0:T(8,128)(2,1)S(1)} collective-permute-done((bf16[16,8,128]{2,1,0:T(8,128)(2,1)S(1)}, bf16[16,8,128]{2,1,0:T(8,128)(2,1)S(1)}, u32[]{:S(2)}, u32[]{:S(2)}) %collective-permute-start.8) | collective-permute-done | bytes 32800 | tf_op jit(solution)/shard_map/ppermute | solution.py:311
  46.8 1.7 %collective-permute-start.9 = (bf16[33,8,128]{2,1,0:T(8,128)(2,1)S(1)}, bf16[33,8,128]{2,1,0:T(8,128)(2,1)S(1)}, u32[]{:S(2)}, u32[]{:S(2)}) collective-permute-start(bf16[33,8,128]{2,1,0:T(8,128)(2,1)S(1)} %pad_maximum_fusion.5), channel_id=1, source_target_pairs={{0,2},{1,3},{2,0},{3,1},{4,6},{5,7},{6,4},{7,5},{8,10},{9,11},{10,... | collective-permute-start | bytes 202760 | tf_op jit(solution)/shard_map/ppermute | solution.py:311
  48.5 2.6 %collective-permute-done.9 = bf16[33,8,128]{2,1,0:T(8,128)(2,1)S(1)} collective-permute-done((bf16[33,8,128]{2,1,0:T(8,128)(2,1)S(1)}, bf16[33,8,128]{2,1,0:T(8,128)(2,1)S(1)}, u32[]{:S(2)}, u32[]{:S(2)}) %collective-permute-start.9) | collective-permute-done | bytes 67616 | tf_op jit(solution)/shard_map/ppermute | solution.py:311
  51.1 0.1 collective-permute-start.10
  51.3 0.7 %copy-done.2 = bf16[128,512]{1,0:T(8,128)(2,1)S(1)} copy-done((bf16[128,512]{1,0:T(8,128)(2,1)S(1)}, bf16[128,512]{1,0:T(8,128)(2,1)}, u32[]{:S(2)}) %copy-start.2) | copy-done | bytes 131096
  52.0 0.1 copy-done.3
  52.1 1.4 %shard_map.115 = (bf16[2,128,8,128]{3,2,1,0:T(8,128)(2,1)S(1)}, bf16[2,2,32,8,128]{4,3,2,1,0:T(8,128)(2,1)S(1)}, f32[2,8,128]{2,1,0:T(8,128)S(1)}) custom-call(bf16[2,64,8,128]{3,2,1,0:T(8,128)(2,1)S(1)} %get-tuple-element.31.refs_8_.refs_0_, bf16[2,64,8,128]{3,2,1,0:T(8,128)(2,1)S(1)} %get-tuple-element.32.refs_1_, ...), custom_call_target="tpu_custom_call" | custom-call | flops 226492416 | bytes 1516032 | tf_op jit(solution)/shard_map/pallas_call | solution.py:333
  53.6 2.3 %shard_map.116 = bf16[2,128,8,128]{3,2,1,0:T(8,128)(2,1)} custom-call(bf16[2,128,8,128]{3,2,1,0:T(8,128)(2,1)S(1)} %get-tuple-element.40.refs_0_, bf16[2,2,32,8,128]{4,3,2,1,0:T(8,128)(2,1)S(1)} %get-tuple-element.41.refs_1_, f32[2,8,128]{2,1,0:T(8,128)S(1)} %get-tuple-element.42.refs_2_, bf16[128,8,128]{2,1,0:T(8,128)(2,1)S(1)} %pad_maximum_fusion.refs_3_, ...), custom_call_target="tpu_custom_call" | custom-call | flops 226492416 | bytes 1614336 | tf_op jit(solution)/shard_map/pallas_call | solution.py:333
  (42 shorter events, 0.4 us)
Async XLA Ops:
  0.0 4.2 %collective-permute-start = (bf16[2,128,8,128]{3,2,1,0:T(8,128)(2,1)}, bf16[2,128,8,128]{3,2,1,0:T(8,128)(2,1)S(1)}, u32[]{:S(2)}, u32[]{:S(2)}) collective-permute-start(bf16[2,128,8,128]{3,2,1,0:T(8,128)(2,1)} %own_ref.3), channel_id=1, source_target_pairs={{0,1},{1,0},{2,3},{3,2},{4,5},{5,4},{6,7},{7,6},{8,9},{9,8},{10,11... | collective-permute-start | bytes 1572872 | tf_op jit(solution)/shard_map/ppermute | solution.py:311
  0.5 1.0 %copy-start.1 = (bf16[2,128,8,128]{3,2,1,0:T(8,128)(2,1)S(1)}, bf16[2,128,8,128]{3,2,1,0:T(8,128)(2,1)}, u32[]{:S(2)}) copy-start(bf16[2,128,8,128]{3,2,1,0:T(8,128)(2,1)} %own_ref.3) | copy-start | bytes 1572868
  1.6 2.6 %copy-start.6 = (bf16[27,128,128]{2,1,0:T(8,128)(2,1)S(1)}, bf16[27,128,128]{2,1,0:T(8,128)(2,1)}, u32[]{:S(2)}) copy-start(bf16[27,128,128]{2,1,0:T(8,128)(2,1)} %param.13) | copy-start | bytes 2654212
  1.6 2.6 %copy-start.7 = (bf16[27,128,128]{2,1,0:T(8,128)(2,1)S(1)}, bf16[27,128,128]{2,1,0:T(8,128)(2,1)}, u32[]{:S(2)}) copy-start(bf16[27,128,128]{2,1,0:T(8,128)(2,1)} %param.14) | copy-start | bytes 2654212
  1.6 7.0 %collective-permute-start.1 = (bf16[2,66,8,128]{3,2,1,0:T(8,128)(2,1)S(1)}, bf16[2,66,8,128]{3,2,1,0:T(8,128)(2,1)S(1)}, u32[]{:S(2)}, u32[]{:S(2)}) collective-permute-start(bf16[2,66,8,128]{3,2,1,0:T(8,128)(2,1)S(1)} %shard_map.111.own_ref), channel_id=1, source_target_pairs={{0,16},{15,31},{1,2},{2,1},{3,4},{4,3},{5,6},{6,5},{7,8},{8,7},{9,... | collective-permute-start | bytes 811016 | tf_op jit(solution)/shard_map/ppermute | solution.py:395
  4.2 4.4 %copy-start.8 = (bf16[128,128]{1,0:T(8,128)(2,1)S(1)}, bf16[128,128]{1,0:T(8,128)(2,1)}, u32[]{:S(2)}) copy-start(bf16[128,128]{1,0:T(8,128)(2,1)} %refs_5_.3) | copy-start | bytes 98308
  4.2 4.4 %copy-start.9 = (bf16[128,128]{1,0:T(8,128)(2,1)S(1)}, bf16[128,128]{1,0:T(8,128)(2,1)}, u32[]{:S(2)}) copy-start(bf16[128,128]{1,0:T(8,128)(2,1)} %refs_6_.4) | copy-start | bytes 98308
  4.2 4.4 %copy-start.10 = (f32[2,128,8]{1,2,0:T(8,128)S(1)}, f32[2,128,8]{1,2,0:T(8,128)}, u32[]{:S(2)}) copy-start(f32[2,128,8]{1,2,0:T(8,128)} %param.12) | copy-start | bytes 24580
  10.6 6.0 %collective-permute-start.3 = (bf16[96,8,128]{2,1,0:T(8,128)(2,1)S(1)}, bf16[96,8,128]{2,1,0:T(8,128)(2,1)S(1)}, u32[]{:S(2)}, u32[]{:S(2)}) collective-permute-start(bf16[96,8,128]{2,1,0:T(8,128)(2,1)S(1)} %get-tuple-element.30), channel_id=1, source_target_pairs={{0,1},{1,0},{2,3},{3,2},{4,5},{5,4},{6,7},{7,6},{8,9},{9,8},{10,11... | collective-permute-start | bytes 589832 | tf_op jit(solution)/shard_map/ppermute | solution.py:311
  12.7 6.5 %collective-permute-start.2 = (bf16[2,66,8,128]{3,2,1,0:T(8,128)(2,1)S(1)}, bf16[2,66,8,128]{3,2,1,0:T(8,128)(2,1)S(1)}, u32[]{:S(2)}, u32[]{:S(2)}) collective-permute-start(bf16[2,66,8,128]{3,2,1,0:T(8,128)(2,1)S(1)} %shard_map.109.own_ref), channel_id=1, source_target_pairs={{0,16},{15,31},{1,2},{2,1},{3,4},{4,3},{5,6},{6,5},{7,8},{8,7},{9,... | collective-permute-start | bytes 811016 | tf_op jit(solution)/shard_map/ppermute | solution.py:396
  21.6 10.4 %collective-permute-start.4 = (bf16[98,8,128]{2,1,0:T(8,128)(2,1)S(1)}, bf16[98,8,128]{2,1,0:T(8,128)(2,1)S(1)}, u32[]{:S(2)}, u32[]{:S(2)}) collective-permute-start(bf16[98,8,128]{2,1,0:T(8,128)(2,1)S(1)} %get-tuple-element.34), channel_id=1, source_target_pairs={{0,1},{1,0},{2,3},{3,2},{4,5},{5,4},{6,7},{7,6},{8,9},{9,8},{10,11... | collective-permute-start | bytes 602120 | tf_op jit(solution)/shard_map/ppermute | solution.py:311
  24.1 7.9 %collective-permute-start.5 = (bf16[96,8,128]{2,1,0:T(8,128)(2,1)S(1)}, bf16[96,8,128]{2,1,0:T(8,128)(2,1)S(1)}, u32[]{:S(2)}, u32[]{:S(2)}) collective-permute-start(bf16[96,8,128]{2,1,0:T(8,128)(2,1)S(1)} %pad_maximum_fusion.1), channel_id=1, source_target_pairs={{0,2},{1,3},{2,0},{3,1},{4,6},{5,7},{6,4},{7,5},{8,10},{9,11},{10,... | collective-permute-start | bytes 589832 | tf_op jit(solution)/shard_map/ppermute | solution.py:311
  32.3 4.7 %collective-permute-start.6 = (bf16[49,8,128]{2,1,0:T(8,128)(2,1)S(1)}, bf16[49,8,128]{2,1,0:T(8,128)(2,1)S(1)}, u32[]{:S(2)}, u32[]{:S(2)}) collective-permute-start(bf16[49,8,128]{2,1,0:T(8,128)(2,1)S(1)} %pad_maximum_fusion.3), channel_id=1, source_target_pairs={{0,4},{1,5},{2,6},{3,7},{4,0},{5,1},{6,2},{7,3},{8,12},{9,13},{10,... | collective-permute-start | bytes 301064 | tf_op jit(solution)/shard_map/ppermute | solution.py:311
  37.1 5.6 %collective-permute-start.7 = (bf16[49,8,128]{2,1,0:T(8,128)(2,1)S(1)}, bf16[49,8,128]{2,1,0:T(8,128)(2,1)S(1)}, u32[]{:S(2)}, u32[]{:S(2)}) collective-permute-start(bf16[49,8,128]{2,1,0:T(8,128)(2,1)S(1)} %pad_maximum_fusion.4), channel_id=1, source_target_pairs={{0,8},{1,9},{2,10},{3,11},{4,12},{5,13},{6,14},{7,15},{8,0},{9,1},... | collective-permute-start | bytes 301064 | tf_op jit(solution)/shard_map/ppermute | solution.py:311
  42.7 8.6 %copy-start.4 = (bf16[9,128,128]{2,1,0:T(8,128)(2,1)S(1)}, bf16[9,128,128]{2,1,0:T(8,128)(2,1)}, u32[]{:S(2)}) copy-start(bf16[9,128,128]{2,1,0:T(8,128)(2,1)} %param.18) | copy-start | bytes 884740
  42.8 8.5 %copy-start = (bf16[9,128,128]{2,1,0:T(8,128)(2,1)S(1)}, bf16[9,128,128]{2,1,0:T(8,128)(2,1)}, u32[]{:S(2)}) copy-start(bf16[9,128,128]{2,1,0:T(8,128)(2,1)} %param.17) | copy-start | bytes 884740
  42.8 4.0 %collective-permute-start.8 = (bf16[16,8,128]{2,1,0:T(8,128)(2,1)S(1)}, bf16[16,8,128]{2,1,0:T(8,128)(2,1)S(1)}, u32[]{:S(2)}, u32[]{:S(2)}) collective-permute-start(bf16[16,8,128]{2,1,0:T(8,128)(2,1)S(1)} %divide_convert_fusion), channel_id=1, source_target_pairs={{0,4},{1,5},{2,6},{3,7},{4,0},{5,1},{6,2},{7,3},{8,12},{9,13},{10,... | collective-permute-start | bytes 98312 | tf_op jit(solution)/shard_map/ppermute | solution.py:311
  46.8 4.3 %collective-permute-start.9 = (bf16[33,8,128]{2,1,0:T(8,128)(2,1)S(1)}, bf16[33,8,128]{2,1,0:T(8,128)(2,1)S(1)}, u32[]{:S(2)}, u32[]{:S(2)}) collective-permute-start(bf16[33,8,128]{2,1,0:T(8,128)(2,1)S(1)} %pad_maximum_fusion.5), channel_id=1, source_target_pairs={{0,2},{1,3},{2,0},{3,1},{4,6},{5,7},{6,4},{7,5},{8,10},{9,11},{10,... | collective-permute-start | bytes 202760 | tf_op jit(solution)/shard_map/ppermute | solution.py:311
  51.1 0.9 %copy-start.2 = (bf16[128,512]{1,0:T(8,128)(2,1)S(1)}, bf16[128,512]{1,0:T(8,128)(2,1)}, u32[]{:S(2)}) copy-start(bf16[128,512]{1,0:T(8,128)(2,1)} %refs_6_.5) | copy-start | bytes 393220
  51.1 1.0 %copy-start.3 = (bf16[512,128]{1,0:T(8,128)(2,1)S(1)}, bf16[512,128]{1,0:T(8,128)(2,1)}, u32[]{:S(2)}) copy-start(bf16[512,128]{1,0:T(8,128)(2,1)} %refs_7_.3) | copy-start | bytes 393220
  51.1 2.4 %collective-permute-start.10 = (bf16[64,8,128]{2,1,0:T(8,128)(2,1)S(1)}, bf16[64,8,128]{2,1,0:T(8,128)(2,1)S(1)}, u32[]{:S(2)}, u32[]{:S(2)}) collective-permute-start(bf16[64,8,128]{2,1,0:T(8,128)(2,1)S(1)} %pad_maximum_fusion.2.refs_4_), channel_id=1, source_target_pairs={{0,1},{1,0},{2,3},{3,2},{4,5},{5,4},{6,7},{7,6},{8,9},{9,8},{10,11... | collective-permute-start | bytes 393224 | tf_op jit(solution)/shard_map/ppermute | solution.py:311
  51.2 0.8 %copy-start.5 = (f32[128]{0:T(128)S(1)}, f32[128]{0:T(128)}, u32[]{:S(2)}) copy-start(f32[128]{0:T(128)} %param.19) | copy-start | bytes 1540
